TPU v7x, 32 devices: a whole 2x2x4 slice. The times are simulated.
32 devices in a mesh: seq: 8 (over y, x, core), tp: 4 (over z).
Axes of the slice: x: 2, y: 2, z: 4, core: 2. Of those that a mesh axis runs over, the one named last changes fastest.
Arguments:
- hidden_in: bfloat16 [8192, 2048], P('seq', 'tp'), may hold values from -6 to 6
- segment_ids: int32 [8192], P('seq'), may hold values from 0 to 7, never falling along the last dimension, each value on 1 to 4096 neighbouring positions
- first_gain: float32 [2048], replicated, may hold values from 0.5 to 1.5
- input_weight: bfloat16 [2048, 2816], P(None, 'tp'), may hold values from -0.125 to 0.125
- gelu_weight: bfloat16 [2048, 2816], P(None, 'tp'), may hold values from -0.125 to 0.125
- conv_weight: float32 [4, 2816], P(None, 'tp'), may hold values from -3 to 3
- conv_bias: float32 [2816], P('tp'), may hold values from -3 to 3
- recur_gate: bfloat16 [16, 176, 176], P('tp'), may hold values from -0.4375 to 0.4375
- input_gate: bfloat16 [16, 176, 176], P('tp'), may hold values from -0.4375 to 0.4375
- recur_bias: float32 [2816], P('tp'), may hold values from -4 to 4
- input_bias: float32 [2816], P('tp'), may hold values from -4 to 4
- decay_param: float32 [2816], P('tp'), may hold values from 5 to 15
- output_weight: bfloat16 [2816, 2048], P('tp'), may hold values from -0.3125 to 0.3125
- second_gain: float32 [2048], replicated, may hold values from 0.5 to 1.5
- gate_weight: bfloat16 [2048, 6144], P('seq', 'tp'), may hold values from -0.125 to 0.125
- up_weight: bfloat16 [2048, 6144], P('seq', 'tp'), may hold values from -0.125 to 0.125
- down_weight: bfloat16 [6144, 2048], P('tp', 'seq'), may hold values from -0.109375 to 0.109375
- grad_out: bfloat16 [8192, 2048], P('seq'), may hold values from -6 to 6
Outputs:
- block_out: bfloat16 [8192, 2048], P('seq', 'tp')
- grad_in: bfloat16 [8192, 2048], P('seq', 'tp')
- grad_first_gain: float32 [2048], replicated
- grad_input_weight: float32 [2048, 2816], P(None, 'tp')
- grad_gelu_weight: float32 [2048, 2816], P(None, 'tp')
- grad_conv_weight: float32 [4, 2816], P(None, 'tp')
- grad_conv_bias: float32 [2816], P('tp')
- grad_recur_gate: float32 [16, 176, 176], P('tp')
- grad_input_gate: float32 [16, 176, 176], P('tp')
- grad_recur_bias: float32 [2816], P('tp')
- grad_input_bias: float32 [2816], P('tp')
- grad_decay: float32 [2816], P('tp')
- grad_output_weight: float32 [2816, 2048], P('tp')
- grad_second_gain: float32 [2048], replicated
- grad_gate_weight: float32 [2048, 6144], P('seq', 'tp')
- grad_up_weight: float32 [2048, 6144], P('seq', 'tp')
- grad_down_weight: float32 [6144, 2048], P('tp', 'seq')
- final_states: float32 [8, 2816], P(None, 'tp')
Inputs may be any that keep to these rules, and one draw needn't show every extreme that they name: `segment_ids`: Non-decreasing along the stream; every segment number occurs; each segment has 1 to 4096 tokens and one has exactly 4096.
All inputs are finite; a program needn't handle non-finite values.
Results may differ from a plain program's by a relative error of at most 0.009.
Values may be sent and summed in bfloat16 or wider, within the bound.
No kernel may reach another device: no remote copies, remote signals or barrier semaphores. Data moves between devices by JAX's collectives and lax.ppermute only.
A program may use at most 448 MiB of HBM per device.

v0:
```python
from functools import partial

import jax
import jax.numpy as jnp
from jax import lax
from jax.sharding import PartitionSpec as P

SEGS = 8


EPSILON = 1e-06
DECAY_SCALE = 8.0


def shifted(x, axis, by):
    peers = lax.axis_size(axis)
    pairs = [(i, i + by) for i in range(peers) if 0 <= i + by < peers]
    return lax.ppermute(x, axis, pairs)


def prefix(part, axis, combine, identity, reverse):
    count = lax.axis_size(axis)
    place = lax.axis_index(axis)
    ahead = count - 1 - place if reverse else place
    gathered = jax.tree.map(lambda a: lax.all_gather(a, axis), part)
    state = jax.tree.map(lambda a, e: jnp.zeros_like(a) + jnp.asarray(e, a.dtype), part, identity)

    def one(hop, state):
        source = count - 1 - hop if reverse else hop
        return combine(
            state, jax.tree.map(lambda a: lax.dynamic_index_in_dim(a, source, 0, False), gathered)
        )

    return lax.fori_loop(0, ahead, one, state)


def rms_norm(value, gain):
    return value * lax.rsqrt(jnp.mean(value * value, axis=1, keepdims=True) + EPSILON) * gain


def compose(earlier, later):
    return (earlier[0] * later[0], later[0] * earlier[1] + later[1])


def gate_math(pre_recur, pre_input, conv_val, bias_recur, bias_input, decay_value, restart):
    rate_gate = jax.nn.sigmoid(pre_recur + bias_recur)
    in_gate = jax.nn.sigmoid(pre_input + bias_input)
    log_decay = -DECAY_SCALE * rate_gate * jax.nn.softplus(-decay_value)
    carried = jnp.where(restart, 0.0, jnp.exp(log_decay))
    scaled = jnp.where(restart, 1.0, jnp.sqrt(-jnp.expm1(2.0 * log_decay)))
    return (carried, scaled * in_gate * conv_val)


def contract_first(left, right):
    return lax.dot_general(
        left, right, (((0,), (0,)), ((), ())), preferred_element_type=jnp.float32
    )


def contract_last(left, right):
    return lax.dot_general(
        left, right, (((1,), (1,)), ((), ())), preferred_element_type=jnp.float32
    )


def exact_dot(left, right):
    return jnp.dot(left, right, precision=lax.Precision.HIGHEST, preferred_element_type=jnp.float32)


def exact_first(left, right):
    return lax.dot_general(
        left,
        right,
        (((0,), (0,)), ((), ())),
        precision=lax.Precision.HIGHEST,
        preferred_element_type=jnp.float32,
    )


def on_device(
    hidden_in,
    segment_ids,
    first_gain,
    input_weight,
    gelu_weight,
    conv_weight,
    conv_bias,
    recur_gate,
    input_gate,
    recur_bias,
    input_bias,
    decay_param,
    output_weight,
    second_gain,
    gate_weight,
    up_weight,
    down_weight,
    grad_out,
):
    tok_dev = hidden_in.shape[0]
    share_width = hidden_in.shape[1]
    channels = input_weight.shape[1]
    conv_taps = conv_weight.shape[0]
    halo_rows = conv_taps - 1
    seq_devices = lax.axis_size("seq")
    seq_place = lax.axis_index("seq")
    tp_place = lax.axis_index("tp")
    share_start = tp_place * share_width
    first_device = seq_place == 0
    final_device = seq_place == seq_devices - 1
    ids_float = segment_ids.astype(jnp.float32)
    row_grid = lax.broadcasted_iota(jnp.int32, (tok_dev, tok_dev), 0)
    col_grid = lax.broadcasted_iota(jnp.int32, (tok_dev, tok_dev), 1)
    edge_rows = lax.broadcasted_iota(jnp.int32, (tok_dev, halo_rows), 0)
    edge_cols = lax.broadcasted_iota(jnp.int32, (tok_dev, halo_rows), 1)
    token_place = lax.broadcasted_iota(jnp.int32, (tok_dev, 1), 0)
    full_in = lax.all_gather(hidden_in, "tp", axis=1, tiled=True).astype(jnp.float32)
    normed1, norm1_back = jax.vjp(rms_norm, full_in, first_gain)
    normed1_low = normed1.astype(jnp.bfloat16)
    branch_x = jnp.dot(normed1_low, input_weight, preferred_element_type=jnp.float32)
    branch_y = jnp.dot(normed1_low, gelu_weight, preferred_element_type=jnp.float32)
    prev_rows, prev_ids = shifted(
        (branch_x[tok_dev - halo_rows :], ids_float[tok_dev - halo_rows :]), "seq", 1
    )
    prev_ids = jnp.where(first_device, -1.0, prev_ids)
    ext_ids = jnp.concatenate([prev_ids, ids_float])
    same_list = [
        (ext_ids[halo_rows - offset : halo_rows - offset + tok_dev] == ids_float).astype(
            jnp.float32
        )[:, None]
        for offset in range(conv_taps)
    ]
    lag_list = [
        (col_grid == row_grid - offset).astype(jnp.float32) * same_list[offset]
        for offset in range(conv_taps)
    ]
    edge_list = [
        (edge_cols == edge_rows - offset + halo_rows).astype(jnp.float32) * same_list[offset]
        for offset in range(conv_taps)
    ]
    window_list = [
        exact_dot(lag_list[offset], branch_x) + exact_dot(edge_list[offset], prev_rows)
        for offset in range(conv_taps)
    ]
    conv_out = conv_bias + sum(
        (conv_weight[offset] * window_list[offset] for offset in range(conv_taps))
    )
    blocks_here = recur_gate.shape[0]
    block_size = recur_gate.shape[1]
    conv_low = conv_out.astype(jnp.bfloat16).reshape(tok_dev, blocks_here, block_size)
    pre_recur = jnp.einsum(
        "tbi,bij->tbj", conv_low, recur_gate, preferred_element_type=jnp.float32
    ).reshape(tok_dev, channels)
    pre_input = jnp.einsum(
        "tbi,bij->tbj", conv_low, input_gate, preferred_element_type=jnp.float32
    ).reshape(tok_dev, channels)
    restart = same_list[1] == 0.0
    (carried, drive), gate_back = jax.vjp(
        partial(gate_math, restart=restart),
        pre_recur,
        pre_input,
        conv_out,
        recur_bias,
        input_bias,
        decay_param,
    )
    cum_decay, local_state = lax.associative_scan(compose, (carried, drive), axis=0)
    ones_row = jnp.ones((channels,), jnp.float32)
    zero_row = jnp.zeros((channels,), jnp.float32)
    incoming = prefix(
        (cum_decay[tok_dev - 1], local_state[tok_dev - 1]),
        "seq",
        compose,
        (ones_row, zero_row),
        False,
    )
    state = local_state + cum_decay * incoming[1]
    gelu_y, gelu_y_back = jax.vjp(jax.nn.gelu, branch_y)
    mixed_low = (gelu_y * state).astype(jnp.bfloat16)
    branch_part = jnp.dot(mixed_low, output_weight, preferred_element_type=jnp.float32)
    resid1 = full_in + lax.psum(branch_part, "tp")
    normed2, norm2_back = jax.vjp(rms_norm, resid1, second_gain)
    normed2_low = normed2.astype(jnp.bfloat16)
    resid_share = lax.dynamic_slice_in_dim(resid1, share_start, share_width, 1)
    hidden_cols = gate_weight.shape[1]
    weight_pieces = (
        lax.all_gather(gate_weight, "seq", axis=0, tiled=True),
        lax.all_gather(up_weight, "seq", axis=0, tiled=True),
    )
    columns = normed2_low
    gate_pre = jnp.dot(columns, weight_pieces[0], preferred_element_type=jnp.float32)
    up_pre = jnp.dot(columns, weight_pieces[1], preferred_element_type=jnp.float32)
    activated, act_back = jax.vjp(jax.nn.gelu, gate_pre)
    hid_low = (activated * up_pre).astype(jnp.bfloat16)
    mlp_part = jnp.dot(
        hid_low,
        lax.all_gather(down_weight, "seq", axis=1, tiled=True),
        preferred_element_type=jnp.float32,
    )
    mlp_share = lax.psum_scatter(mlp_part, "tp", scatter_dimension=1, tiled=True)
    block_out = (resid_share + mlp_share).astype(jnp.bfloat16)
    grad_full = grad_out.astype(jnp.float32)
    columns = grad_out
    d_hid = contract_last(columns, lax.all_gather(down_weight, "seq", axis=1, tiled=True))
    d_gate_low = act_back(d_hid * up_pre)[0].astype(jnp.bfloat16)
    d_up_low = (d_hid * activated).astype(jnp.bfloat16)
    weight_pieces = lax.all_gather((gate_weight, up_weight), "seq", axis=0, tiled=True)
    d_norm2_part = contract_last(d_gate_low, weight_pieces[0]) + contract_last(
        d_up_low, weight_pieces[1]
    )
    d_norm2 = lax.psum(d_norm2_part, "tp")
    d_resid_from2, grad_second = norm2_back(d_norm2)
    d_resid1 = grad_full + d_resid_from2
    d_resid_low = d_resid1.astype(jnp.bfloat16)
    d_resid_share = lax.dynamic_slice_in_dim(d_resid1, share_start, share_width, 1)
    mlp_grads = lax.psum_scatter(
        jnp.concatenate(
            [
                contract_first(normed2_low, d_gate_low),
                contract_first(normed2_low, d_up_low),
                contract_first(grad_out, hid_low),
            ],
            axis=1,
        ),
        "seq",
        scatter_dimension=0,
        tiled=True,
    )
    grad_gate_weight = mlp_grads[:, :hidden_cols]
    grad_up_weight = mlp_grads[:, hidden_cols : 2 * hidden_cols]
    grad_down_weight = mlp_grads[:, 2 * hidden_cols :].T
    d_mixed = contract_last(d_resid_low, output_weight)
    grad_out_weight = contract_first(mixed_low, d_resid_low)
    d_state = d_mixed * gelu_y
    d_branch_y = gelu_y_back(d_mixed * state)[0]
    lead_matrix = (col_grid == row_grid + 1).astype(jnp.float32)
    last_mark = (token_place == tok_dev - 1).astype(jnp.float32)
    first_mark = (token_place == 0).astype(jnp.float32)
    coefficient = exact_dot(lead_matrix, carried) + last_mark
    rev_decay, local_grad = lax.associative_scan(
        compose, (coefficient, d_state), reverse=True, axis=0
    )
    outgoing = (carried[0] * rev_decay[0], carried[0] * local_grad[0])
    from_above = prefix(outgoing, "seq", compose, (ones_row, zero_row), True)
    d_state_all = local_grad + rev_decay * from_above[1]
    trail_matrix = (col_grid == row_grid - 1).astype(jnp.float32)
    prev_state = exact_dot(trail_matrix, state) + first_mark * incoming[1]
    d_pre_recur, d_pre_input, d_conv_direct, grad_rbias, grad_ibias, grad_decay = gate_back(
        (d_state_all * prev_state, d_state_all)
    )
    d_recur_low = d_pre_recur.astype(jnp.bfloat16).reshape(tok_dev, blocks_here, block_size)
    d_input_low = d_pre_input.astype(jnp.bfloat16).reshape(tok_dev, blocks_here, block_size)
    grad_recur_gate = jnp.einsum(
        "tbi,tbj->bij", conv_low, d_recur_low, preferred_element_type=jnp.float32
    )
    grad_input_gate = jnp.einsum(
        "tbi,tbj->bij", conv_low, d_input_low, preferred_element_type=jnp.float32
    )
    d_conv_gates = jnp.einsum(
        "tbj,bij->tbi", d_recur_low, recur_gate, preferred_element_type=jnp.float32
    ) + jnp.einsum("tbj,bij->tbi", d_input_low, input_gate, preferred_element_type=jnp.float32)
    d_conv = d_conv_direct + d_conv_gates.reshape(tok_dev, channels)
    grad_conv_bias = jnp.sum(d_conv, axis=0)
    grad_conv_weight = jnp.stack(
        [jnp.sum(d_conv * window_list[offset], axis=0) for offset in range(conv_taps)], axis=0
    )
    tap_grads = [conv_weight[offset] * d_conv for offset in range(conv_taps)]
    d_local = sum((exact_first(lag_list[offset], tap_grads[offset]) for offset in range(conv_taps)))
    d_edge = sum((exact_first(edge_list[offset], tap_grads[offset]) for offset in range(conv_taps)))
    back_rows, next_first = shifted((d_edge, ids_float[:1]), "seq", -1)
    tail_matrix = (edge_rows == tok_dev - halo_rows + edge_cols).astype(jnp.float32)
    d_branch_x = d_local + exact_dot(tail_matrix, back_rows)
    d_x_low = d_branch_x.astype(jnp.bfloat16)
    d_y_low = d_branch_y.astype(jnp.bfloat16)
    grad_in_weight = contract_first(normed1_low, d_x_low)
    grad_gelu_weight = contract_first(normed1_low, d_y_low)
    d_norm1_part = contract_last(d_x_low, input_weight) + contract_last(d_y_low, gelu_weight)
    d_norm1 = lax.psum(d_norm1_part, "tp")
    d_in_from1, grad_first = norm1_back(d_norm1)
    grad_in = (
        d_resid_share + lax.dynamic_slice_in_dim(d_in_from1, share_start, share_width, 1)
    ).astype(jnp.bfloat16)
    next_first = jnp.where(final_device, -1.0, next_first)
    next_ids = jnp.concatenate([ids_float[1:], next_first])
    segment_ends = (next_ids != ids_float).astype(jnp.float32)[:, None]
    member = (segment_ids[:, None] == jnp.arange(SEGS, dtype=jnp.int32)[None, :]).astype(
        jnp.float32
    )
    final_part = lax.dot_general(
        member,
        state * segment_ends,
        (((0,), (0,)), ((), ())),
        precision=lax.Precision.HIGHEST,
        preferred_element_type=jnp.float32,
    )
    summed = lax.psum(
        (
            grad_in_weight,
            grad_gelu_weight,
            grad_out_weight,
            grad_conv_weight,
            grad_conv_bias,
            grad_recur_gate,
            grad_input_gate,
            grad_rbias,
            grad_ibias,
            grad_decay,
            grad_first,
            grad_second,
            final_part,
        ),
        "seq",
    )
    return (
        block_out,
        grad_in,
        summed[10],
        summed[0],
        summed[1],
        summed[3],
        summed[4],
        summed[5],
        summed[6],
        summed[7],
        summed[8],
        summed[9],
        summed[2],
        summed[11],
        grad_gate_weight,
        grad_up_weight,
        grad_down_weight,
        summed[12],
    )


def solution(mesh):
    return jax.shard_map(
        on_device,
        mesh=mesh,
        in_specs=(
            P("seq", "tp"),
            P("seq"),
            P(),
            P(None, "tp"),
            P(None, "tp"),
            P(None, "tp"),
            P("tp"),
            P("tp", None, None),
            P("tp", None, None),
            P("tp"),
            P("tp"),
            P("tp"),
            P("tp", None),
            P(),
            P("seq", "tp"),
            P("seq", "tp"),
            P("tp", "seq"),
            P("seq", None),
        ),
        out_specs=(
            P("seq", "tp"),
            P("seq", "tp"),
            P(),
            P(None, "tp"),
            P(None, "tp"),
            P(None, "tp"),
            P("tp"),
            P("tp", None, None),
            P("tp", None, None),
            P("tp"),
            P("tp"),
            P("tp"),
            P("tp", None),
            P(),
            P("seq", "tp"),
            P("seq", "tp"),
            P("tp", "seq"),
            P(None, "tp"),
        ),
        check_vma=False,
    )
```

profile of v0, /device:TPU:0, one launch (start us, length us, event | category | flops | bytes accessed | tf_op | source)
XLA Modules:
  0.0 4483.2 jit_solution(468092202798711800)
XLA Ops:
  20.0 73.9 %all-gather.9.cloned.1.call-done = bf16[1024,2048]{1,0:T(8,128)(2,1)} async-done(((bf16[1024,512]{1,0:T(8,128)(2,1)}), bf16[1024,2048]{1,0:T(8,128)(2,1)}) %all-gather.9.cloned.1.call-update) | async-done | bytes 4194320 | tf_op jit(solution)/shard_map/all_gather | solution.py:117
  166.0 51.2 %slice.745 = f32[511,704]{0,1:T(8,128)} slice(f32[1024,704]{0,1:T(8,128)} %copy-done.17), slice={[2:1024:2], [0:704:1]} | slice | bytes 2877952 | tf_op jit(solution)/shard_map/slice | solution.py:167
  217.2 51.3 %slice.675 = f32[512,704]{0,1:T(8,128)} slice(f32[1024,704]{0,1:T(8,128)} %copy-done.17), slice={[1:1024:2], [0:704:1]} | slice | bytes 2883584 | tf_op jit(solution)/shard_map/slice | solution.py:167
  268.5 51.2 %slice.674 = f32[512,704]{0,1:T(8,128)} slice(f32[1024,704]{0,1:T(8,128)} %copy-done.17), slice={[0:1023:2], [0:704:1]} | slice | bytes 2883584 | tf_op jit(solution)/shard_map/slice | solution.py:167
  323.6 51.6 %slice.677 = f32[512,704]{0,1:T(8,128)} slice(f32[1024,704]{0,1:T(8,128)} %copy-done.16), slice={[0:1023:2], [0:704:1]} | slice | bytes 2883584 | tf_op jit(solution)/shard_map/slice | solution.py:167
  375.2 51.3 %slice.673 = f32[512,704]{0,1:T(8,128)} slice(f32[1024,704]{0,1:T(8,128)} %copy-done.16), slice={[1:1024:2], [0:704:1]} | slice | bytes 2883584 | tf_op jit(solution)/shard_map/slice | solution.py:167
  432.9 28.2 slice.743
  461.1 28.5 slice.681
  489.6 28.3 slice.680
  519.6 28.3 slice.683
  547.9 28.3 slice.679
  576.3 28.4 slice.678
  884.9 51.3 %slice.672 = f32[511,704]{0,1:T(8,128)} slice(f32[1024,704]{0,1:T(8,128)} %copy-done.16), slice={[2:1024:2], [0:704:1]} | slice | bytes 2877952 | tf_op jit(solution)/shard_map/slice | solution.py:167
  1169.7 28.8 pad.280
  1198.5 28.7 pad.260
  1227.2 28.7 pad.261
  1255.9 28.9 pad.281
  1288.0 57.1 %pad.283 = f32[1024,704]{0,1:T(8,128)} pad(f32[512,704]{0,1:T(8,128)} %add.730, f32[]{:T(128)} %constant.114.clone.1), padding=1_0_1x0_0_0 | pad | bytes 4325380 | tf_op jit(solution)/shard_map/pad | solution.py:167
  1354.5 57.2 %pad.282 = f32[1024,704]{0,1:T(8,128)} pad(f32[512,704]{0,1:T(8,128)} %pad_maximum_fusion.2, f32[]{:T(128)} %constant.114.clone.1), padding=0_1_1x0_0_0 | pad | bytes 4325380 | tf_op jit(solution)/shard_map/pad | solution.py:167
  1422.4 57.1 %pad.263 = f32[1024,704]{0,1:T(8,128)} pad(f32[512,704]{0,1:T(8,128)} %add.719, f32[]{:T(128)} %constant.114.clone.1), padding=1_0_1x0_0_0 | pad | bytes 4325380 | tf_op jit(solution)/shard_map/pad | solution.py:167
  1482.4 57.1 %pad.262 = f32[1024,704]{0,1:T(8,128)} pad(f32[512,704]{0,1:T(8,128)} %pad_maximum_fusion.1, f32[]{:T(128)} %constant.114.clone.1), padding=0_1_1x0_0_0 | pad | bytes 4325380 | tf_op jit(solution)/shard_map/pad | solution.py:167
  1569.9 287.2 %all-reduce.87.cloned.1.call-done = f32[1024,2048]{1,0:T(8,128)} async-done(((f32[1024,2048]{1,0:T(8,128)}), f32[1024,2048]{1,0:T(8,128)}) %all-reduce.87.cloned.1.call-update) | async-done | bytes 8388624 | tf_op jit(solution)/shard_map/psum | solution.py:181
  1940.5 51.5 %slice.777 = f32[512,704]{0,1:T(8,128)} slice(f32[1024,704]{0,1:T(8,128)} %copy-done.46), slice={[1:1024:2], [0:704:1]} | slice | bytes 2883584 | tf_op jit(solution)/shard_map/slice | solution.py:240
  1991.9 51.2 %slice.770 = f32[512,704]{0,1:T(8,128)} slice(f32[1024,704]{0,1:T(8,128)} %copy-done.46), slice={[0:1023:2], [0:704:1]} | slice | bytes 2883584 | tf_op jit(solution)/shard_map/slice | solution.py:240
  2043.2 51.3 %slice.768 = f32[511,704]{0,1:T(8,128)} slice(f32[1024,704]{0,1:T(8,128)} %copy-done.46), slice={[1:1022:2], [0:704:1]} | slice | bytes 2877952 | tf_op jit(solution)/shard_map/slice | solution.py:240
  2146.3 74.1 %all-reduce.89.cloned.1.call-done = f32[1024,2048]{1,0:T(8,128)} async-done(((f32[1024,2048]{1,0:T(8,128)}), f32[1024,2048]{1,0:T(8,128)}) %all-reduce.89.cloned.1.call-update) | async-done | bytes 8388624 | tf_op jit(solution)/shard_map/psum | solution.py:211
  2247.3 51.3 %slice.774 = f32[512,704]{0,1:T(8,128)} slice(f32[1024,704]{0,1:T(8,128)} %get-tuple-element.297), slice={[0:1023:2], [0:704:1]} | slice | bytes 2883584 | tf_op jit(solution)/shard_map/slice | solution.py:240
  2298.6 51.3 %slice.772 = f32[512,704]{0,1:T(8,128)} slice(f32[1024,704]{0,1:T(8,128)} %get-tuple-element.297), slice={[1:1024:2], [0:704:1]} | slice | bytes 2883584 | tf_op jit(solution)/shard_map/slice | solution.py:240
  2381.3 28.7 slice.782
  2410.0 28.3 slice.781
  2438.3 28.3 slice.784
  2466.6 28.3 slice.780
  2682.4 51.3 %slice.846 = f32[511,704]{0,1:T(8,128)} slice(f32[1024,704]{0,1:T(8,128)} %get-tuple-element.297), slice={[1:1022:2], [0:704:1]} | slice | bytes 2877952 | tf_op jit(solution)/shard_map/slice | solution.py:240
  2737.2 28.2 slice.844
  2765.4 28.2 slice.779
  3155.2 28.6 pad.320
  3186.1 28.7 pad.300
  3214.8 29.0 pad.301
  3243.7 28.7 pad.321
  3282.7 57.1 %pad.302 = f32[1024,704]{0,1:T(8,128)} pad(f32[512,704]{0,1:T(8,128)} %pad_maximum_fusion.3, f32[]{:T(128)} %constant.114.clone.1), padding=0_1_1x0_0_0 | pad | bytes 4325380 | tf_op jit(solution)/shard_map/pad | solution.py:240
  3339.8 57.2 %pad.303 = f32[1024,704]{0,1:T(8,128)} pad(f32[512,704]{0,1:T(8,128)} %add.769, f32[]{:T(128)} %constant.114.clone.1), padding=1_0_1x0_0_0 | pad | bytes 4325380 | tf_op jit(solution)/shard_map/pad | solution.py:240
  3402.1 25.7 rev.8
  3430.7 57.1 %pad.322 = f32[1024,704]{0,1:T(8,128)} pad(f32[512,704]{0,1:T(8,128)} %pad_maximum_fusion.4, f32[]{:T(128)} %constant.114.clone.1), padding=0_1_1x0_0_0 | pad | bytes 4325380 | tf_op jit(solution)/shard_map/pad | solution.py:240
  3487.8 57.3 %pad.323 = f32[1024,704]{0,1:T(8,128)} pad(f32[512,704]{0,1:T(8,128)} %add.780, f32[]{:T(128)} %constant.114.clone.1), padding=1_0_1x0_0_0 | pad | bytes 4325380 | tf_op jit(solution)/shard_map/pad | solution.py:240
  3550.2 25.7 rev.9
  3789.2 197.0 %all-reduce.91.cloned.1.call-done = f32[1024,2048]{1,0:T(8,128)} async-done(((f32[1024,2048]{1,0:T(8,128)}), f32[1024,2048]{1,0:T(8,128)}) %all-reduce.91.cloned.1.call-update) | async-done | bytes 8388624 | tf_op jit(solution)/shard_map/psum | solution.py:278
  4025.6 188.5 %reduce-scatter.5.cloned.1.call-done = f32[256,4608]{0,1:T(8,128)} async-done(((f32[2048,4608]{0,1:T(8,128)}), f32[256,4608]{0,1:T(8,128)}) %reduce-scatter.5.cloned.1.call-update) | async-done | bytes 4718608 | tf_op jit(solution)/shard_map/reduce_scatter | solution.py:216
  4224.8 236.9 %all-reduce.93.cloned.1.call-done = (f32[2048,704]{0,1:T(8,128)}, f32[2048,704]{0,1:T(8,128)}, f32[4,176,176]{2,1,0:T(8,128)}, f32[4,176,176]{2,1,0:T(8,128)}, f32[704,2048]{1,0:T(8,128)}) async-done(((f32[2048,704]{0,1:T(8,128)}, f32[2048,704]{0,1:T(8,128)}, f32[4,176,176]{2,1,0:T(8,128)}, f32[4,176,176]{2,1,0:T(8,128)}, f32[704,2048]{1,0:T(8,128)}), (f32[2048,704]{0,1:T(8,128)}, f32[2048,704]{0,1:T(8,128)}, ...) | async-done | bytes 18292752 | tf_op jit(solution)/shard_map/psum | solution.py:296
  (787 shorter events, 1712.4 us)
Async XLA Ops:
  8.0 1542.1 %copy-start = (bf16[2048,704]{0,1:T(8,128)(2,1)S(1)}, bf16[2048,704]{0,1:T(8,128)(2,1)}, u32[]{:S(2)}) copy-start(bf16[2048,704]{0,1:T(8,128)(2,1)} %param.26) | copy-start | bytes 8650756
  8.0 89.7 %copy-start.137 = (f32[2048]{0:T(1024)S(1)}, f32[2048]{0:T(1024)}, u32[]{:S(2)}) copy-start(f32[2048]{0:T(1024)} %param.24) | copy-start | bytes 24580
  8.0 85.9 %all-gather.9.cloned.1.call-start = ((), (), s32[]{:S(2)}) async-start(), calls=%async_computation.2 | async-start | bytes 5242880 | tf_op jit(solution)/shard_map/all_gather | solution.py:117
  8.8 1848.3 %all-reduce.87.cloned.1.call-start = ((), (), s32[]{:S(2)}) async-start(), calls=%async_computation.3 | async-start | bytes 16777216 | tf_op jit(solution)/shard_map/psum | solution.py:181
  9.7 10.2 collective-permute-start
  12.5 5.4 collective-permute-start.3
  13.9 110.8 %copy-start.143 = (s32[1024]{0:T(1024)}, s32[1024]{0:T(1024)S(1)}, u32[]{:S(2)}) copy-start(s32[1024]{0:T(1024)S(1)} %iota_add_fusion.4) | copy-start | bytes 12292
  13.9 130.4 %copy-start.114 = (s32[1024]{0:T(1024)}, s32[1024]{0:T(1024)S(1)}, u32[]{:S(2)}) copy-start(s32[1024]{0:T(1024)S(1)} %iota_add_fusion.1) | copy-start | bytes 12292
  13.9 135.7 %copy-start.112 = (s32[1024]{0:T(1024)}, s32[1024]{0:T(1024)S(1)}, u32[]{:S(2)}) copy-start(s32[1024]{0:T(1024)S(1)} %iota_add_fusion.5) | copy-start | bytes 12292
  13.9 133.0 %copy-start.116 = (s32[1024]{0:T(1024)}, s32[1024]{0:T(1024)S(1)}, u32[]{:S(2)}) copy-start(s32[1024]{0:T(1024)S(1)} %iota_add_fusion.3) | copy-start | bytes 12292
  14.0 100.8 %copy-start.145 = (s32[1024]{0:T(1024)}, s32[1024]{0:T(1024)S(1)}, u32[]{:S(2)}) copy-start(s32[1024]{0:T(1024)S(1)} %iota_add_fusion.2) | copy-start | bytes 12292
  14.0 91.0 %copy-start.147 = (s32[1024]{0:T(1024)}, s32[1024]{0:T(1024)S(1)}, u32[]{:S(2)}) copy-start(s32[1024]{0:T(1024)S(1)} %iota_add_fusion) | copy-start | bytes 12292
  14.9 137.5 %copy-start.104 = (f32[704]{0:T(1024)}, f32[704]{0:T(1024)S(1)}, u32[]{:S(2)}) copy-start(f32[704]{0:T(1024)S(1)} %get-tuple-element.233) | copy-start | bytes 8452
  14.9 137.5 %copy-start.106 = (f32[704]{0:T(1024)}, f32[704]{0:T(1024)S(1)}, u32[]{:S(2)}) copy-start(f32[704]{0:T(1024)S(1)} %get-tuple-element.234) | copy-start | bytes 8452
  14.9 137.5 %copy-start.108 = (f32[704]{0:T(1024)}, f32[704]{0:T(1024)S(1)}, u32[]{:S(2)}) copy-start(f32[704]{0:T(1024)S(1)} %get-tuple-element.236) | copy-start | bytes 8452
  14.9 137.5 %copy-start.110 = (f32[704]{0:T(1024)}, f32[704]{0:T(1024)S(1)}, u32[]{:S(2)}) copy-start(f32[704]{0:T(1024)S(1)} %get-tuple-element.235) | copy-start | bytes 8452
  16.2 303.5 %copy-start.101 = (f32[704]{0:T(1024)}, f32[704]{0:T(1024)S(1)}, u32[]{:S(2)}) copy-start(f32[704]{0:T(1024)S(1)} %get-tuple-element.390) | copy-start | bytes 8452
  19.9 129.8 %copy-start.118 = (f32[1024]{0:T(1024)}, f32[1024]{0:T(1024)S(1)}, u32[]{:S(2)}) copy-start(f32[1024]{0:T(1024)S(1)} %get-tuple-element.388) | copy-start | bytes 12292
  20.0 124.3 %copy-start.122 = (f32[1024]{0:T(1024)}, f32[1024]{0:T(1024)S(1)}, u32[]{:S(2)}) copy-start(f32[1024]{0:T(1024)S(1)} %get-tuple-element.386) | copy-start | bytes 12292
  20.0 127.0 %copy-start.120 = (f32[1024]{0:T(1024)}, f32[1024]{0:T(1024)S(1)}, u32[]{:S(2)}) copy-start(f32[1024]{0:T(1024)S(1)} %get-tuple-element.285) | copy-start | bytes 12292
  20.0 132.4 %copy-start.124 = (f32[1024]{0:T(1024)}, f32[1024]{0:T(1024)S(1)}, u32[]{:S(2)}) copy-start(f32[1024]{0:T(1024)S(1)} %get-tuple-element.385) | copy-start | bytes 12292
  20.0 299.7 %copy-start.132 = (pred[1024]{0:T(1024)(128)(4,1)}, pred[1024]{0:T(1024)(128)(4,1)S(1)}, u32[]{:S(2)}) copy-start(pred[1024]{0:T(1024)(128)(4,1)S(1)} %get-tuple-element.284) | copy-start | bytes 3076
  97.8 1452.3 %copy-start.129 = (f32[1024]{0:T(1024)}, f32[1024]{0:T(1024)S(1)}, u32[]{:S(2)}) copy-start(f32[1024]{0:T(1024)S(1)} %fusion.172) | copy-start | bytes 12292
  103.0 41.3 collective-permute-start.1
  714.5 47.9 %copy-start.32 = (f32[128,704]{0,1:T(8,128)}, f32[128,704]{0,1:T(8,128)S(1)}, u32[]{:S(2)}) copy-start(f32[128,704]{0,1:T(8,128)S(1)} %get-tuple-element.384) | copy-start | bytes 1081348
  762.3 22.0 copy-start.35
  884.9 51.3 %copy-start.44 = (f32[16,704]{0,1:T(8,128)S(1)}, f32[16,704]{0,1:T(8,128)}, u32[]{:S(2)}) copy-start(f32[16,704]{0,1:T(8,128)} %get-tuple-element.377) | copy-start | bytes 135172
  1057.2 29.8 copy-start.33
  1102.6 45.4 %copy-start.89 = (f32[128,704]{0,1:T(8,128)S(1)}, f32[128,704]{0,1:T(8,128)}, u32[]{:S(2)}) copy-start(f32[128,704]{0,1:T(8,128)} %add.728) | copy-start | bytes 1081348
  1411.7 67.8 %copy-start.80 = (f32[1,704]{0,1:T(8,128)S(1)}, f32[1,704]{0,1:T(8,128)}, u32[]{:S(2)}) copy-start(f32[1,704]{0,1:T(8,128)} %slice.879) | copy-start | bytes 8452
  1568.1 300.9 %all-gather.13.cloned.1.call-start = ((), (), s32[]{:S(2)}) async-start(), calls=%async_computation.5 | async-start | bytes 7077888 | tf_op jit(solution)/shard_map/all_gather | solution.py:188
  1568.7 312.3 %all-gather.11.cloned.1.call-start = ((), (), s32[]{:S(2)}) async-start(), calls=%async_computation.4 | async-start | bytes 7077888 | tf_op jit(solution)/shard_map/all_gather | solution.py:187
  1569.3 323.5 %all-gather.15.cloned.1.call-start = ((), (), s32[]{:S(2)}) async-start(), calls=%async_computation.6 | async-start | bytes 7077888 | tf_op jit(solution)/shard_map/all_gather | solution.py:197
  1569.8 296.4 %copy-start.103 = (f32[2048]{0:T(1024)S(1)}, f32[2048]{0:T(1024)}, u32[]{:S(2)}) copy-start(f32[2048]{0:T(1024)} %param.35) | copy-start | bytes 24580
  1569.8 650.6 %all-reduce.89.cloned.1.call-start = ((), (), s32[]{:S(2)}) async-start(), calls=%async_computation.8 | async-start | bytes 16777216 | tf_op jit(solution)/shard_map/psum | solution.py:211
  1930.5 1855.1 %reduce-scatter.3.cloned.1.call-start = ((), (), s32[]{:S(2)}) async-start(), calls=%async_computation.7 | async-start | bytes 10485760 | tf_op jit(solution)/shard_map/reduce_scatter | solution.py:200
  2146.3 1839.9 %all-reduce.91.cloned.1.call-start = ((), (), s32[]{:S(2)}) async-start(), calls=%async_computation.9 | async-start | bytes 16777216 | tf_op jit(solution)/shard_map/psum | solution.py:278
  3088.0 46.5 %copy-start.90 = (f32[128,704]{0,1:T(8,128)S(1)}, f32[128,704]{0,1:T(8,128)}, u32[]{:S(2)}) copy-start(f32[128,704]{0,1:T(8,128)} %add.778) | copy-start | bytes 1081348
  3154.1 29.8 copy-start.84
  3402.1 25.7 copy-start.79
  3550.2 46.8 %copy-start.102 = (f32[704]{0:T(1024)S(1)}, f32[704]{0:T(1024)}, u32[]{:S(2)}) copy-start(f32[704]{0:T(1024)} %copy-done.101) | copy-start | bytes 8452
  3550.2 46.8 %copy-start.133 = (pred[1024]{0:T(1024)(128)(4,1)S(1)}, pred[1024]{0:T(1024)(128)(4,1)}, u32[]{:S(2)}) copy-start(pred[1024]{0:T(1024)(128)(4,1)} %copy-done.132) | copy-start | bytes 3076
  3642.6 42.3 collective-permute-start.2
  3696.2 517.9 %reduce-scatter.5.cloned.1.call-start = ((), (), s32[]{:S(2)}) async-start(), calls=%async_computation.10 | async-start | bytes 42467328 | tf_op jit(solution)/shard_map/reduce_scatter | solution.py:216
  3752.8 708.9 %all-reduce.93.cloned.1.call-start = ((), (), s32[]{:S(2)}) async-start(), calls=%async_computation.11 | async-start | bytes 37486592 | tf_op jit(solution)/shard_map/psum | solution.py:296
  3789.2 205.3 %copy-start.131 = (f32[2048]{0:T(1024)S(1)}, f32[2048]{0:T(1024)}, u32[]{:S(2)}) copy-start(f32[2048]{0:T(1024)} %get-tuple-element.220) | copy-start | bytes 24580
  3789.2 205.3 %copy-start.134 = (f32[704]{0:T(1024)S(1)}, f32[704]{0:T(1024)}, u32[]{:S(2)}) copy-start(f32[704]{0:T(1024)} %get-tuple-element.270) | copy-start | bytes 8452
  3789.2 230.8 %copy-start.127 = (f32[1024]{0:T(1024)S(1)}, f32[1024]{0:T(1024)}, u32[]{:S(2)}) copy-start(f32[1024]{0:T(1024)} %copy-done.126) | copy-start | bytes 12292
  (130 other events, 752.8 us)
Sparse Core Ops, SparseCore 0:
  10.5 83.4 all-gather.8
  1568.2 288.8 all-reduce.86
  1930.6 289.8 all-reduce.88
  2222.7 143.4 reduce-scatter.2
  3696.3 289.8 all-reduce.90
  3989.7 224.3 reduce-scatter.4
  4220.6 241.0 all-reduce.92
Sparse Core Ops, SparseCore 1:
  1570.4 43.4 all-gather.12
  1615.6 45.3 all-gather.10
  1662.8 46.5 all-gather.14
where the time goes:
time: 4510 us; the launch traced here: 4480 us
  local copies, waits for them, and re-layouts  2710 us (60%)
  waiting for transfers between devices  1060 us (24%)
  other arithmetic  323 us (7%)
  matrix products  302 us (7%)
  blocking collectives  61.7 us (1%)
    slice x63, local copies, waits for them, and re-layouts, on_device(): lax.associative_scan(compose, (coefficient, d_state), reverse=True, axis=0)  809 us
    slice x59, local copies, waits for them, and re-layouts, on_device(): lax.associative_scan(compose, (carried, drive), axis=0)  741 us
    pad x36, local copies, waits for them, and re-layouts, on_device(): lax.associative_scan(compose, (coefficient, d_state), reverse=True, axis=0)  508 us
    pad x36, local copies, waits for them, and re-layouts, on_device(): lax.associative_scan(compose, (carried, drive), axis=0)  500 us
    psum x1, waiting for transfers between devices, on_device(): resid1 = full_in + lax.psum(branch_part, 'tp')  287 us
    psum x1, waiting for transfers between devices, on_device(): lax.psum((grad_in_weight, grad_gelu_weight, grad_out_weight, grad_conv_we...  237 us
    psum x1, waiting for transfers between devices, on_device(): d_norm1 = lax.psum(d_norm1_part, 'tp')  197 us
    reduce_scatter x1, waiting for transfers between devices, on_device(): lax.psum_scatter(jnp.concatenate([contract_first(normed2_low, d_gate_low)...  189 us
  transfers between devices with their start and end apart: 14, of which 7 were waited for; matrix products, arithmetic and copies ran while one was open for 41% of the time, Pallas kernels for 0%

commit v1 on v0

v1 whole, which is shorter than its diff:
```python
import functools

import jax
import jax.numpy as jnp
from jax import lax
from jax.experimental import pallas as pl
from jax.experimental.pallas import tpu as pltpu
from jax.sharding import PartitionSpec as P

SEGS = 8
EPSILON = 1e-06
DECAY_SCALE = 8.0
GELU_C = 0.7978845608028654
GELU_A = 0.044715
F32 = jnp.float32
BF16 = jnp.bfloat16
VMEM_LIMIT = 48 << 20


def shifted(x, axis, by):
    peers = lax.axis_size(axis)
    pairs = [(i, i + by) for i in range(peers) if 0 <= i + by < peers]
    return lax.ppermute(x, axis, pairs)


def dot(left, right):
    return jnp.dot(left, right, preferred_element_type=F32)


def contract_first(left, right):
    return lax.dot_general(left, right, (((0,), (0,)), ((), ())), preferred_element_type=F32)


def contract_last(left, right):
    return lax.dot_general(left, right, (((1,), (1,)), ((), ())), preferred_element_type=F32)


def gelu_parts(y):
    y2 = y * y
    t = jnp.tanh(GELU_C * y * (1.0 + GELU_A * y2))
    half = 0.5 * (1.0 + t)
    slope = half + 0.5 * y * (1.0 - t * t) * (GELU_C * (1.0 + 3.0 * GELU_A * y2))
    return y * half, slope


def gelu(y):
    return y * (0.5 * (1.0 + jnp.tanh(GELU_C * y * (1.0 + GELU_A * y * y))))


def retained(log_decay, carried):
    y = 2.0 * log_decay
    series = -y * (
        1.0
        + y
        * (1 / 2 + y * (1 / 6 + y * (1 / 24 + y * (1 / 120 + y * (1 / 720 + y * (1 / 5040))))))
    )
    return jnp.maximum(jnp.where(y > -0.25, series, 1.0 - carried * carried), 1e-36)


def block_scan(a, b, reverse):
    row = lax.broadcasted_iota(jnp.int32, a.shape, 0)
    for s in (1, 2, 4):
        by = 8 - s if reverse else s
        live = row < 8 - s if reverse else row >= s
        b_shift = pltpu.roll(b, by, 0)
        a_shift = pltpu.roll(a, by, 0)
        b = b + a * jnp.where(live, b_shift, 0.0)
        a = a * jnp.where(live, a_shift, 1.0)
    return a, b


def forward_kernel(
    bx_ref, prev_ref, mask_ref, par_ref, gates_ref,
    conv_ref, low_ref, r_ref, i_ref, state_ref, decay_ref,
    window, pre, carry,
):
    rows, width = bx_ref.shape
    tile = pl.program_id(0)

    @pl.when(tile == 0)
    def _():
        window[pl.ds(0, 8), :] = prev_ref[...]
        carry[pl.ds(0, 8), :] = jnp.zeros((8, width), F32)
        carry[pl.ds(8, 8), :] = jnp.ones((8, width), F32)

    @pl.when(tile > 0)
    def _():
        window[pl.ds(0, 8), :] = window[pl.ds(rows, 8), :]

    window[pl.ds(8, rows), :] = bx_ref[...]

    def conv_step(j, _):
        at = pl.multiple_of(j * 16, 16)
        win = window[pl.ds(at, 24), :]
        mask = mask_ref[pl.ds(at, 16), :]
        out = par_ref[pl.ds(0, 1), :] + par_ref[pl.ds(1, 1), :] * win[8:24]
        for k in range(1, 4):
            out = out + par_ref[pl.ds(1 + k, 1), :] * (win[8 - k : 24 - k] * mask[:, k : k + 1])
        conv_ref[pl.ds(at, 16), :] = out
        low_ref[pl.ds(at, 16), :] = out.astype(BF16)
        return 0

    lax.fori_loop(0, rows // 16, conv_step, 0)
    pre[...] = dot(low_ref[...], gates_ref[...])

    def scan_step(j, _):
        at = pl.multiple_of(j * 8, 8)
        here = pl.ds(at, 8)
        keep = mask_ref[here, :][:, 1:2]
        r = jax.nn.sigmoid(pre[here, pl.ds(0, width)] + par_ref[pl.ds(5, 1), :])
        i = jax.nn.sigmoid(pre[here, pl.ds(width, width)] + par_ref[pl.ds(6, 1), :])
        log_decay = par_ref[pl.ds(7, 1), :] * r
        a = jnp.exp(log_decay)
        e = retained(log_decay, a)
        s = e * lax.rsqrt(e)
        r_ref[here, :] = r
        i_ref[here, :] = i
        whole = jnp.broadcast_to(keep, a.shape) != 0.0
        b = jnp.where(whole, s, 1.0) * (i * conv_ref[here, :])
        a = jnp.where(whole, a, 0.0)
        a, b = block_scan(a, b, False)
        state = b + a * carry[pl.ds(0, 8), :]
        decay = a * carry[pl.ds(8, 8), :]
        state_ref[here, :] = state
        decay_ref[here, :] = decay
        carry[pl.ds(0, 8), :] = jnp.broadcast_to(state[7:8], state.shape)
        carry[pl.ds(8, 8), :] = jnp.broadcast_to(decay[7:8], state.shape)
        return 0

    lax.fori_loop(0, rows // 8, scan_step, 0)


def forward_recurrence(bx, prev_rows, masks, params, gates):
    tokens, width = bx.shape
    rows = min(128, tokens)
    wide = pl.BlockSpec((rows, width), lambda t: (t, 0))
    whole = lambda a: pl.BlockSpec(a.shape, lambda t: (0,) * a.ndim)
    shape = lambda d: jax.ShapeDtypeStruct((tokens, width), d)
    return pl.pallas_call(
        forward_kernel,
        name="forward_recurrence",
        grid=(tokens // rows,),
        in_specs=[
            wide, whole(prev_rows), pl.BlockSpec((rows, 8), lambda t: (t, 0)), whole(params),
            whole(gates),
        ],
        out_specs=[wide] * 6,
        out_shape=[shape(F32), shape(BF16), shape(F32), shape(F32), shape(F32), shape(F32)],
        scratch_shapes=[
            pltpu.VMEM((rows + 8, width), F32),
            pltpu.VMEM((rows, 2 * width), F32),
            pltpu.VMEM((16, width), F32),
        ],
        compiler_params=pltpu.CompilerParams(
            dimension_semantics=("arbitrary",), vmem_limit_bytes=VMEM_LIMIT
        ),
        cost_estimate=pl.CostEstimate(
            flops=4 * tokens * width * width, bytes_accessed=30 * tokens * width,
            transcendentals=6 * tokens * width,
        ),
    )(bx, prev_rows, masks, params, gates)


def reverse_kernel(
    dm_ref, by_ref, r_ref, state_ref, mask_ref, par_ref,
    grad_ref, reach_ref, dby_ref, head_ref, carry,
):
    rows, width = dm_ref.shape

    @pl.when(pl.program_id(0) == 0)
    def _():
        carry[pl.ds(0, 8), :] = jnp.zeros((8, width), F32)
        carry[pl.ds(8, 8), :] = jnp.ones((8, width), F32)

    groups = rows // 16

    def step(j, _):
        base = pl.multiple_of((groups - 1 - j) * 16, 16)
        slopes = []
        for half in (1, 0):
            at = pl.multiple_of(base + 8 * half, 8)
            here = pl.ds(at, 8)
            dm = dm_ref[here, :]
            act, slope = gelu_parts(by_ref[here, :])
            slopes.append(slope * (state_ref[here, :] * dm))
            keep = mask_ref[here, :][:, 1:2]
            a = jnp.exp(par_ref[pl.ds(7, 1), :] * r_ref[here, :])
            a = jnp.where(jnp.broadcast_to(keep, a.shape) != 0.0, a, 0.0)
            dh = dm * act
            acc, u = block_scan(a, a * dh, True)
            u_next = carry[pl.ds(0, 8), :]
            reach_next = carry[pl.ds(8, 8), :]
            u = u + acc * u_next
            reach = acc * reach_next
            last = lax.broadcasted_iota(jnp.int32, u.shape, 0) == 7
            grad_ref[here, :] = dh + jnp.where(last, u_next, pltpu.roll(u, 7, 0))
            reach_ref[here, :] = jnp.where(last, reach_next, pltpu.roll(reach, 7, 0))
            carry[pl.ds(0, 8), :] = jnp.broadcast_to(u[0:1], u.shape)
            carry[pl.ds(8, 8), :] = jnp.broadcast_to(reach[0:1], u.shape)
        dby_ref[pl.ds(base, 16), :] = jnp.concatenate(slopes[::-1], axis=0).astype(BF16)
        return 0

    lax.fori_loop(0, groups, step, 0)
    head_ref[...] = carry[...]


def reverse_recurrence(dm, by, r, state, masks, params):
    tokens, width = dm.shape
    rows = min(128, tokens)
    tiles = tokens // rows
    wide = pl.BlockSpec((rows, width), lambda t: (tiles - 1 - t, 0))
    whole = lambda a: pl.BlockSpec(a.shape, lambda t: (0,) * a.ndim)
    shape = lambda d: jax.ShapeDtypeStruct((tokens, width), d)
    return pl.pallas_call(
        reverse_kernel,
        name="reverse_recurrence",
        grid=(tiles,),
        in_specs=[
            wide, wide, wide, wide, pl.BlockSpec((rows, 8), lambda t: (tiles - 1 - t, 0)),
            whole(params),
        ],
        out_specs=[wide, wide, wide, pl.BlockSpec((16, width), lambda t: (0, 0))],
        out_shape=[shape(F32), shape(F32), shape(BF16), jax.ShapeDtypeStruct((16, width), F32)],
        scratch_shapes=[pltpu.VMEM((16, width), F32)],
        compiler_params=pltpu.CompilerParams(
            dimension_semantics=("arbitrary",), vmem_limit_bytes=VMEM_LIMIT
        ),
        cost_estimate=pl.CostEstimate(
            flops=60 * tokens * width, bytes_accessed=28 * tokens * width,
            transcendentals=2 * tokens * width,
        ),
    )(dm, by, r, state, masks, params)


def gate_grad_kernel(
    grad_ref, reach_ref, r_ref, i_ref, conv_ref, state_ref, before_ref, bx_ref, bx_before_ref,
    mask_ref, low_ref, prev_ref, ends_ref, par_ref, gates_ref,
    dbx_ref, tail_ref, edge_ref, sums_ref, gate_ref,
    window, states, pair, direct, spread,
):
    rows, width = grad_ref.shape
    step_at = pl.program_id(0)
    tiles = pl.num_programs(0)
    first = step_at == tiles - 1

    @pl.when(step_at == 0)
    def _():
        sums_ref[...] = jnp.zeros_like(sums_ref)
        spread[...] = jnp.zeros_like(spread)

    @pl.when(first)
    def _():
        window[pl.ds(0, 8), :] = prev_ref[...]
        states[pl.ds(0, 8), :] = jnp.broadcast_to(ends_ref[pl.ds(0, 1), :], (8, width))

    @pl.when(jnp.logical_not(first))
    def _():
        window[pl.ds(0, 8), :] = bx_before_ref[...]
        states[pl.ds(0, 8), :] = before_ref[...]

    window[pl.ds(8, rows), :] = bx_ref[...]
    states[pl.ds(8, rows), :] = state_ref[...]

    def gates_step(j, sums):
        sum_r, sum_i, sum_d = sums
        at = pl.multiple_of(j * 16, 16)
        outs = []
        for half in (0, 1):
            off = pl.multiple_of(at + 8 * half, 8)
            here = pl.ds(off, 8)
            grad = grad_ref[here, :] + reach_ref[here, :] * ends_ref[pl.ds(1, 1), :]
            r, i = r_ref[here, :], i_ref[here, :]
            conv = conv_ref[here, :]
            keep = jnp.broadcast_to(mask_ref[here, :][:, 1:2], grad.shape) != 0.0
            log_decay = par_ref[pl.ds(7, 1), :] * r
            a = jnp.exp(log_decay)
            e = retained(log_decay, a)
            inv = lax.rsqrt(e)
            s = jnp.where(keep, e * inv, 1.0)
            states_win = states[pl.ds(off, 16), :]
            before = states_win[7:15]
            gi = grad * i
            d_log = jnp.where(keep, a * (grad * before - gi * conv * a * inv), 0.0)
            d_pa = d_log * par_ref[pl.ds(7, 1), :] * r * (1.0 - r)
            gs = gi * s
            d_pi = gs * conv * (1.0 - i)
            direct[here, :] = gs
            sum_r = sum_r + d_pa
            sum_i = sum_i + d_pi
            sum_d = sum_d + d_log * r
            outs.append((d_pa, d_pi))
        pair[pl.ds(at, 16), pl.ds(0, width)] = jnp.concatenate([o[0] for o in outs], 0).astype(BF16)
        pair[pl.ds(at, 16), pl.ds(width, width)] = jnp.concatenate([o[1] for o in outs], 0).astype(BF16)
        return sum_r, sum_i, sum_d

    zero = jnp.zeros((8, width), F32)
    sum_r, sum_i, sum_d = lax.fori_loop(0, rows // 16, gates_step, (zero, zero, zero))
    for n, total in enumerate((sum_r, sum_i, sum_d)):
        sums_ref[pl.ds(8 * n, 8), :] += total

    part = contract_first(low_ref[...], pair[...])

    @pl.when(step_at == 0)
    def _():
        gate_ref[...] = part

    @pl.when(step_at > 0)
    def _():
        gate_ref[...] += part

    direct[...] += contract_last(pair[...], gates_ref[...])

    for k in range(1, 4):
        spread[k - 1, pl.ds(rows, 8), :] = spread[k - 1, pl.ds(0, 8), :]

    def conv_step(j, sums):
        at = pl.multiple_of(j * 8, 8)
        here = pl.ds(at, 8)
        d_conv = direct[here, :]
        mask = mask_ref[here, :]
        win = window[pl.ds(at, 16), :]
        out = [sums[0] + d_conv, sums[1] + d_conv * win[8:16]]
        for k in range(1, 4):
            masked = d_conv * mask[:, k : k + 1]
            spread[k - 1, here, :] = masked
            out.append(sums[k + 1] + masked * win[8 - k : 16 - k])
        return tuple(out)

    totals = lax.fori_loop(0, rows // 8, conv_step, (zero,) * 5)
    for n, total in enumerate(totals):
        sums_ref[pl.ds(24 + 8 * n, 8), :] += total

    def back_step(j, _):
        at = pl.multiple_of(j * 16, 16)
        out = par_ref[pl.ds(1, 1), :] * direct[pl.ds(at, 16), :]
        for k in range(1, 4):
            win = spread[k - 1, pl.ds(at, 24), :]
            out = out + par_ref[pl.ds(1 + k, 1), :] * win[k : 16 + k]
        direct[pl.ds(at, 16), :] = out
        dbx_ref[pl.ds(at, 16), :] = out.astype(BF16)
        return 0

    lax.fori_loop(0, rows // 16, back_step, 0)

    @pl.when(step_at == 0)
    def _():
        tail_ref[...] = direct[pl.ds(rows - 8, 8), :]

    @pl.when(first)
    def _():
        row = lax.broadcasted_iota(jnp.int32, (8, width), 0)
        edge = jnp.zeros((8, width), F32)
        for k in range(1, 4):
            head = pltpu.roll(spread[k - 1, pl.ds(0, 8), :], 8 - k, 0)
            edge = edge + par_ref[pl.ds(1 + k, 1), :] * jnp.where(row >= 8 - k, head, 0.0)
        edge_ref[...] = edge


def gate_gradients(grad, reach, r, i, conv, state, bx, masks, low, prev_rows, ends, params, gates):
    tokens, width = grad.shape
    rows = min(128, tokens)
    tiles = tokens // rows
    wide = pl.BlockSpec((rows, width), lambda t: (tiles - 1 - t, 0))
    before = pl.BlockSpec(
        (8, width), lambda t: (jnp.maximum((tiles - 1 - t) * (rows // 8) - 1, 0), 0)
    )
    whole = lambda a: pl.BlockSpec(a.shape, lambda t: (0,) * a.ndim)
    fixed = lambda *dims: pl.BlockSpec(dims, lambda t: (0,) * len(dims))
    return pl.pallas_call(
        gate_grad_kernel,
        name="gate_gradients",
        grid=(tiles,),
        in_specs=[
            wide, wide, wide, wide, wide, wide, before, wide, before,
            pl.BlockSpec((rows, 8), lambda t: (tiles - 1 - t, 0)), wide, whole(prev_rows),
            whole(ends), whole(params), whole(gates),
        ],
        out_specs=[
            wide, fixed(8, width), fixed(8, width), fixed(64, width), fixed(width, 2 * width),
        ],
        out_shape=[
            jax.ShapeDtypeStruct((tokens, width), BF16),
            jax.ShapeDtypeStruct((8, width), F32),
            jax.ShapeDtypeStruct((8, width), F32),
            jax.ShapeDtypeStruct((64, width), F32),
            jax.ShapeDtypeStruct((width, 2 * width), F32),
        ],
        scratch_shapes=[
            pltpu.VMEM((rows + 8, width), F32),
            pltpu.VMEM((rows + 8, width), F32),
            pltpu.VMEM((rows, 2 * width), BF16),
            pltpu.VMEM((rows, width), F32),
            pltpu.VMEM((3, rows + 8, width), F32),
        ],
        compiler_params=pltpu.CompilerParams(
            dimension_semantics=("arbitrary",), vmem_limit_bytes=VMEM_LIMIT
        ),
        cost_estimate=pl.CostEstimate(
            flops=8 * tokens * width * width, bytes_accessed=32 * tokens * width,
            transcendentals=2 * tokens * width,
        ),
    )(grad, reach, r, i, conv, state, state, bx, bx, masks, low, prev_rows, ends, params, gates)


def chained(decays, values, place, reverse):
    count = decays.shape[0]
    total = jnp.zeros_like(values[0])
    for hop in range(count - 1):
        source = count - 1 - hop if reverse else hop
        live = source > place if reverse else source < place
        total = jnp.where(live, values[source] + decays[source] * total, total)
    return total


def block_diagonal(blocks):
    count, size, _ = blocks.shape
    rows = [
        jnp.pad(blocks[b], ((0, 0), (b * size, (count - 1 - b) * size))) for b in range(count)
    ]
    return jnp.concatenate(rows, axis=0)


def on_device(
    hidden_in, segment_ids, first_gain, input_weight, gelu_weight, conv_weight, conv_bias,
    recur_gate, input_gate, recur_bias, input_bias, decay_param, output_weight, second_gain,
    gate_weight, up_weight, down_weight, grad_out,
):
    tokens, share = hidden_in.shape
    channels = input_weight.shape[1]
    taps = conv_weight.shape[0]
    halo = taps - 1
    blocks, size = recur_gate.shape[0], recur_gate.shape[1]
    width = grad_out.shape[1]
    seq_devices = lax.axis_size("seq")
    seq_place = lax.axis_index("seq")
    share_start = lax.axis_index("tp") * share

    gate_full = lax.all_gather(gate_weight, "seq", axis=0, tiled=True)
    up_full = lax.all_gather(up_weight, "seq", axis=0, tiled=True)
    down_full = lax.all_gather(down_weight, "seq", axis=1, tiled=True)

    ids = segment_ids.astype(F32)
    prev_ids = shifted(ids[tokens - halo :], "seq", 1)
    prev_ids = jnp.where(seq_place == 0, -1.0, prev_ids)
    next_id = jnp.where(seq_place == seq_devices - 1, -1.0, shifted(ids[:1], "seq", -1))
    ext = jnp.concatenate([prev_ids, ids])
    same = [(ext[halo - k : halo - k + tokens] == ids).astype(F32) for k in range(taps)]
    masks = jnp.stack(same + [jnp.zeros_like(ids)] * (8 - taps), axis=1)

    slope = -DECAY_SCALE * jax.nn.softplus(-decay_param)
    params = jnp.concatenate(
        [jnp.stack([conv_bias]), conv_weight, jnp.stack([recur_bias, input_bias, slope])], axis=0
    )
    gates = jnp.concatenate([block_diagonal(recur_gate), block_diagonal(input_gate)], axis=1)

    full = lax.all_gather(hidden_in, "tp", axis=1, tiled=True)
    x = full.astype(F32)
    r1 = lax.rsqrt(jnp.mean(x * x, axis=1, keepdims=True) + EPSILON)
    n1 = (x * r1 * first_gain).astype(BF16)
    bx = dot(n1, input_weight)
    by = dot(n1, gelu_weight)
    prev_rows = jnp.pad(shifted(bx[tokens - halo :], "seq", 1), ((8 - halo, 0), (0, 0)))
    conv, low, r, i, local, reach = forward_recurrence(bx, prev_rows, masks, params, gates)
    ends = lax.all_gather(
        jnp.stack([reach[tokens - 1], local[tokens - 1]]), "seq", axis=0
    )
    incoming = chained(ends[:, 0], ends[:, 1], seq_place, False)
    state = local + reach * incoming
    mixed = (gelu(by) * state).astype(BF16)
    branch = dot(mixed, output_weight).astype(BF16)
    x_share = hidden_in.astype(F32)
    resid = x_share + lax.psum_scatter(branch, "tp", scatter_dimension=1, tiled=True).astype(F32)

    resid_full = lax.all_gather(resid.astype(BF16), "tp", axis=1, tiled=True).astype(F32)
    r2 = lax.rsqrt(jnp.mean(resid_full * resid_full, axis=1, keepdims=True) + EPSILON)
    n2 = (resid_full * r2 * second_gain).astype(BF16)
    gate = dot(n2, gate_full)
    up = dot(n2, up_full)
    d_hid = contract_last(grad_out, down_full)
    act, act_slope = gelu_parts(gate)
    hid = (act * up).astype(BF16)
    d_gate_f = act_slope * up * d_hid
    d_up_f = act * d_hid
    d_gate = d_gate_f.astype(BF16)
    d_up = d_up_f.astype(BF16)
    mlp = dot(hid, down_full).astype(BF16)
    d_n2_part = (contract_last(d_gate, gate_full) + contract_last(d_up, up_full)).astype(BF16)
    pull2 = lax.psum(
        jnp.sum(d_gate.astype(F32) * gate + d_up.astype(F32) * up, axis=1), "tp"
    )[:, None]
    d_n2 = lax.psum_scatter(d_n2_part, "tp", scatter_dimension=1, tiled=True).astype(F32)
    grad_second = jnp.sum(d_n2 * resid * r2, axis=0)
    gain_share = lax.dynamic_slice_in_dim(second_gain, share_start, share)
    scaled = d_n2 * gain_share * r2
    centre = r2 * r2 * pull2 * (1.0 / width)
    g_share = lax.dynamic_slice_in_dim(grad_out, share_start, share, 1).astype(F32)
    d_resid_share = g_share + scaled - resid * centre
    scaled_full = lax.all_gather(scaled.astype(BF16), "tp", axis=1, tiled=True).astype(F32)
    d_resid_low = (grad_out.astype(F32) + scaled_full - resid_full * centre).astype(BF16)
    block_out = (
        resid + lax.psum_scatter(mlp, "tp", scatter_dimension=1, tiled=True).astype(F32)
    ).astype(BF16)

    grad_gate_weight = lax.psum_scatter(
        contract_first(n2, d_gate).astype(BF16), "seq", scatter_dimension=0, tiled=True
    ).astype(F32)
    grad_up_weight = lax.psum_scatter(
        contract_first(n2, d_up).astype(BF16), "seq", scatter_dimension=0, tiled=True
    ).astype(F32)
    grad_down_weight = lax.psum_scatter(
        contract_first(hid, grad_out).astype(BF16), "seq", scatter_dimension=1, tiled=True
    ).astype(F32)

    dm = contract_last(d_resid_low, output_weight)
    grad_output_weight = lax.psum(contract_first(mixed, d_resid_low).astype(BF16), "seq").astype(F32)
    grad_local, reach_back, dby, heads = reverse_recurrence(dm, by, r, state, masks, params)
    outgoing = lax.all_gather(jnp.stack([heads[8], heads[0]]), "seq", axis=0)
    message = chained(outgoing[:, 0], outgoing[:, 1], seq_place, True)
    border = jnp.pad(jnp.stack([incoming, message]), ((0, 6), (0, 0)))
    dbx_main, tail, edge, sums, gate_grads = gate_gradients(
        grad_local, reach_back, r, i, conv, state, bx, masks, low, prev_rows, border, params, gates
    )
    tail = (tail + shifted(edge, "seq", -1)).astype(BF16)
    dbx = lax.dynamic_update_slice_in_dim(dbx_main, tail, tokens - 8, 0)
    d_n1_part = (contract_last(dbx, input_weight) + contract_last(dby, gelu_weight)).astype(BF16)
    pull1 = lax.psum(
        jnp.sum(dbx.astype(F32) * bx + dby.astype(F32) * by, axis=1), "tp"
    )[:, None]
    grad_gelu_weight = lax.psum(contract_first(dby, n1).astype(BF16), "seq").astype(F32).T
    grad_input_weight = lax.psum(contract_first(dbx, n1).astype(BF16), "seq").astype(F32).T
    d_n1 = lax.psum_scatter(d_n1_part, "tp", scatter_dimension=1, tiled=True).astype(F32)
    grad_first = jnp.sum(d_n1 * x_share * r1, axis=0)
    gain1_share = lax.dynamic_slice_in_dim(first_gain, share_start, share)
    grad_in = (
        d_resid_share + d_n1 * gain1_share * r1 - x_share * (r1 * r1 * pull1 * (1.0 / width))
    ).astype(BF16)

    sums = jnp.sum(sums.reshape(8, 8, channels), axis=1)
    corner = lambda n: jnp.stack(
        [
            gate_grads[b * size : (b + 1) * size, n * channels + b * size : n * channels + (b + 1) * size]
            for b in range(blocks)
        ]
    )
    next_ids = jnp.concatenate([ids[1:], next_id])
    closing = (next_ids != ids).astype(F32)[None, :]
    member = (segment_ids[None, :] == jnp.arange(SEGS, dtype=jnp.int32)[:, None]).astype(F32)
    finals = jnp.dot(
        member * closing, state, precision=lax.Precision.HIGHEST, preferred_element_type=F32
    )
    small = lax.psum(jnp.concatenate([sums, finals], axis=0), "seq")
    recur_grads, input_grads = lax.psum((corner(0), corner(1)), "seq")
    gains = jnp.zeros((2, width), F32)
    gains = lax.dynamic_update_slice(
        gains, jnp.stack([grad_first, grad_second]), (0, share_start)
    )
    gains = lax.psum(gains, ("seq", "tp"))
    grad_decay = small[2] * (DECAY_SCALE * jax.nn.sigmoid(-decay_param))
    return (
        block_out,
        grad_in,
        gains[0],
        grad_input_weight,
        grad_gelu_weight,
        small[4:8],
        small[3],
        recur_grads,
        input_grads,
        small[0],
        small[1],
        grad_decay,
        grad_output_weight,
        gains[1],
        grad_gate_weight,
        grad_up_weight,
        grad_down_weight,
        small[8:],
    )


def solution(mesh):
    row = P("tp")
    return jax.shard_map(
        on_device,
        mesh=mesh,
        in_specs=(
            P("seq", "tp"), P("seq"), P(), P(None, "tp"), P(None, "tp"), P(None, "tp"), row,
            P("tp", None, None), P("tp", None, None), row, row, row, P("tp", None), P(),
            P("seq", "tp"), P("seq", "tp"), P("tp", "seq"), P("seq", None),
        ),
        out_specs=(
            P("seq", "tp"), P("seq", "tp"), P(), P(None, "tp"), P(None, "tp"), P(None, "tp"), row,
            P("tp", None, None), P("tp", None, None), row, row, row, P("tp", None), P(),
            P("seq", "tp"), P("seq", "tp"), P("tp", "seq"), P(None, "tp"),
        ),
        check_vma=False,
    )
```

time: 4510 us -> 1130 us (0.25)
  local copies, waits for them, and re-layouts: 2710 us -> 23.6 us
  waiting for transfers between devices: 1060 us -> 637 us
  other arithmetic: 323 us -> 63.1 us
  matrix products: 302 us -> 165 us
  Pallas kernels: 0 us -> 94.7 us
  blocking collectives: 61.7 us -> 110 us
    slice x127 -> x11, local copies, waits for them, and re-layouts: 1550 us -> 4.63 us  [the longest x1 0.77 us: on_device(): local[tokens - 1]]
    pad x72 -> x1, local copies, waits for them, and re-layouts: 1010 us -> 0.01 us  [on_device(): jnp.pad(shifted(bx[tokens - halo:], 'seq', 1), ((8 - halo, 0), (0, 0)))]
    psum x4 -> x2, waiting for transfers between devices: 795 us -> 92.1 us  [the longest x1 75.3 us: on_device(): lax.psum(contract_first(dbx, n1).astype(BF16), 'seq').astype(F32)]
    all_gather x4 -> x6, waiting for transfers between devices: 73.9 us -> 244 us  [the longest x1 67.9 us: on_device(): lax.all_gather(resid.astype(BF16), 'tp', axis=1, tiled=True).astype(F32)]
    add x87 -> x0, other arithmetic: 157 us -> none  [the longest x45 70.7 us: compose(): return (earlier[0] * later[0], later[0] * earlier[1] + later[1])]
    dot_general x32 -> x7, matrix products: 195 us -> 64.5 us  [the longest x6 61 us: dot(): return jnp.dot(left, right, preferred_element_type=F32)]
    reduce_scatter x2 -> x7, waiting for transfers between devices: 189 us -> 297 us  [the longest x1 79.6 us: on_device(): lax.psum_scatter(d_n1_part, 'tp', scatter_dimension=1, tiled=True)]
    pallas_call x0 -> x3, Pallas kernels: none -> 94.7 us  [the longest x1 46.4 us: gate_gradients(): pl.pallas_call(gate_grad_kernel, name='gate_gradients', grid=(tiles,), in...]
  transfers between devices with their start and end apart: 14 -> 19, of which waited for: 7 -> 12; matrix products, arithmetic and copies ran while one was open for 41% -> 15% of each run, Pallas kernels for 0% -> 5%
where the time goes in v1:
time: 1130 us; the launch traced here: 1120 us
  waiting for transfers between devices  637 us (56%)
  matrix products  165 us (15%)
  blocking collectives  110 us (10%)
  Pallas kernels  94.7 us (8%)
  other arithmetic  63.1 us (6%)
  local copies, waits for them, and re-layouts  23.6 us (2%)
  between operations  17.2 us (2%)
    reduce_scatter x1, waiting for transfers between devices, on_device(): lax.psum_scatter(d_n1_part, 'tp', scatter_dimension=1, tiled=True)  79.6 us
    reduce_scatter x1, waiting for transfers between devices, on_device(): lax.psum_scatter(d_n2_part, 'tp', scatter_dimension=1, tiled=True)  76.8 us
    psum x1, waiting for transfers between devices, on_device(): lax.psum(contract_first(dbx, n1).astype(BF16), 'seq').astype(F32)  75.3 us
    reduce_scatter x1, waiting for transfers between devices, on_device(): lax.psum_scatter(branch, 'tp', scatter_dimension=1, tiled=True).astype(F32)  73.9 us
    all_gather x1, waiting for transfers between devices, on_device(): lax.all_gather(resid.astype(BF16), 'tp', axis=1, tiled=True).astype(F32)  67.9 us
    reduce_scatter x1, waiting for transfers between devices, on_device(): lax.psum_scatter(mlp, 'tp', scatter_dimension=1, tiled=True).astype(F32)  66.9 us
    all_gather x1, waiting for transfers between devices, on_device(): full = lax.all_gather(hidden_in, 'tp', axis=1, tiled=True)  64 us
    dot_general x6, matrix products, dot(): return jnp.dot(left, right, preferred_element_type=F32)  61 us
  transfers between devices with their start and end apart: 19, of which 12 were waited for; matrix products, arithmetic and copies ran while one was open for 15% of the time, Pallas kernels for 5%

profile of v1, /device:TPU:0, one launch (start us, length us, event | category | flops | bytes accessed | tf_op | source)
XLA Modules:
  0.0 1118.1 jit_solution(13547724549006734481)
XLA Ops:
  18.7 10.0 fusion.56.gates_ref
  30.0 64.0 %all-gather.11.cloned.1.call-done = bf16[1024,2048]{1,0:T(8,128)(2,1)} async-done(((bf16[1024,512]{1,0:T(8,128)(2,1)}), bf16[1024,2048]{1,0:T(8,128)(2,1)}) %all-gather.11.cloned.1.call-update) | async-done | bytes 4194320 | tf_op jit(solution)/shard_map/all_gather | solution.py:456
  94.0 3.2 fusion
  97.8 5.3 fusion.112.bx_ref.bx_before_ref
  108.9 35.8 %forward_recurrence.1 = (f32[1024,704]{1,0:T(8,128)}, bf16[1024,704]{1,0:T(8,128)(2,1)S(1)}, f32[1024,704]{1,0:T(8,128)}, f32[1024,704]{1,0:T(8,128)}, f32[1024,704]{1,0:T(8,128)}, /*index=5*/f32[1024,704]{1,0:T(8,128)}) custom-call(f32[1024,704]{1,0:T(8,128)} %copy-done.13, f32[8,704]{1,0:T(8,128)S(1)} %pad.36.prev_ref, f32[1024,8]{1,0:T(8,128)S(1)} %copy.70.mask_ref, ...), custom_call_target="tpu_custom_call" | custom-call | flops 2030043136 | bytes 21626880 | tf_op jit(solution)/shard_map/forward_recurrence/pallas_call | solution.py:139
  146.2 12.4 %all-gather.2 = f32[8,2,704]{2,1,0:T(2,128)S(1)} all-gather(f32[1,2,704]{2,1,0:T(2,128)S(1)} %maximum_bitcast_fusion), channel_id=2, replica_groups=mesh['seq'=8,'tp'=4] {'seq'}, dimensions={0}, use_global_device_ids=true | all-gather | bytes 50688 | tf_op jit(solution)/shard_map/all_gather | solution.py:464
  158.9 8.4 fusion.38
  168.4 4.9 convolution_convert_fusion.4
  174.0 73.9 %reduce-scatter.8.cloned.1.call-done = bf16[1024,512]{1,0:T(8,128)(2,1)} async-done(((bf16[1024,2048]{1,0:T(8,128)(2,1)}), bf16[1024,512]{1,0:T(8,128)(2,1)}) %reduce-scatter.8.cloned.1.call-update) | async-done | bytes 1048592 | tf_op jit(solution)/shard_map/reduce_scatter | solution.py:472
  252.3 11.7 %fusion.118 = f32[1024,1536]{1,0:T(8,128)} fusion(bf16[1024,2048]{1,0:T(8,128)(2,1)} %param.35, bf16[1536,2048]{1,0:T(8,128)(2,1)} %all-gather.19.cloned.1.call-done), kind=kOutput, calls=%fused_computation.241 | convolution fusion | flops 6442450944 | bytes 16777216 | tf_op jit(solution)/shard_map/dot_general | solution.py:35
  264.0 67.9 %all-gather.13.cloned.1.call-done = bf16[1024,2048]{1,0:T(8,128)(2,1)} async-done(((bf16[1024,512]{1,0:T(8,128)(2,1)}), bf16[1024,2048]{1,0:T(8,128)(2,1)}) %all-gather.13.cloned.1.call-update) | async-done | bytes 4194320 | tf_op jit(solution)/shard_map/all_gather | solution.py:474
  331.9 3.1 fusion.3
  335.0 42.7 %all-gather.15.cloned.1.call-done = bf16[2048,1536]{1,0:T(8,128)(2,1)} async-done(((bf16[256,1536]{1,0:T(8,128)(2,1)}), bf16[2048,1536]{1,0:T(8,128)(2,1)}) %all-gather.15.cloned.1.call-update) | async-done | bytes 6291472 | tf_op jit(solution)/shard_map/all_gather | solution.py:438
  377.7 12.2 %fusion.108 = f32[1024,1536]{1,0:T(8,128)} fusion(bf16[2048,1536]{1,0:T(8,128)(2,1)} %all-gather.15.cloned.1.call-done, bf16[1024,2048]{1,0:T(8,128)(2,1)} %all-gather.13.cloned.1.call-done, f32[2048]{0:T(1024)S(1)} %copy-done.27, f32[1024]{0:T(1024)S(1)} %add_rsqrt_fusion), kind=kOutput, calls=%fused_computation.236 | convolution fusion | flops 6450839552 | bytes 16789504 | tf_op jit(solution)/shard_map/dot_general | solution.py:27
  390.0 35.2 %all-gather.17.cloned.1.call-done = bf16[2048,1536]{1,0:T(8,128)(2,1)} async-done(((bf16[256,1536]{1,0:T(8,128)(2,1)}), bf16[2048,1536]{1,0:T(8,128)(2,1)}) %all-gather.17.cloned.1.call-update) | async-done | bytes 6291472 | tf_op jit(solution)/shard_map/all_gather | solution.py:439
  425.2 19.0 %add_reduce_fusion = (f32[1024]{0:T(1024)S(1)}, bf16[1024,1536]{1,0:T(8,128)(2,1)}, bf16[1024,1536]{1,0:T(8,128)(2,1)}, bf16[1024,1536]{1,0:T(8,128)(2,1)}) fusion(f32[1024,1536]{1,0:T(8,128)} %fusion.108, f32[1024,1536]{1,0:T(8,128)} %fusion.118, bf16[2048,1536]{1,0:T(8,128)(2,1)} %all-gather.17.cloned.1.call-done, ...), kind=kOutput, calls=%fused_computation.18 | convolution fusion | flops 6498024448 | bytes 32522240 | tf_op jit(solution)/shard_map/dot_general | solution.py:27
  444.2 10.9 fusion.119
  455.2 10.5 add_convert_fusion.1
  465.8 76.8 %reduce-scatter.12.cloned.1.call-done = bf16[1024,512]{1,0:T(8,128)(2,1)} async-done(((bf16[1024,2048]{1,0:T(8,128)(2,1)}), bf16[1024,512]{1,0:T(8,128)(2,1)}) %reduce-scatter.12.cloned.1.call-update) | async-done | bytes 1048592 | tf_op jit(solution)/shard_map/reduce_scatter | solution.py:491
  545.2 11.2 %convolution_convert_fusion = bf16[1536,2048]{1,0:T(8,128)(2,1)} fusion(bf16[1024,1536]{1,0:T(8,128)(2,1)} %get-tuple-element.77, bf16[1024,2048]{1,0:T(8,128)(2,1)} %param.35), kind=kOutput, calls=%fused_computation.15 | convolution fusion | flops 6445596672 | bytes 13631488 | tf_op jit(solution)/shard_map/dot_general | solution.py:31
  556.5 11.6 %convolution_convert_fusion.1 = bf16[2048,1536]{1,0:T(8,128)(2,1)} fusion(bf16[1024,1536]{1,0:T(8,128)(2,1)} %get-tuple-element.73, bf16[1024,2048]{1,0:T(8,128)(2,1)} %all-gather.13.cloned.1.call-done, f32[2048]{0:T(1024)S(1)} %copy-done.27, f32[1024]{0:T(1024)S(1)} %add_rsqrt_fusion), kind=kOutput, calls=%fused_computation.16 | convolution fusion | flops 6453985280 | bytes 13643776 | tf_op jit(solution)/shard_map/dot_general | solution.py:31
  568.1 12.5 %convolution_convert_fusion.2 = bf16[2048,1536]{1,0:T(8,128)(2,1)} fusion(bf16[1024,1536]{1,0:T(8,128)(2,1)} %get-tuple-element.74, bf16[1024,2048]{1,0:T(8,128)(2,1)} %all-gather.13.cloned.1.call-done, f32[2048]{0:T(1024)S(1)} %copy-done.27, f32[1024]{0:T(1024)S(1)} %add_rsqrt_fusion), kind=kOutput, calls=%fused_computation.17 | convolution fusion | flops 6453985280 | bytes 13643776 | tf_op jit(solution)/shard_map/dot_general | solution.py:31
  580.8 11.6 %psum.63 = f32[1024]{0:T(1024)S(1)} all-reduce(f32[1024]{0:T(1024)S(1)} %get-tuple-element.72), channel_id=1, replica_groups=mesh['seq'=8,'tp'=4] {'tp'}, use_global_device_ids=true, to_apply=%region_6.7 | all-reduce | flops 1024 | bytes 8192 | tf_op jit(solution)/shard_map/psum | solution.py:488
  592.4 34.4 %all-gather.21.cloned.1.call-done = bf16[1024,2048]{1,0:T(8,128)(2,1)} async-done(((bf16[1024,512]{1,0:T(8,128)(2,1)}), bf16[1024,2048]{1,0:T(8,128)(2,1)}) %all-gather.21.cloned.1.call-update) | async-done | bytes 4194320 | tf_op jit(solution)/shard_map/all_gather | solution.py:498
  626.8 7.8 fusion.7
  634.6 5.1 fusion.120.dm_ref
  639.8 12.5 %reverse_recurrence.1 = (f32[1024,704]{1,0:T(8,128)S(1)}, f32[1024,704]{1,0:T(8,128)}, bf16[1024,704]{1,0:T(8,128)(2,1)S(1)}, f32[16,704]{1,0:T(8,128)S(1)}) custom-call(f32[1024,704]{1,0:T(8,128)} %fusion.120.dm_ref, f32[1024,704]{1,0:T(8,128)} %get-tuple-element.105.by_ref, f32[1024,704]{1,0:T(8,128)} %get-tuple-element.35.r_ref, ...), custom_call_target="tpu_custom_call" | custom-call | flops 43253760 | bytes 20185088 | tf_op jit(solution)/shard_map/reverse_recurrence/pallas_call | solution.py:214
  654.1 9.5 all-gather.3
  663.7 46.4 %gate_gradients.1 = (bf16[1024,704]{1,0:T(8,128)(2,1)S(1)}, f32[8,704]{1,0:T(8,128)S(1)}, f32[8,704]{1,0:T(8,128)S(1)}, f32[64,704]{1,0:T(8,128)S(1)}, f32[704,1408]{1,0:T(8,128)}) custom-call(f32[1024,704]{1,0:T(8,128)} %copy-done.3, f32[1024,704]{1,0:T(8,128)} %get-tuple-element.37.reach_ref, f32[1024,704]{1,0:T(8,128)} %get-tuple-element.35.r_ref, ...), custom_call_target="tpu_custom_call" | custom-call | flops 4060086272 | bytes 23068672 | tf_op jit(solution)/shard_map/gate_gradients/pallas_call | solution.py:369
  711.6 7.6 fusion.40
  719.1 4.7 convolution_convert_fusion.5
  725.0 4.8 fusion.39
  729.9 11.2 %convolution_convert_fusion.3 = bf16[1024,2048]{1,0:T(8,128)(2,1)} fusion(bf16[1024,1536]{1,0:T(8,128)(2,1)} %get-tuple-element.77, bf16[1536,2048]{1,0:T(8,128)(2,1)} %all-gather.19.cloned.1.call-done), kind=kOutput, calls=%fused_computation.56 | convolution fusion | flops 6444548096 | bytes 13631488 | tf_op jit(solution)/shard_map/dot_general | solution.py:27
  741.5 5.0 fusion.121
  746.5 5.0 add_convert_fusion
  752.2 3.5 fusion.65
  763.1 27.2 %psum.68 = f32[16,704]{1,0:T(8,128)S(1)} all-reduce(f32[16,704]{1,0:T(8,128)S(1)} %pad_maximum_fusion.2), channel_id=1, replica_groups=mesh['seq'=8,'tp'=4] {'seq'}, use_global_device_ids=true, to_apply=%region_16.17 | all-reduce | flops 11264 | bytes 90112 | tf_op jit(solution)/shard_map/psum | solution.py:551
  796.5 4.6 add_reduce_fusion.1
  801.1 8.4 psum.64
  809.5 75.3 %all-reduce.17.cloned.1.call-done = (bf16[2048,704]{0,1:T(8,128)(2,1)}, bf16[2048,704]{0,1:T(8,128)(2,1)}, bf16[704,2048]{1,0:T(8,128)(2,1)}) async-done(((bf16[2048,704]{0,1:T(8,128)(2,1)}, bf16[2048,704]{0,1:T(8,128)(2,1)}, bf16[704,2048]{1,0:T(8,128)(2,1)}), (bf16[2048,704]{0,1:T(8,128)(2,1)}, bf16[2048,704]{0,1:T(8,128)(2,1)}, bf16[704,2048]{1,0:T(8,128)(2,1)})) %all-reduce.17.cloned.1.call-update) | async-done | bytes 8650768 | tf_op jit(solution)/shard_map/psum | solution.py:530
  884.8 5.3 transpose.25
  890.1 3.5 transpose.27
  893.6 3.3 convert_element_type.184
  896.9 66.9 %reduce-scatter.10.cloned.1.call-done = bf16[1024,512]{1,0:T(8,128)(2,1)} async-done(((bf16[1024,2048]{1,0:T(8,128)(2,1)}), bf16[1024,512]{1,0:T(8,128)(2,1)}) %reduce-scatter.10.cloned.1.call-update) | async-done | bytes 1048592 | tf_op jit(solution)/shard_map/reduce_scatter | solution.py:501
  963.9 79.6 %reduce-scatter.14.cloned.1.call-done = bf16[1024,512]{1,0:T(8,128)(2,1)} async-done(((bf16[1024,2048]{1,0:T(8,128)(2,1)}), bf16[1024,512]{1,0:T(8,128)(2,1)}) %reduce-scatter.14.cloned.1.call-update) | async-done | bytes 1048592 | tf_op jit(solution)/shard_map/reduce_scatter | solution.py:531
  1043.5 4.7 fusion.52
  1048.2 40.7 %psum.65 = f32[2,2048]{1,0:T(2,128)S(1)} all-reduce(f32[2,2048]{1,0:T(2,128)S(1)} %maximum_dynamic-update-slice_fusion), channel_id=1, replica_groups=mesh['seq'=8,'tp'=4] {'seq','tp'}, use_global_device_ids=true, to_apply=%region_12.13 | all-reduce | flops 4096 | bytes 32768 | tf_op jit(solution)/shard_map/psum | solution.py:557
  1089.6 16.7 %all-reduce.15.cloned.1.call-done = (f32[4,176,176]{2,1,0:T(8,128)}, f32[4,176,176]{2,1,0:T(8,128)}) async-done(((f32[4,176,176]{2,1,0:T(8,128)}, f32[4,176,176]{2,1,0:T(8,128)}), (f32[4,176,176]{2,1,0:T(8,128)}, f32[4,176,176]{2,1,0:T(8,128)})) %all-reduce.15.cloned.1.call-update) | async-done | bytes 991248 | tf_op jit(solution)/shard_map/psum | solution.py:552
  (173 shorter events, 52.3 us)
Async XLA Ops:
  8.0 150.8 %copy-start = (bf16[2048,704]{0,1:T(8,128)(2,1)S(1)}, bf16[2048,704]{0,1:T(8,128)(2,1)}, u32[]{:S(2)}) copy-start(bf16[2048,704]{0,1:T(8,128)(2,1)} %param.22) | copy-start | bytes 8650756
  8.0 21.2 %copy-start.21 = (s32[1024]{0:T(1024)S(1)}, s32[1024]{0:T(1024)}, u32[]{:S(2)}) copy-start(s32[1024]{0:T(1024)} %param.19) | copy-start | bytes 12292
  8.0 85.9 %all-gather.11.cloned.1.call-start = ((), (), s32[]{:S(2)}) async-start(), calls=%async_computation.7 | async-start | bytes 5242880 | tf_op jit(solution)/shard_map/all_gather | solution.py:456
  8.8 239.1 %reduce-scatter.8.cloned.1.call-start = ((), (), s32[]{:S(2)}) async-start(), calls=%async_computation.8 | async-start | bytes 5242880 | tf_op jit(solution)/shard_map/reduce_scatter | solution.py:472
  9.7 20.3 %collective-permute-start.1 = (f32[3]{0:T(128)S(1)}, f32[3]{0:T(128)S(1)}, u32[]{:S(2)}, u32[]{:S(2)}) collective-permute-start(f32[3]{0:T(128)S(1)} %slice.250), channel_id=1, source_target_pairs={{0,4},{4,8},{8,12},{12,16},{16,20},{20,24},{24,28},{1,5},{5,9},{9,... | collective-permute-start | bytes 44 | tf_op jit(solution)/shard_map/ppermute | solution.py:23
  12.5 16.1 %collective-permute-start.3 = (f32[1]{0:T(128)}, f32[1]{0:T(128)}, u32[]{:S(2)}, u32[]{:S(2)}) collective-permute-start(f32[1]{0:T(128)} %slice.296), channel_id=1, source_target_pairs={{4,0},{8,4},{12,8},{16,12},{20,16},{24,20},{28,24},{5,1},{9,5},{13... | collective-permute-start | bytes 20 | tf_op jit(solution)/shard_map/ppermute | solution.py:23
  17.4 80.3 %copy-start.28 = (f32[2048]{0:T(1024)S(1)}, f32[2048]{0:T(1024)}, u32[]{:S(2)}) copy-start(f32[2048]{0:T(1024)} %param.20) | copy-start | bytes 24580
  94.0 3.8 copy-start.14
  97.8 61.0 %copy-start.23 = (f32[1024]{0:T(1024)}, f32[1024]{0:T(1024)S(1)}, u32[]{:S(2)}) copy-start(f32[1024]{0:T(1024)S(1)} %add_rsqrt_fusion.1) | copy-start | bytes 12292
  104.8 2.6 collective-permute-start
  108.9 35.8 %copy-start.11 = (f32[8,704]{1,0:T(8,128)}, f32[8,704]{1,0:T(8,128)S(1)}, u32[]{:S(2)}) copy-start(f32[8,704]{1,0:T(8,128)S(1)} %pad.36.prev_ref) | copy-start | bytes 67588
  108.9 49.9 %copy-start.15 = (bf16[1024,2048]{1,0:T(8,128)(2,1)S(1)}, bf16[1024,2048]{1,0:T(8,128)(2,1)}, u32[]{:S(2)}) copy-start(bf16[1024,2048]{1,0:T(8,128)(2,1)} %all-gather.11.cloned.1.call-done) | copy-start | bytes 12582916
  144.7 22.5 %copy-start.4 = (bf16[1024,704]{1,0:T(8,128)(2,1)}, bf16[1024,704]{1,0:T(8,128)(2,1)S(1)}, u32[]{:S(2)}) copy-start(bf16[1024,704]{1,0:T(8,128)(2,1)S(1)} %get-tuple-element.40.low_ref) | copy-start | bytes 4325380
  158.8 9.5 copy-start.32
  173.3 79.0 %all-gather.19.cloned.1.call-start = ((), (), s32[]{:S(2)}) async-start(), calls=%async_computation.12 | async-start | bytes 7077888 | tf_op jit(solution)/shard_map/all_gather | solution.py:440
  173.9 158.0 %all-gather.13.cloned.1.call-start = ((), (), s32[]{:S(2)}) async-start(), calls=%async_computation.9 | async-start | bytes 5242880 | tf_op jit(solution)/shard_map/all_gather | solution.py:474
  250.7 127.1 %all-gather.15.cloned.1.call-start = ((), (), s32[]{:S(2)}) async-start(), calls=%async_computation.10 | async-start | bytes 7077888 | tf_op jit(solution)/shard_map/all_gather | solution.py:438
  251.3 173.9 %all-gather.17.cloned.1.call-start = ((), (), s32[]{:S(2)}) async-start(), calls=%async_computation.11 | async-start | bytes 7077888 | tf_op jit(solution)/shard_map/all_gather | solution.py:439
  252.0 290.6 %reduce-scatter.12.cloned.1.call-start = ((), (), s32[]{:S(2)}) async-start(), calls=%async_computation.14 | async-start | bytes 5242880 | tf_op jit(solution)/shard_map/reduce_scatter | solution.py:491
  264.0 113.7 %copy-start.27 = (f32[2048]{0:T(1024)S(1)}, f32[2048]{0:T(1024)}, u32[]{:S(2)}) copy-start(f32[2048]{0:T(1024)} %param.31) | copy-start | bytes 24580
  425.2 19.0 %copy-start.30 = (bf16[2048,1536]{1,0:T(8,128)(2,1)S(1)}, bf16[2048,1536]{1,0:T(8,128)(2,1)}, u32[]{:S(2)}) copy-start(bf16[2048,1536]{1,0:T(8,128)(2,1)} %all-gather.15.cloned.1.call-done) | copy-start | bytes 18874372
  444.2 10.9 copy-start.31
  444.2 10.9 copy-start.37
  465.7 161.1 %all-gather.21.cloned.1.call-start = ((), (), s32[]{:S(2)}) async-start(), calls=%async_computation.15 | async-start | bytes 5242880 | tf_op jit(solution)/shard_map/all_gather | solution.py:498
  545.1 210.6 %reduce-scatter.20.cloned.1.call-start = ((), (), s32[]{:S(2)}) async-start(), calls=%async_computation.19 | async-start | bytes 7077888 | tf_op jit(solution)/shard_map/reduce_scatter | solution.py:510
  556.4 201.7 %reduce-scatter.18.cloned.1.call-start = ((), (), s32[]{:S(2)}) async-start(), calls=%async_computation.18 | async-start | bytes 7077888 | tf_op jit(solution)/shard_map/reduce_scatter | solution.py:507
  568.1 192.5 %reduce-scatter.16.cloned.1.call-start = ((), (), s32[]{:S(2)}) async-start(), calls=%async_computation.17 | async-start | bytes 7077888 | tf_op jit(solution)/shard_map/reduce_scatter | solution.py:504
  580.7 304.2 %all-reduce.17.cloned.1.call-start = ((), (), s32[]{:S(2)}) async-start(), calls=%async_computation.21 | async-start | bytes 17301504 | tf_op jit(solution)/shard_map/psum | solution.py:530
  626.8 7.8 copy-start.33
  639.7 23.9 %copy-start.2 = (bf16[704,1408]{1,0:T(8,128)(2,1)S(1)}, bf16[704,1408]{1,0:T(8,128)(2,1)}, u32[]{:S(2)}) copy-start(bf16[704,1408]{1,0:T(8,128)(2,1)} %fusion.56.gates_ref) | copy-start | bytes 5947396
  639.7 23.9 %copy-start.5 = (bf16[1024,704]{1,0:T(8,128)(2,1)S(1)}, bf16[1024,704]{1,0:T(8,128)(2,1)}, u32[]{:S(2)}) copy-start(bf16[1024,704]{1,0:T(8,128)(2,1)} %copy-done.4) | copy-start | bytes 4325380
  639.8 23.9 %copy-start.12 = (f32[8,704]{1,0:T(8,128)S(1)}, f32[8,704]{1,0:T(8,128)}, u32[]{:S(2)}) copy-start(f32[8,704]{1,0:T(8,128)} %copy-done.11) | copy-start | bytes 67588
  654.0 57.5 %copy-start.6 = (bf16[1024,704]{1,0:T(8,128)(2,1)}, bf16[1024,704]{1,0:T(8,128)(2,1)S(1)}, u32[]{:S(2)}) copy-start(bf16[1024,704]{1,0:T(8,128)(2,1)S(1)} %get-tuple-element.45) | copy-start | bytes 4325380
  663.6 47.9 %copy-start.24 = (f32[1024]{0:T(1024)S(1)}, f32[1024]{0:T(1024)}, u32[]{:S(2)}) copy-start(f32[1024]{0:T(1024)} %copy-done.23) | copy-start | bytes 12292
  663.6 47.9 %copy-start.29 = (f32[2048]{0:T(1024)S(1)}, f32[2048]{0:T(1024)}, u32[]{:S(2)}) copy-start(f32[2048]{0:T(1024)} %param.20) | copy-start | bytes 24580
  710.0 9.1 copy-start.9
  710.0 13.8 %collective-permute-start.2 = (f32[8,704]{1,0:T(8,128)S(1)}, f32[8,704]{1,0:T(8,128)S(1)}, u32[]{:S(2)}, u32[]{:S(2)}) collective-permute-start(f32[8,704]{1,0:T(8,128)S(1)} %get-tuple-element.44), channel_id=1, source_target_pairs={{4,0},{8,4},{12,8},{16,12},{20,16},{24,20},{28,24},{5,1},{9,5},{13... | collective-permute-start | bytes 67592 | tf_op jit(solution)/shard_map/ppermute | solution.py:23
  711.6 7.6 copy-start.36
  719.1 5.9 copy-start.16
  729.9 234.0 %reduce-scatter.10.cloned.1.call-start = ((), (), s32[]{:S(2)}) async-start(), calls=%async_computation.13 | async-start | bytes 5242880 | tf_op jit(solution)/shard_map/reduce_scatter | solution.py:501
  741.1 302.4 %reduce-scatter.14.cloned.1.call-start = ((), (), s32[]{:S(2)}) async-start(), calls=%async_computation.16 | async-start | bytes 5242880 | tf_op jit(solution)/shard_map/reduce_scatter | solution.py:531
  741.5 5.0 copy-start.8
  741.5 5.0 copy-start.34
  751.5 354.8 %all-reduce.15.cloned.1.call-start = ((), (), s32[]{:S(2)}) async-start(), calls=%async_computation.20 | async-start | bytes 2883584 | tf_op jit(solution)/shard_map/psum | solution.py:552
  755.7 7.4 copy-start.10
  760.6 35.3 %copy-start.26 = (f32[704]{0:T(1024)S(1)}, f32[704]{0:T(1024)}, u32[]{:S(2)}) copy-start(f32[704]{0:T(1024)} %param.29) | copy-start | bytes 8452
  796.5 13.0 %copy-start.20 = (f32[1024]{0:T(1024)S(1)}, f32[1024]{0:T(1024)}, u32[]{:S(2)}) copy-start(f32[1024]{0:T(1024)} %copy-done.19) | copy-start | bytes 12292
  884.8 5.3 copy-start.18
  (9 other events, 12.8 us)
Sparse Core Ops, SparseCore 0:
  10.5 83.4 all-gather.10
  173.4 74.3 reduce-scatter.7
  465.8 76.7 reduce-scatter.11
  545.2 81.5 all-gather.20
Sparse Core Ops, SparseCore 1:
  175.7 44.1 all-gather.18
  250.8 81.1 all-gather.12
  333.8 43.8 all-gather.14
  379.8 45.3 all-gather.16
  556.5 62.0 reduce-scatter.19
  622.0 61.7 reduce-scatter.17
  687.4 61.6 reduce-scatter.15
  754.1 130.7 all-reduce.16
  887.0 76.8 reduce-scatter.9
  966.3 77.2 reduce-scatter.13
  1047.8 58.5 all-reduce.14

commit v2 on v1

v2 whole, which is shorter than its diff:
```python
import jax
import jax.numpy as jnp
from jax import lax
from jax.experimental import pallas as pl
from jax.experimental.layout import Layout, with_layout_constraint
from jax.experimental.pallas import tpu as pltpu
from jax.sharding import PartitionSpec as P

SEGS = 8
EPSILON = 1e-06
DECAY_SCALE = 8.0
GELU_C = 0.7978845608028654
GELU_A = 0.044715
F32 = jnp.float32
BF16 = jnp.bfloat16
VMEM_LIMIT = 58 << 20
STEPS = 16
ROWS = 8 * STEPS


def dot(left, right):
    return jnp.dot(left, right, preferred_element_type=F32)


def contract_first(left, right):
    return lax.dot_general(left, right, (((0,), (0,)), ((), ())), preferred_element_type=F32)


def contract_last(left, right):
    return lax.dot_general(left, right, (((1,), (1,)), ((), ())), preferred_element_type=F32)


def gelu_parts(y):
    y2 = y * y
    t = jnp.tanh(y * (GELU_C + (GELU_C * GELU_A) * y2))
    half = 0.5 + 0.5 * t
    slope = half + (0.5 * y) * (1.0 - t * t) * (GELU_C + (3.0 * GELU_C * GELU_A) * y2)
    return y * half, slope


def retained(log_decay, carried):
    y = 2.0 * log_decay
    series = -y * (1.0 + y * (1 / 2 + y * (1 / 6 + y * (1 / 24 + y * (1 / 120)))))
    return jnp.maximum(jnp.where(y > -0.0625, series, 1.0 - carried * carried), 1e-36)


def at(j):
    return pl.ds(8 * j, 8)


def tile_params():
    return pltpu.CompilerParams(dimension_semantics=("arbitrary",), vmem_limit_bytes=VMEM_LIMIT)


def wide_block(width, tiles=None, column=0):
    row = (lambda t: t) if tiles is None else (lambda t: tiles - 1 - t)
    return pl.BlockSpec((ROWS, width), lambda t: (row(t), column))


def whole(a):
    return pl.BlockSpec(a.shape, lambda t: (0,) * a.ndim)


def fixed(*dims):
    return pl.BlockSpec(dims, lambda t: (0,) * len(dims))


def forward_kernel(
    bx_ref, prev_ref, mask_ref, par_ref, gates_ref,
    conv_ref, low_ref, r_ref, i_ref, state_ref, decay_ref,
    lags, pre, carry,
):
    width = bx_ref.shape[1]

    @pl.when(pl.program_id(0) == 0)
    def _():
        lags[...] = prev_ref[...]
        carry[at(0), :] = jnp.zeros((8, width), F32)
        carry[at(1), :] = jnp.ones((8, width), F32)

    past = [lags[at(2 - k), :] for k in range(3)]
    for j in range(STEPS):
        now = bx_ref[at(j), :]
        m = mask_ref[at(j), :]
        out = par_ref[pl.ds(0, 1), :] + par_ref[pl.ds(1, 1), :] * now
        for k in range(3):
            out = out + par_ref[pl.ds(2 + k, 1), :] * (past[k] * m[:, k + 1 : k + 2])
        conv_ref[at(j), :] = out
        past = [now, past[0], past[1]]
    for k in range(3):
        lags[at(2 - k), :] = past[k]
    low = conv_ref[...].astype(BF16)
    low_ref[...] = low
    pre[...] = jnp.dot(low, gates_ref[...], preferred_element_type=F32)

    state, decay = carry[at(0), :], carry[at(1), :]
    for j in range(STEPS):
        live = jnp.broadcast_to(mask_ref[at(j), :][:, 1:2], state.shape) != 0.0
        r = 1.0 / (1.0 + jnp.exp(-(pre[at(j), pl.ds(0, width)] + par_ref[pl.ds(5, 1), :])))
        i = 0.5 + 0.5 * jnp.tanh(
            0.5 * (pre[at(j), pl.ds(width, width)] + par_ref[pl.ds(6, 1), :])
        )
        log_decay = par_ref[pl.ds(7, 1), :] * r
        a = jnp.exp(log_decay)
        e = retained(log_decay, a)
        drive = jnp.where(live, e * lax.rsqrt(e), 1.0) * (i * conv_ref[at(j), :])
        a = jnp.where(live, a, 0.0)
        state = a * state + drive
        decay = a * decay
        r_ref[at(j), :] = r
        i_ref[at(j), :] = i
        state_ref[at(j), :] = state
        decay_ref[at(j), :] = decay
    carry[at(0), :] = state
    carry[at(1), :] = decay


def forward_recurrence(both, prev, masks, params, gates):
    tokens, width = both.shape[0], prev.shape[1]
    size = tokens * width
    wide = wide_block(width)
    shape = lambda d: jax.ShapeDtypeStruct((tokens, width), d)
    return pl.pallas_call(
        forward_kernel,
        name="forward_recurrence",
        grid=(tokens // ROWS,),
        in_specs=[
            wide, whole(prev), pl.BlockSpec((ROWS, 8), lambda t: (t, 0)), whole(params),
            whole(gates),
        ],
        out_specs=[wide] * 6,
        out_shape=[shape(F32), shape(BF16), shape(F32), shape(F32), shape(F32), shape(F32)],
        scratch_shapes=[
            pltpu.VMEM((24, width), F32),
            pltpu.VMEM((ROWS, 2 * width), F32),
            pltpu.VMEM((16, width), F32),
        ],
        compiler_params=tile_params(),
        cost_estimate=pl.CostEstimate(
            flops=4 * size * width, bytes_accessed=30 * size, transcendentals=6 * size
        ),
    )(both, prev, masks, params, gates)


def reverse_kernel(
    dm_ref, by_ref, r_ref, state_ref, mask_ref, par_ref,
    grad_ref, reach_ref, dby_ref, head_ref,
    slopes,
):
    width = dm_ref.shape[1]

    @pl.when(pl.program_id(0) == 0)
    def _():
        head_ref[at(0), :] = jnp.zeros((8, width), F32)
        head_ref[at(1), :] = jnp.ones((8, width), F32)

    u, reach = head_ref[at(0), :], head_ref[at(1), :]
    for j in range(STEPS - 1, -1, -1):
        d = dm_ref[at(j), :]
        act, slope = gelu_parts(by_ref[at(j), :])
        slopes[at(j), :] = slope * (state_ref[at(j), :] * d)
        live = jnp.broadcast_to(mask_ref[at(j), :][:, 1:2], u.shape) != 0.0
        a = jnp.where(live, jnp.exp(par_ref[pl.ds(7, 1), :] * r_ref[at(j), :]), 0.0)
        g = d * act + u
        grad_ref[at(j), :] = g
        reach_ref[at(j), :] = reach
        u = a * g
        reach = a * reach
    head_ref[at(0), :] = u
    head_ref[at(1), :] = reach
    dby_ref[...] = slopes[...].astype(BF16)


def reverse_recurrence(dm, both, r, state, masks, params):
    tokens, width = dm.shape
    tiles = tokens // ROWS
    wide = wide_block(width, tiles)
    shape = lambda d: jax.ShapeDtypeStruct(dm.shape, d)
    return pl.pallas_call(
        reverse_kernel,
        name="reverse_recurrence",
        grid=(tiles,),
        in_specs=[
            wide, wide_block(width, tiles, 1), wide, wide, wide_block(8, tiles), whole(params),
        ],
        out_specs=[wide, wide, wide, fixed(16, width)],
        out_shape=[shape(F32), shape(F32), shape(BF16), jax.ShapeDtypeStruct((16, width), F32)],
        scratch_shapes=[pltpu.VMEM((ROWS, width), F32)],
        compiler_params=tile_params(),
        cost_estimate=pl.CostEstimate(
            flops=30 * dm.size, bytes_accessed=26 * dm.size, transcendentals=2 * dm.size
        ),
    )(dm, both, r, state, masks, params)


def gate_grad_kernel(
    grad_ref, reach_ref, r_ref, i_ref, conv_ref, state_ref, before_ref, bx_ref, bx_before_ref,
    mask_ref, dby_ref, prev_ref, ends_ref, par_ref, gates_ref,
    out_ref, tail_ref, edge_ref, sums_ref, both_ref,
    pair, direct, ahead,
):
    width = grad_ref.shape[1]
    step_at = pl.program_id(0)
    first = step_at == pl.num_programs(0) - 1

    @pl.when(step_at == 0)
    def _():
        sums_ref[...] = jnp.zeros_like(sums_ref)
        edge_ref[...] = jnp.zeros_like(edge_ref)

    @pl.when(first)
    def _():
        ahead[at(0), :] = ends_ref[at(0), :]
        for k in range(3):
            ahead[at(1 + k), :] = prev_ref[at(2 - k), :]

    @pl.when(jnp.logical_not(first))
    def _():
        ahead[at(0), :] = before_ref[...]
        for k in range(3):
            ahead[at(1 + k), :] = bx_before_ref[at(3 - k), :]

    message = ends_ref[at(1), :]
    zero = jnp.zeros((8, width), F32)
    sum_r = sum_i = sum_d = zero
    slope = par_ref[pl.ds(7, 1), :]
    past = ahead[at(0), :]
    for j in range(STEPS):
        g = grad_ref[at(j), :] + reach_ref[at(j), :] * message
        r, i, conv = r_ref[at(j), :], i_ref[at(j), :], conv_ref[at(j), :]
        live = jnp.broadcast_to(mask_ref[at(j), :][:, 1:2], g.shape) != 0.0
        log_decay = slope * r
        a = jnp.exp(log_decay)
        e = retained(log_decay, a)
        inv = lax.rsqrt(e)
        s = jnp.where(live, e * inv, 1.0)
        gi = g * i
        gic = gi * conv
        d_log = jnp.where(live, a * (g * past - gic * (a * inv)), 0.0)
        d_r = d_log * r
        d_pa = (slope * d_r) * (1.0 - r)
        d_pi = (gic * s) * (1.0 - i)
        direct[at(j), :] = gi * s
        pair[at(j), pl.ds(0, width)] = d_pa
        pair[at(j), pl.ds(width, width)] = d_pi
        sum_r = sum_r + d_pa
        sum_i = sum_i + d_pi
        sum_d = sum_d + d_r
        past = state_ref[at(j), :]
    for n, total in enumerate((sum_r, sum_i, sum_d)):
        sums_ref[at(n), :] += total

    both = pair[...].astype(BF16)
    both_ref[...] = both
    direct[...] += contract_last(both, gates_ref[...])

    p1, p2, p3 = (edge_ref[at(k), :] for k in range(3))
    sums = [zero] * 5
    w = [par_ref[pl.ds(1 + k, 1), :] for k in range(4)]

    def behind(j, k):
        return bx_ref[at(j - k), :] if j >= k else ahead[at(k - j), :]

    for j in range(STEPS - 1, -1, -1):
        d = direct[at(j), :]
        m = mask_ref[at(j), :]
        d1, d2, d3 = (d * m[:, k : k + 1] for k in (1, 2, 3))
        direct[at(j), :] = w[0] * d + p1
        p1 = w[1] * d1 + p2
        p2 = w[2] * d2 + p3
        p3 = w[3] * d3
        for n, term in enumerate((d * behind(j, 0), d1 * behind(j, 1), d2 * behind(j, 2), d3 * behind(j, 3))):
            sums[n + 1] = sums[n + 1] + term
        sums[0] = sums[0] + d
    for n, total in enumerate(sums):
        sums_ref[at(3 + n), :] += total
    for k, p in enumerate((p1, p2, p3)):
        edge_ref[at(k), :] = p
    out_ref[:, pl.ds(0, width)] = direct[...].astype(BF16)
    out_ref[:, pl.ds(width, width)] = dby_ref[...]

    @pl.when(step_at == 0)
    def _():
        tail_ref[...] = direct[pl.ds(ROWS - 32, 32), :]


def gate_gradients(grad, reach, r, i, conv, state, both, masks, dby, prev, ends, params, gates):
    tokens, width = grad.shape
    tiles = tokens // ROWS
    wide = wide_block(width, tiles)
    ahead = lambda n: pl.BlockSpec(
        (n, width), lambda t: (jnp.maximum((tiles - 1 - t) * (ROWS // n) - 1, 0), 0)
    )
    return pl.pallas_call(
        gate_grad_kernel,
        name="gate_gradients",
        grid=(tiles,),
        in_specs=[
            wide, wide, wide, wide, wide, wide, ahead(8), wide, ahead(32), wide_block(8, tiles),
            wide, whole(prev), whole(ends), whole(params), whole(gates),
        ],
        out_specs=[
            wide_block(2 * width, tiles), fixed(32, width), fixed(24, width), fixed(64, width),
            wide_block(2 * width, tiles),
        ],
        out_shape=[
            jax.ShapeDtypeStruct((tokens, 2 * width), BF16),
            jax.ShapeDtypeStruct((32, width), F32),
            jax.ShapeDtypeStruct((24, width), F32),
            jax.ShapeDtypeStruct((64, width), F32),
            jax.ShapeDtypeStruct((tokens, 2 * width), BF16),
        ],
        scratch_shapes=[
            pltpu.VMEM((ROWS, 2 * width), F32),
            pltpu.VMEM((ROWS, width), F32),
            pltpu.VMEM((32, width), F32),
        ],
        compiler_params=tile_params(),
        cost_estimate=pl.CostEstimate(
            flops=4 * grad.size * width, bytes_accessed=38 * grad.size,
            transcendentals=2 * grad.size,
        ),
    )(grad, reach, r, i, conv, state, state, both, both, masks, dby, prev, ends, params, gates)


def settle_kernel(main_ref, tail_ref, edge_ref, beyond_ref, out_ref):
    del main_ref
    width = tail_ref.shape[1]
    row = lax.broadcasted_iota(jnp.int32, (8, width), 0)
    steps = [tail_ref[at(0), :]]
    for k in (2, 1, 0):
        up = pltpu.roll(edge_ref[at(k), :], 7, 0)
        up = jnp.where(row == 7, beyond_ref[pl.ds(k, 1), :], up)
        steps.append(tail_ref[at(3 - k), :] + up)
    out_ref[...] = jnp.concatenate(steps, axis=0).astype(BF16)


def settled(main, tail, edge, beyond):
    rows, width = tail.shape
    last = pl.BlockSpec((rows, width), lambda t: (main.shape[0] // rows - 1, 0))
    return pl.pallas_call(
        settle_kernel,
        name="settle",
        grid=(1,),
        in_specs=[last, whole(tail), whole(edge), whole(beyond)],
        out_specs=last,
        out_shape=jax.ShapeDtypeStruct(main.shape, main.dtype),
        input_output_aliases={0: 0},
        compiler_params=tile_params(),
        cost_estimate=pl.CostEstimate(flops=4 * tail.size, bytes_accessed=12 * tail.size, transcendentals=0),
    )(main, tail, edge, beyond)


def units_kernel(
    n2_ref, gate_ref, up_ref, d_hid_ref, hid_ref, d_gate_ref, d_up_ref, pull_ref
):
    tokens = n2_ref.shape[0]
    step_at = pl.program_id(0)
    rows = min(256, tokens)
    for t in range(tokens // rows):
        here = pl.ds(t * rows, rows)
        gate = dot(n2_ref[here, :], gate_ref[...])
        up = dot(n2_ref[here, :], up_ref[...])
        act, slope = gelu_parts(gate)
        d_hid = d_hid_ref[here, :]
        d_gate = (slope * up * d_hid).astype(BF16)
        d_up = (act * d_hid).astype(BF16)
        hid_ref[here, :] = (act * up).astype(BF16)
        d_gate_ref[here, :] = d_gate
        d_up_ref[here, :] = d_up
        pull = d_gate.astype(F32) * gate + d_up.astype(F32) * up
        pull = sum(pull[:, n : n + 128] for n in range(0, pull.shape[1], 128))

        @pl.when(step_at == 0)
        def _():
            pull_ref[here, :] = pull

        @pl.when(step_at > 0)
        def _():
            pull_ref[here, :] += pull


def mlp_units(n2, gate_weight, up_weight, d_hid):
    tokens, width = n2.shape
    units = d_hid.shape[1]
    each = 512 if units % 512 == 0 else 256
    column = lambda rows: pl.BlockSpec((rows, each), lambda j: (0, j))
    low = jax.ShapeDtypeStruct((tokens, units), BF16)
    return pl.pallas_call(
        units_kernel,
        name="mlp_units",
        grid=(units // each,),
        in_specs=[
            pl.BlockSpec((tokens, width), lambda j: (0, 0), pipeline_mode=pl.Buffered(1)),
            column(width), column(width), column(tokens),
        ],
        out_specs=[column(tokens)] * 3 + [pl.BlockSpec((tokens, 128), lambda j: (0, 0))],
        out_shape=[low, low, low, jax.ShapeDtypeStruct((tokens, 128), F32)],
        compiler_params=pltpu.CompilerParams(
            dimension_semantics=("arbitrary",), vmem_limit_bytes=48 << 20
        ),
        cost_estimate=pl.CostEstimate(
            flops=4 * tokens * width * units, transcendentals=tokens * units,
            bytes_accessed=2 * (tokens * width + 2 * width * units) + 10 * tokens * units,
        ),
    )(n2, gate_weight, up_weight, d_hid)


def shifted(x, axis, by):
    peers = lax.axis_size(axis)
    pairs = [(i, i + by) for i in range(peers) if 0 <= i + by < peers]
    return lax.ppermute(x, axis, pairs)


def bit_orders():
    bits = (lax.axis_size("seq") - 1).bit_length()
    outer = list(range(1, bits))
    return outer, outer[::-1]


def across(x, bit, axis="seq"):
    n = lax.axis_size(axis)
    return lax.ppermute(x, axis, [(i, i ^ (1 << bit)) for i in range(n)])


def own_bit(bit, axis="seq"):
    return (lax.axis_index(axis) >> bit) & 1


def relative(x, order, axis=1):
    n = lax.axis_size("seq")
    each = x.shape[axis] // n
    bits = len(order)
    out = []
    for place in range(n):
        number = sum(1 << bit for k, bit in enumerate(order) if place >> (bits - 1 - k) & 1)
        start = (lax.axis_index("seq") ^ number) * each
        out.append(lax.dynamic_slice_in_dim(x, start, each, axis))
    return jnp.concatenate(out, axis=axis)


def crossed(x, bit, axis):
    half = x.shape[axis] // 2
    give = lax.slice_in_dim(x, half, 2 * half, axis=axis).astype(BF16)
    keep = lax.slice_in_dim(x, 0, half, axis=axis).astype(F32)
    return keep + across(give, bit).astype(F32)


def exchanged(x, axis):
    n = lax.axis_size(axis)
    for bit in range((n - 1).bit_length()):
        x = x + across(x, bit, axis)
    return x


def places(order):
    n = lax.axis_size("seq")
    away = lax.axis_index("seq") ^ jnp.arange(n, dtype=jnp.int32)
    bits = len(order)
    return sum(((away >> bit) & 1) << (bits - 1 - k) for k, bit in enumerate(order))


def picked(own_a, far_a, own_b, far_b, tables, fill, outs, name):
    n = lax.axis_size("seq")
    half = n // 2

    def kernel(at_a, at_b, own_a_ref, far_a_ref, own_b_ref, far_b_ref, *refs):
        step_at = pl.program_id(0)
        for at, side, own, far in ((at_a, 0, own_a_ref, far_a_ref), (at_b, 1, own_b_ref, far_b_ref)):
            near = at[step_at] < half

            @pl.when(near)
            def _():
                fill(side, own, refs)

            @pl.when(jnp.logical_not(near))
            def _():
                fill(side, far, refs)

    def pick(array, which, far):
        def block(s, *at):
            here, other = at[which][s], at[which][s ^ 1]
            return array[2](lax.rem(jnp.where((here >= half) == far, here, other), half))

        return pl.BlockSpec(array[1], block)

    arrays = (own_a, far_a, own_b, far_b)
    return pl.pallas_call(
        kernel,
        name=name,
        grid_spec=pltpu.PrefetchScalarGridSpec(
            num_scalar_prefetch=2,
            grid=(n,),
            in_specs=[
                pick(own_a, 0, False), pick(far_a, 0, True), pick(own_b, 1, False),
                pick(far_b, 1, True),
            ],
            out_specs=[pl.BlockSpec(block, at) for _, block, at in outs],
        ),
        out_shape=[shape for shape, _, _ in outs],
        compiler_params=pltpu.CompilerParams(
            dimension_semantics=("arbitrary",), vmem_limit_bytes=40 << 20
        ),
        cost_estimate=pl.CostEstimate(
            flops=0, transcendentals=0,
            bytes_accessed=sum(a[0].size * 2 for a in arrays) + sum(o[0].size * 4 for o in outs),
        ),
    )(*tables, *(a[0] for a in arrays))


def ordered(own_a, far_a, own_b, far_b, tables, outputs, name):
    n = lax.axis_size("seq")
    each = own_a.shape[1] // (n // 2)
    wrap = lambda a: (a, (a.shape[0], each), lambda place: (0, place))

    def fill(side, ref, refs):
        for out, pieces in zip(refs, outputs):
            row = 0
            for route, start, rows in pieces:
                if route == side:
                    out[pl.ds(row, rows), :] = ref[pl.ds(start, rows), :].astype(F32)
                row += rows

    heights = [sum(rows for _, _, rows in pieces) for pieces in outputs]
    outs = [
        (jax.ShapeDtypeStruct((h, n * each), F32), (h, each), lambda s, *at: (0, s))
        for h in heights
    ]
    return picked(wrap(own_a), wrap(far_a), wrap(own_b), wrap(far_b), tables, fill, outs, name)


def joined(x, order):
    x = x[None]
    for bit in order:
        x = jnp.concatenate([x, across(x, bit)])
    return x


def mlp_weights(own_a, far_a, own_b, far_b, tables, lead):
    n = lax.axis_size("seq")
    units = own_a.shape[2]
    cut = own_a.shape[1] - lead
    wrap = lambda a: (a, (1, *a.shape[1:]), lambda place: (place, 0, 0))

    def fill(side, ref, refs):
        refs[side][0] = ref[0, pl.ds(0, lead), :]
        refs[2][0, side] = ref[0, pl.ds(lead, cut), :]

    full = (jax.ShapeDtypeStruct((n, lead, units), BF16), (1, lead, units), lambda s, *at: (s, 0, 0))
    down = (
        jax.ShapeDtypeStruct((n, 2, cut, units), BF16), (1, 2, cut, units),
        lambda s, *at: (s, 0, 0, 0),
    )
    gate, up, down = picked(
        wrap(own_a), wrap(far_a), wrap(own_b), wrap(far_b), tables, fill, [full, full, down], "mlp_weights"
    )
    return gate.reshape(-1, units), up.reshape(-1, units), down.reshape(-1, units)


def output_rows(own_a, far_a, own_b, far_b, tables):
    n = lax.axis_size("seq")
    _, groups, part, middle = own_a.shape
    wrap = lambda a: (a, (1, *a.shape[1:]), lambda place: (place, 0, 0, 0))

    def fill(side, ref, refs):
        refs[0][:, 0, :, pl.ds(side * middle, middle)] = ref[0]

    out = (
        jax.ShapeDtypeStruct((groups, n, part, 2 * middle), BF16), (groups, 1, part, 2 * middle),
        lambda s, *at: (0, s, 0, 0),
    )
    return picked(
        wrap(own_a), wrap(far_a), wrap(own_b), wrap(far_b), tables, fill, [out], "output_rows"
    )[0].reshape(-1, 2 * middle)


def chained(decays, values, place, reverse):
    devices, stretches = decays.shape[:2]
    total = jnp.zeros_like(values[0, 0])
    out = []
    hops = [(d, s) for d in range(devices) for s in range(stretches)]
    own_d = lax.dynamic_index_in_dim(decays, place, 0, False)
    own_v = lax.dynamic_index_in_dim(values, place, 0, False)
    order = range(stretches - 1, -1, -1) if reverse else range(stretches)
    whole_d, whole_v = [], []
    for d in range(devices):
        decay, value = jnp.ones_like(total), jnp.zeros_like(total)
        for s in order:
            value = values[d, s] + decays[d, s] * value
            decay = decay * decays[d, s]
        whole_d.append(decay)
        whole_v.append(value)
    for hop in range(devices - 1):
        d = devices - 1 - hop if reverse else hop
        live = d > place if reverse else d < place
        total = jnp.where(live, whole_v[d] + whole_d[d] * total, total)
    for s in order:
        out.append(total)
        total = own_v[s] + own_d[s] * total
    return jnp.stack(out[::-1] if reverse else out)


def gelu(y):
    return y * (0.5 + 0.5 * jnp.tanh(y * (GELU_C + (GELU_C * GELU_A) * (y * y))))


def side_by_side(x):
    rows = x.shape[0]
    return jnp.swapaxes(x.reshape(8, rows // 8, *x.shape[1:]), 0, 1).reshape(x.shape)


def in_order(x):
    rows = x.shape[0]
    return jnp.swapaxes(x.reshape(rows // 8, 8, *x.shape[1:]), 0, 1).reshape(x.shape)


def block_diagonal(blocks, padded):
    count, size, _ = blocks.shape
    rows = [
        jnp.pad(blocks[b], ((0, 0), (b * size, padded - (b + 1) * size))) for b in range(count)
    ]
    return jnp.pad(jnp.concatenate(rows, axis=0), ((0, padded - count * size), (0, 0)))


def after(value, *others):
    return lax.optimization_barrier((value, *others))[0]


def row_major(x):
    return with_layout_constraint(x, Layout(major_to_minor=tuple(range(x.ndim))))


def gather_features(x):
    return lax.all_gather(x, "tp", axis=1, tiled=True)


def scatter_features(x):
    return lax.psum_scatter(x.astype(BF16), "tp", scatter_dimension=1, tiled=True).astype(F32)


def on_device(
    hidden_in, segment_ids, first_gain, input_weight, gelu_weight, conv_weight, conv_bias,
    recur_gate, input_gate, recur_bias, input_bias, decay_param, output_weight, second_gain,
    gate_weight, up_weight, down_weight, grad_out,
):
    tokens, share = hidden_in.shape
    channels = input_weight.shape[1]
    padded = -(-channels // 128) * 128
    extra = padded - channels
    taps = conv_weight.shape[0]
    halo = taps - 1
    blocks, size = recur_gate.shape[0], recur_gate.shape[1]
    width = grad_out.shape[1]
    units = gate_weight.shape[1]
    seq_devices = lax.axis_size("seq")
    tp_devices = lax.axis_size("tp")
    seq_place = lax.axis_index("seq")
    share_start = lax.axis_index("tp") * share
    order_a, order_b = bit_orders()

    route_a, route_b = [0, *order_a], [0, *order_b]

    x_low = side_by_side(hidden_in)
    full = gather_features(x_low)

    down_t = down_weight.T
    lead = down_t.shape[0]
    cut = lead // 2
    legs = [
        (jnp.concatenate([gate_weight, down_t[:cut]]), order_a),
        (jnp.concatenate([up_weight, down_t[cut:]]), order_b),
    ]
    first = [joined(a, order[:-1]) for a, order in legs]
    (
        segment_ids, input_weight, gelu_weight, recur_gate, input_gate, output_weight, grad_out,
        *first,
    ) = lax.optimization_barrier(
        (segment_ids, input_weight, gelu_weight, recur_gate, input_gate, output_weight, grad_out, *first)
    )
    second = [across(a, order[-1]) for a, (_, order) in zip(first, legs)]
    part = channels // seq_devices
    own_rows = lax.dynamic_slice_in_dim(output_weight, seq_place * part, part, 0)

    ids = segment_ids.astype(F32)
    prev_ids = shifted(ids[tokens - halo :], "seq", 1)
    prev_ids = jnp.where(seq_place == 0, -1.0, prev_ids)
    next_id = jnp.where(seq_place == seq_devices - 1, -1.0, shifted(ids[:1], "seq", -1))
    ext = jnp.concatenate([prev_ids, ids])
    same = [(ext[halo - k : halo - k + tokens] == ids).astype(F32) for k in range(taps)]
    masks = side_by_side(jnp.stack(same + [jnp.zeros_like(ids)] * (8 - taps), axis=1))
    next_ids = jnp.concatenate([ids[1:], next_id])
    closing = (next_ids != ids).astype(F32)[None, :]
    member = (segment_ids[None, :] == jnp.arange(SEGS, dtype=jnp.int32)[:, None]).astype(F32)
    picks = side_by_side((member * closing).T).T

    slope = -DECAY_SCALE * jax.nn.softplus(-decay_param)
    params = jnp.concatenate(
        [jnp.stack([conv_bias]), conv_weight, jnp.stack([recur_bias, input_bias, slope])], axis=0
    )
    params = jnp.pad(params, ((0, 0), (0, extra)))
    gates = jnp.concatenate(
        [block_diagonal(recur_gate, padded), block_diagonal(input_gate, padded)], axis=1
    )
    pad_rows = lambda a: jnp.pad(a, ((0, extra), (0, 0)))
    branch_weight = jnp.concatenate([pad_rows(input_weight.T), pad_rows(gelu_weight.T)], axis=0)
    output_padded = pad_rows(output_weight)
    grad_rows = side_by_side(grad_out)
    params, gates, branch_weight, output_padded, grad_rows, masks, own_rows, full = (
        lax.optimization_barrier(
            (params, gates, branch_weight, output_padded, grad_rows, masks, own_rows, full)
        )
    )

    x = full.astype(F32)
    r1 = lax.rsqrt(jnp.mean(x * x, axis=1, keepdims=True) + EPSILON)
    n1 = (x * r1 * first_gain).astype(BF16)
    both = row_major(contract_last(n1, branch_weight))
    last = both[tokens - 8 * halo :, :padded].reshape(halo, 8, padded)
    before = shifted(last[:, 7], "seq", 1)
    prev = jnp.concatenate([before[:, None], last[:, :7]], axis=1).reshape(8 * halo, padded)
    over_tp = lax.all_gather(own_rows, "tp", axis=0, tiled=True)
    both, *second = lax.optimization_barrier((both, *second))
    conv, low, r, i, local, reach = forward_recurrence(both, prev, masks, params, gates)
    ends = jnp.stack([reach[tokens - 8 :], local[tokens - 8 :]])
    ends, over_tp = lax.optimization_barrier((ends, over_tp))
    ends = lax.all_gather(ends, "seq", axis=0)
    incoming = chained(ends[:, 0], ends[:, 1], seq_place, False)
    steps = lambda a: a.reshape(tokens // 8, 8, padded)
    state = (steps(local) + steps(reach) * incoming[None]).reshape(tokens, padded)
    mixed = (gelu(both[:, padded : padded + channels]) * state[:, :channels]).astype(BF16)
    mixed_full = lax.all_gather(mixed, "tp", axis=1, tiled=True)
    over_tp, _ = lax.optimization_barrier((over_tp, mixed))
    over_tp = over_tp.reshape(tp_devices, part, width)
    middle = width // 2
    rows_a = joined(over_tp[:, :, :middle], order_a)
    rows_b = joined(over_tp[:, :, middle:], order_b)
    grad_rows, *held = lax.optimization_barrier((grad_rows, *first, *second, mixed))
    own_a, own_b = (
        jnp.concatenate([held[leg], held[leg + len(legs)]]) for leg in range(len(legs))
    )
    tables = places([0, *order_a[::-1]]), places([0, *order_b[::-1]])
    gate_full, up_full, down_full = mlp_weights(
        own_a, across(own_a, 0), own_b, across(own_b, 0), tables, lead
    )
    d_hid = dot(grad_rows, down_full)
    output_full = output_rows(rows_a, across(rows_a, 0), rows_b, across(rows_b, 0), tables)
    d_hid, output_full, gate_full, up_full = lax.optimization_barrier(
        (d_hid, output_full, gate_full, up_full)
    )
    resid = x + dot(mixed_full, output_full)

    r2 = lax.rsqrt(jnp.mean(resid * resid, axis=1, keepdims=True) + EPSILON)
    n2 = (resid * r2 * second_gain).astype(BF16)
    hid, d_gate, d_up, pull2 = mlp_units(n2, gate_full, up_full, d_hid)
    d_n2_part = (contract_last(d_gate, gate_full) + contract_last(d_up, up_full)).astype(BF16)
    d_n2 = scatter_features(d_n2_part)
    n2_w, hid_w, pull2 = lax.optimization_barrier((n2, hid, pull2, d_n2_part))[:3]
    pull2 = lax.psum(jnp.sum(pull2, axis=1), "tp")[:, None]
    grad_w = after(grad_rows, d_n2_part)
    grad_a, grad_b = relative(grad_w, route_a), relative(grad_w, route_b)
    half = units // 2
    n2_a, n2_b = relative(n2_w, route_a), relative(n2_w, route_b)
    products = [
        (n2_a, d_gate, order_a), (n2_b, d_up, order_b),
        (grad_a, hid_w[:, :half], order_a), (grad_b, hid_w[:, half:], order_b),
    ]
    middle = width // 2
    gives = [across(contract_first(l[:, middle:], r).astype(BF16), 0) for l, r, _ in products]
    sums2 = [
        contract_first(l[:, :middle], r) + give.astype(F32)
        for (l, r, _), give in zip(products, gives)
    ]
    d_n2, pull2, *sums2 = lax.optimization_barrier((d_n2, pull2, *sums2))
    gain_share = lax.dynamic_slice_in_dim(second_gain, share_start, share)
    scaled = d_n2 * gain_share * r2
    scaled_low = scaled.astype(BF16)
    scaled_full = gather_features(scaled_low)
    hid_w, state_w, resid_w, d_n2_w, n1_w, _, *sums2 = lax.optimization_barrier(
        (hid_w, state, resid, d_n2, n1, scaled_low, *sums2)
    )
    n1_a, n1_b = relative(n1_w, route_a), relative(n1_w, route_b)
    finals = jnp.dot(picks, state_w, precision=lax.Precision.HIGHEST, preferred_element_type=F32)
    resid_share = lax.dynamic_slice_in_dim(resid_w, share_start, share, 1)
    grad_second = jnp.sum(d_n2_w * resid_share * r2, axis=0)
    mlp = contract_last(hid_w, down_full).astype(BF16)
    for leg in range(len(order_a) - 1):
        sums2 = [crossed(v, order[leg], 0) for v, (_, _, order) in zip(sums2, products)]
    centre = r2 * r2 * pull2 * (1.0 / width)
    last_gives = [v[v.shape[0] // 2 :].astype(BF16) for v in sums2]
    kept2 = [v[: v.shape[0] // 2] for v in sums2]
    scaled_full, mlp, finals, grad_second, n1_a, n1_b, *last_gives = lax.optimization_barrier(
        (scaled_full, mlp, finals, grad_second, n1_a, n1_b, *last_gives)
    )
    mlp_sum = lax.psum_scatter(mlp, "tp", scatter_dimension=1, tiled=True)
    d_resid_low = (
        grad_rows.astype(F32) + scaled_full.astype(F32) - resid * centre
    ).astype(BF16)
    last_gives = [across(v, order[-1]) for v, (_, _, order) in zip(last_gives, products)]

    dm = row_major(contract_last(d_resid_low, output_padded))
    grad_local, reach_back, dby, heads = reverse_recurrence(dm, both, r, state, masks, params)
    heads, *last_gives = lax.optimization_barrier((heads, *last_gives))
    outgoing = lax.all_gather(heads.reshape(2, 8, padded), "seq", axis=0)
    message = chained(outgoing[:, 1], outgoing[:, 0], seq_place, True)
    border = jnp.concatenate([incoming, message])
    d_main, tail, edge, sums, pair = gate_gradients(
        grad_local, reach_back, r, i, conv, state, both, masks, dby, prev, border, params, gates
    )
    beyond = shifted(edge.reshape(halo, 8, padded)[:, 0], "seq", -1)
    d_branch = settled(d_main, tail, edge, beyond)
    d_n1_part = dot(d_branch, branch_weight).astype(BF16)
    d_n1_part, mlp_sum = lax.optimization_barrier((d_n1_part, mlp_sum))
    d_n1 = scatter_features(d_n1_part)
    d_branch_w, pair, sums, d_n1_w = lax.optimization_barrier((d_branch, pair, sums, d_n1_part))
    dbx_w, dby_w = d_branch_w[:, :channels], d_branch_w[:, padded : padded + channels]
    back = lambda l, r: contract_first(l, r[:, middle:]).astype(BF16)
    front = lambda l, r: contract_first(l, r[:, :middle])
    give_a, give_b = back(dbx_w, n1_a), back(dby_w, n1_b)
    give_a, give_b, pair, sums, d_resid_w, d_n1_w, dbx_w, dby_w = lax.optimization_barrier(
        (give_a, give_b, pair, sums, d_resid_low, d_n1_w, dbx_w, dby_w)
    )

    def rest(total_a, total_b):
        for bit_a, bit_b in zip(order_a, order_b):
            total_a, total_b = crossed(total_a, bit_a, 1), crossed(total_b, bit_b, 1)
        total_a, total_b = total_a.astype(BF16), total_b.astype(BF16)
        alone = total_a, total_b
        for bit_a, bit_b in zip(order_a[::-1], order_b[::-1]):
            total_a = jnp.concatenate([total_a, across(total_a, bit_a)], axis=1)
            total_b = jnp.concatenate([total_b, across(total_b, bit_b)], axis=1)
        return alone, (total_a, across(total_a, 0), total_b, across(total_b, 0))

    far_a, far_b = across(give_a, 0), across(give_b, 0)
    ready, branch_parts = rest(
        front(dbx_w, n1_a) + far_a.astype(F32), front(dby_w, n1_b) + far_b.astype(F32)
    )
    first_part = jnp.sum(d_n1_w.astype(F32) * n1.astype(F32), axis=0) / first_gain
    pull1 = jnp.sum(d_n1_w.astype(F32) * n1.astype(F32), axis=1)
    second_part = lax.dynamic_update_slice(jnp.zeros((width,), F32), grad_second, (share_start,))
    over_tp = exchanged(jnp.concatenate([pull1, first_part, second_part]), "tp")
    pull1, gains = over_tp[:tokens, None], over_tp[tokens:]
    resid_a, resid_b = relative(d_resid_w, route_a), relative(d_resid_w, route_b)
    cut = channels // 2
    mixed_a, mixed_b = mixed[:, :cut], mixed[:, cut:]
    gate_grads = contract_first(low, pair)
    corner = lambda n, b: gate_grads[
        b * size : (b + 1) * size, n * padded + b * size : n * padded + (b + 1) * size
    ]
    corners = jnp.concatenate([corner(n, b) for b in range(blocks) for n in (0, 1)], axis=1)
    corners = jnp.pad(corners, ((0, 0), (0, width - corners.shape[1])))
    corners = relative(corners, route_b)
    sums = jnp.sum(sums.reshape(8, 8, padded), axis=1)
    small = jnp.concatenate([sums, finals], axis=0)[:, :channels]
    packed = jnp.concatenate([gains, small.reshape(-1)])
    packed = jnp.pad(packed, (0, -packed.size % (8 * width))).reshape(-1, width)
    few = packed.shape[0]
    packed = relative(packed, route_a)
    far_a = across(
        jnp.concatenate([back(mixed_a, resid_a), packed[:, middle:].astype(BF16)]), 0
    )
    far_b = across(
        jnp.concatenate([back(mixed_b, resid_b), corners[:, middle:].astype(BF16)]), 0
    )
    _, other_parts = rest(
        jnp.concatenate(
            [
                front(mixed_a, resid_a) + far_a[:cut].astype(F32),
                packed[:, :middle] + far_a[cut:].astype(F32),
            ]
        ),
        jnp.concatenate(
            [
                front(mixed_b, resid_b) + far_b[:cut].astype(F32),
                corners[:, :middle] + far_b[cut:].astype(F32),
            ]
        ),
    )

    kept2, last_gives, mlp_sum, d_n1, resid_share = lax.optimization_barrier(
        (kept2, last_gives, mlp_sum, d_n1, resid_share, ready)
    )[:5]
    done2 = [v + give.astype(F32) for v, give in zip(kept2, last_gives)]
    grad_gate_weight, grad_up_weight = done2[:2]
    grad_down_weight = jnp.concatenate(done2[2:], axis=1).T
    g_share = lax.dynamic_slice_in_dim(grad_rows, share_start, share, 1).astype(F32)
    d_resid_share = g_share + scaled - resid_share * centre
    block_out = in_order((resid_share + mlp_sum.astype(F32)).astype(BF16))
    gain1_share = lax.dynamic_slice_in_dim(first_gain, share_start, share)
    grad_in = (
        d_resid_share
        + d_n1 * gain1_share * r1
        - x_low.astype(F32) * (r1 * r1 * pull1 * (1.0 / width))
    )
    grad_in = in_order(grad_in.astype(BF16))
    tables = places(route_a), places(route_b)
    grad_input, grad_gelu = ordered(
        *branch_parts, tables, [[(0, 0, channels)], [(1, 0, channels)]], "branch_gradients"
    )
    done = (block_out, grad_in, grad_gate_weight, grad_up_weight, grad_down_weight, grad_input, grad_gelu)
    other_parts, done = lax.optimization_barrier((other_parts, done))
    block_out, grad_in, grad_gate_weight, grad_up_weight, grad_down_weight, grad_input, grad_gelu = done
    grad_output_weight, packed, corners = ordered(
        *other_parts,
        tables,
        [[(0, 0, cut), (1, 0, cut)], [(0, cut, few)], [(1, cut, size)]],
        "other_gradients",
    )
    packed = packed.reshape(-1)
    gains = packed[: 2 * width]
    small = packed[2 * width : 2 * width + small.size].reshape(small.shape)
    corners = jnp.swapaxes(corners[:, : 2 * blocks * size].reshape(size, blocks, 2, size), 0, 1)
    grad_decay = small[2] * (DECAY_SCALE * jax.nn.sigmoid(-decay_param))
    return (
        block_out,
        grad_in,
        gains[:width],
        grad_input.T,
        grad_gelu.T,
        small[4:8],
        small[3],
        corners[:, :, 0],
        corners[:, :, 1],
        small[0],
        small[1],
        grad_decay,
        grad_output_weight,
        gains[width:],
        grad_gate_weight,
        grad_up_weight,
        grad_down_weight,
        small[8:],
    )


def solution(mesh):
    row = P("tp")
    return jax.shard_map(
        on_device,
        mesh=mesh,
        in_specs=(
            P("seq", "tp"), P("seq"), P(), P(None, "tp"), P(None, "tp"), P(None, "tp"), row,
            P("tp", None, None), P("tp", None, None), row, row, row, P("tp", None), P(),
            P("seq", "tp"), P("seq", "tp"), P("tp", "seq"), P("seq", None),
        ),
        out_specs=(
            P("seq", "tp"), P("seq", "tp"), P(), P(None, "tp"), P(None, "tp"), P(None, "tp"), row,
            P("tp", None, None), P("tp", None, None), row, row, row, P("tp", None), P(),
            P("seq", "tp"), P("seq", "tp"), P("tp", "seq"), P(None, "tp"),
        ),
        check_vma=False,
    )
```

time: 1130 us -> 760 us (0.67)
  waiting for transfers between devices: 637 us -> 212 us
  blocking collectives: 110 us -> 32.4 us
  local copies, waits for them, and re-layouts: 23.6 us -> 96.8 us
  starting transfers between devices: 7.96 us -> 55.9 us
  other arithmetic: 63.1 us -> 78.2 us
    reduce_scatter x7 -> x3, waiting for transfers between devices: 297 us -> 16.3 us  [the longest x2 14.6 us: scatter_features(): lax.psum_scatter(x.astype(BF16), 'tp', scatter_dimension=1, tiled=True)]
    all_gather x6 -> x4, waiting for transfers between devices: 244 us -> 44.5 us  [the longest x2 34.5 us: gather_features(): return lax.all_gather(x, 'tp', axis=1, tiled=True)]
    ppermute x0 -> x50, waiting for transfers between devices: none -> 149 us  [across(): return lax.ppermute(x, axis, [(i, i ^ 1 << bit) for i in range(n)])]
    psum x2 -> x0, waiting for transfers between devices: 92.1 us -> none  [the longest x1 75.3 us: on_device(): lax.psum(contract_first(dbx, n1).astype(BF16), 'seq').astype(F32)]
    psum x4 -> x1, blocking collectives: 87.9 us -> 9.9 us  [on_device(): pull2 = lax.psum(jnp.sum(pull2, axis=1), 'tp')[:, None]]
    pallas_call x0 -> x6, Pallas kernels: none -> 58.7 us  [the longest x4 33.8 us: picked(): pl.pallas_call(kernel, name=name, grid_spec=pltpu.PrefetchScalarGridSpec(...]
    ppermute x0 -> x50, starting transfers between devices: none -> 48 us  [across(): return lax.ppermute(x, axis, [(i, i ^ 1 << bit) for i in range(n)])]
    pallas_call x1, Pallas kernels: 46.4 us -> 18.4 us  [gate_gradients(): pl.pallas_call(gate_grad_kernel, name='gate_gradients', grid=(tiles,), in...]
  transfers between devices with their start and end apart: 19 -> 61, of which waited for: 12 -> 29; matrix products, arithmetic and copies ran while one was open for 15% -> 32% of each run, Pallas kernels for 5% -> 9%
where the time goes in v2:
time: 760 us; the launch traced here: 749 us
  waiting for transfers between devices  212 us (28%)
  matrix products  157 us (21%)
  Pallas kernels  99.4 us (13%)
  local copies, waits for them, and re-layouts  96.8 us (13%)
  other arithmetic  78.2 us (10%)
  starting transfers between devices  55.9 us (7%)
  blocking collectives  32.4 us (4%)
  between operations  17.1 us (2%)
    ppermute x50, waiting for transfers between devices, across(): return lax.ppermute(x, axis, [(i, i ^ 1 << bit) for i in range(n)])  149 us
    dot_general x17, matrix products, contract_first(): lax.dot_general(left, right, (((0,), (0,)), ((), ())), preferred_element_...  64.8 us
    ppermute x50, starting transfers between devices, across(): return lax.ppermute(x, axis, [(i, i ^ 1 << bit) for i in range(n)])  48 us
    dot_general x5, matrix products, contract_last(): lax.dot_general(left, right, (((1,), (1,)), ((), ())), preferred_element_...  47.4 us
    dot_general x3, matrix products, dot(): return jnp.dot(left, right, preferred_element_type=F32)  41.5 us
    unnamed x262, local copies, waits for them, and re-layouts  35.4 us
    all_gather x2, waiting for transfers between devices, gather_features(): return lax.all_gather(x, 'tp', axis=1, tiled=True)  34.5 us
    pallas_call x4, Pallas kernels, picked(): pl.pallas_call(kernel, name=name, grid_spec=pltpu.PrefetchScalarGridSpec(...  33.8 us
  transfers between devices with their start and end apart: 61, of which 29 were waited for; matrix products, arithmetic and copies ran while one was open for 32% of the time, Pallas kernels for 9%

profile of v2, /device:TPU:0, one launch (start us, length us, event | category | flops | bytes accessed | tf_op | source)
XLA Modules:
  0.0 749.4 jit_solution(17721197101665175336)
XLA Ops:
  19.2 20.5 %collective-permute-done.1 = bf16[1,384,1536]{2,1,0:T(8,128)(2,1)} collective-permute-done((bf16[1,384,1536]{2,1,0:T(8,128)(2,1)S(1)}, bf16[1,384,1536]{2,1,0:T(8,128)(2,1)}, u32[]{:S(2)}, u32[]{:S(2)}) %collective-permute-start.1) | collective-permute-done | bytes 1179680 | tf_op jit(solution)/shard_map/ppermute | solution.py:423
  49.4 4.3 copy.100
  64.1 10.5 %fusion.7 = bf16[1536,2048]{1,0:T(8,128)(2,1)} fusion(bf16[704,2048]{1,0:T(8,128)(2,1)S(1)} %bitcast.1907, bf16[704,2048]{1,0:T(8,128)(2,1)S(1)} %bitcast.1908), kind=kLoop, calls=%fused_computation.17 | loop fusion | flops 25165824 | bytes 12058624 | tf_op jit(solution)/shard_map/concatenate | solution.py:705
  77.1 16.7 %all-gather.6.cloned.1.call-done = bf16[1024,2048]{1,0:T(8,128)(2,1)} async-done(((bf16[1024,512]{1,0:T(8,128)(2,1)}), bf16[1024,2048]{1,0:T(8,128)(2,1)}) %all-gather.6.cloned.1.call-update) | async-done | bytes 4194320 | tf_op jit(solution)/shard_map/all_gather | solution.py:634
  100.4 10.4 %fusion.402.bx_ref.by_ref.bx_before_ref = f32[1024,1536]{1,0:T(8,128)S(1)} fusion(bf16[1024,2048]{1,0:T(8,128)(2,1)S(1)} %fusion.4, bf16[1536,2048]{1,0:T(8,128)(2,1)} %fusion.7), kind=kOutput, calls=%fused_computation.874 | convolution fusion | flops 6442450944 | bytes 16777216 | tf_op jit(solution)/shard_map/dot_general | solution.py:30
  116.8 12.0 %forward_recurrence.1 = (f32[1024,768]{1,0:T(8,128)}, bf16[1024,768]{1,0:T(8,128)(2,1)}, f32[1024,768]{1,0:T(8,128)}, f32[1024,768]{1,0:T(8,128)}, f32[1024,768]{1,0:T(8,128)}, /*index=5*/f32[1024,768]{1,0:T(8,128)}) custom-call(f32[1024,1536]{1,0:T(8,128)} %copy-done.7, f32[24,768]{1,0:T(8,128)} %maximum_bitcast_fusion.3.prev_ref, f32[1024,8]{1,0:T(8,128)} %bitcast.1894, ...), custom_call_target="tpu_custom_call" | custom-call | flops 2415919104 | bytes 23592960 | tf_op jit(solution)/shard_map/forward_recurrence/pallas_call | solution.py:123
  130.5 12.8 %all-gather = f32[16,8,768]{2,1,0:T(8,128)S(1)} all-gather(f32[2,8,768]{2,1,0:T(8,128)S(1)} %pad_maximum_fusion.73), channel_id=2, replica_groups=mesh['seq'=8,'tp'=4] {'seq'}, dimensions={0}, use_global_device_ids=true | all-gather | bytes 442368 | tf_op jit(solution)/shard_map/all_gather | solution.py:726
  163.0 16.4 %collective-permute-done.11 = bf16[1,4,88,1024]{3,2,1,0:T(8,128)(2,1)S(1)} collective-permute-done((bf16[1,4,88,1024]{3,2,1,0:T(8,128)(2,1)S(1)}, bf16[1,4,88,1024]{3,2,1,0:T(8,128)(2,1)S(1)}, u32[]{:S(2)}, u32[]{:S(2)}) %collective-permute-start.11) | collective-permute-done | bytes 720928 | tf_op jit(solution)/shard_map/ppermute | solution.py:423
  181.7 30.9 %collective-permute-done.12 = bf16[2,4,88,1024]{3,2,1,0:T(8,128)(2,1)S(1)} collective-permute-done((bf16[2,4,88,1024]{3,2,1,0:T(8,128)(2,1)S(1)}, bf16[2,4,88,1024]{3,2,1,0:T(8,128)(2,1)S(1)}, u32[]{:S(2)}, u32[]{:S(2)}) %collective-permute-start.12) | collective-permute-done | bytes 1441824 | tf_op jit(solution)/shard_map/ppermute | solution.py:423
  216.1 11.8 %mlp_weights.1 = (bf16[8,256,1536]{2,1,0:T(8,128)(2,1)}, bf16[8,256,1536]{2,1,0:T(8,128)(2,1)}, bf16[8,2,128,1536]{3,2,1,0:T(8,128)(2,1)}) custom-call(s32[8]{0:T(128)S(1)} %get-tuple-element.474.at_a.at_b, s32[8]{0:T(128)S(1)} %get-tuple-element.473.at_b.at_a, bf16[4,384,1536]{2,1,0:T(8,128)(2,1)S(1)} %constant_dynamic-update-slice_fusion.own_a_ref, ...), custom_call_target="tpu_custom_call" | custom-call | bytes 56623104 | tf_op jit(solution)/shard_map/mlp_weights/pallas_call | solution.py:488
  227.9 11.8 %fusion.403.d_hid_ref = f32[1024,1536]{1,0:T(8,128)} fusion(bf16[1024,2048]{1,0:T(8,128)(2,1)} %bitcast.1889, bf16[2048,1536]{1,0:T(8,128)(2,1)} %bitcast.1934), kind=kOutput, calls=%fused_computation.875 | convolution fusion | flops 6442450944 | bytes 16777216 | tf_op jit(solution)/shard_map/dot_general | solution.py:22
  239.7 8.7 %output_rows.1 = bf16[4,8,88,2048]{3,2,1,0:T(8,128)(2,1)} custom-call(s32[8]{0:T(128)S(1)} %get-tuple-element.474.at_a.at_b, s32[8]{0:T(128)S(1)} %get-tuple-element.473.at_b.at_a, bf16[4,4,88,1024]{3,2,1,0:T(8,128)(2,1)S(1)} %pad_maximum_fusion.own_a_ref, bf16[4,4,88,1024]{3,2,1,0:T(8,128)(2,1)} %collective-permute-done.10.far_a_ref, ...), custom_call_target="tpu_custom_call" | custom-call | bytes 34603008 | tf_op jit(solution)/shard_map/output_rows/pallas_call | solution.py:488
  248.4 9.8 %all-gather.10.cloned.1.call-done = bf16[1024,2816]{0,1:T(8,128)(2,1)} async-done(((bf16[1024,704]{0,1:T(8,128)(2,1)}), bf16[1024,2816]{0,1:T(8,128)(2,1)}) %all-gather.10.cloned.1.call-update) | async-done | bytes 5767184 | tf_op jit(solution)/shard_map/all_gather | solution.py:731
  258.2 18.7 %multiply_reduce_fusion = (f32[1024]{0:T(1024)S(1)}, f32[1024,2048]{1,0:T(8,128)S(1)}) fusion(bf16[1024,2816]{0,1:T(8,128)(2,1)} %all-gather.10.cloned.1.call-done, bf16[2816,2048]{1,0:T(8,128)(2,1)} %bitcast.1893, bf16[1024,2048]{1,0:T(8,128)(2,1)} %all-gather.6.cloned.1.call-done), kind=kOutput, calls=%fused_computation.14 | convolution fusion | flops 11819547648 | bytes 29888512 | tf_op jit(solution)/shard_map/dot_general | solution.py:22
  282.9 23.3 %mlp_units.1 = (bf16[1024,1536]{1,0:T(8,128)(2,1)S(1)}, bf16[1024,1536]{1,0:T(8,128)(2,1)}, bf16[1024,1536]{1,0:T(8,128)(2,1)}, f32[1024,128]{1,0:T(8,128)S(1)}) custom-call(bf16[1024,2048]{1,0:T(8,128)(2,1)} %multiply_convert_fusion.n2_ref, bf16[2048,1536]{1,0:T(8,128)(2,1)} %bitcast.1942, bf16[2048,1536]{1,0:T(8,128)(2,1)} %bitcast.1938, ...), custom_call_target="tpu_custom_call" | custom-call | flops 12884901888 | bytes 32505856 | tf_op jit(solution)/shard_map/mlp_units/pallas_call | solution.py:389
  306.2 13.0 %fusion.404 = f32[1024,2048]{1,0:T(8,128)} fusion(bf16[1024,1536]{1,0:T(8,128)(2,1)} %get-tuple-element.183, bf16[2048,1536]{1,0:T(8,128)(2,1)} %bitcast.1943), kind=kOutput, calls=%fused_computation.876 | convolution fusion | flops 6442450944 | bytes 17825792 | tf_op jit(solution)/shard_map/dot_general | solution.py:30
  319.2 10.4 %add_convert_fusion = bf16[1024,2048]{1,0:T(8,128)(2,1)} fusion(f32[1024,2048]{1,0:T(8,128)} %fusion.404, bf16[1024,1536]{1,0:T(8,128)(2,1)S(1)} %copy-done.110, bf16[2048,1536]{1,0:T(8,128)(2,1)S(1)} %bitcast.1941), kind=kOutput, calls=%fused_computation.12 | convolution fusion | flops 6446645248 | bytes 22020096 | tf_op jit(solution)/shard_map/dot_general | solution.py:30
  329.8 3.8 constant_dynamic-slice_fusion.49
  339.3 5.5 convolution_convert_fusion.2
  344.7 5.1 convolution_convert_fusion.3
  353.7 9.9 %psum.7 = f32[1024,1]{0,1:T(1,128)S(1)} all-reduce(f32[1024,1]{0,1:T(1,128)S(1)} %bitcast.1923), channel_id=1, replica_groups=mesh['seq'=8,'tp'=4] {'tp'}, use_global_device_ids=true, to_apply=%region_4.5 | all-reduce | flops 1024 | bytes 8192 | tf_op jit(solution)/shard_map/psum | solution.py:758
  364.8 6.3 convert_add_fusion.5
  371.1 5.1 convert_add_fusion.6
  376.3 7.2 convert_add_fusion.1
  383.5 7.1 convert_add_fusion.2
  390.6 14.6 %reduce-scatter.4.cloned.1.call-done = bf16[1024,512]{1,0:T(8,128)(2,1)} async-done(((bf16[1024,2048]{1,0:T(8,128)(2,1)}), bf16[1024,512]{1,0:T(8,128)(2,1)}) %reduce-scatter.4.cloned.1.call-update) | async-done | bytes 1048592 | tf_op jit(solution)/shard_map/reduce_scatter | solution.py:638
  428.3 4.9 multiply_reduce_fusion.1
  433.2 8.4 %convolution_convert_fusion.1 = bf16[1024,2048]{1,0:T(8,128)(2,1)} fusion(bf16[1024,1536]{1,0:T(8,128)(2,1)S(1)} %copy-done.6, bf16[2048,1536]{1,0:T(8,128)(2,1)S(1)} %bitcast.1937), kind=kOutput, calls=%fused_computation.26 | convolution fusion | flops 6444548096 | bytes 13631488 | tf_op jit(solution)/shard_map/dot_general | solution.py:30
  443.9 3.8 fusion.121
  457.6 7.9 %collective-permute-done.20 = bf16[512,1536]{1,0:T(8,128)(2,1)} collective-permute-done((bf16[512,1536]{1,0:T(8,128)(2,1)}, bf16[512,1536]{1,0:T(8,128)(2,1)}, u32[]{:S(2)}, u32[]{:S(2)}) %collective-permute-start.20) | collective-permute-done | bytes 1572896 | tf_op jit(solution)/shard_map/ppermute | solution.py:423
  472.9 17.8 %all-gather.12.cloned.1.call-done = bf16[1024,2048]{1,0:T(8,128)(2,1)} async-done(((bf16[1024,512]{1,0:T(8,128)(2,1)}), bf16[1024,2048]{1,0:T(8,128)(2,1)}) %all-gather.12.cloned.1.call-update) | async-done | bytes 4194320 | tf_op jit(solution)/shard_map/all_gather | solution.py:634
  494.9 8.2 %subtract_convert_fusion = bf16[1024,2048]{1,0:T(8,128)(2,1)S(1)} fusion(f32[1024,2048]{1,0:T(8,128)} %copy-done.9, bf16[1024,2048]{1,0:T(8,128)(2,1)} %all-gather.12.cloned.1.call-done, bf16[1024,2048]{1,0:T(8,128)(2,1)} %bitcast.1891, f32[1024]{0:T(1024)S(1)} %bitcast.1921), kind=kLoop, calls=%fused_computation.11 | loop fusion | flops 12582912 | bytes 20975616 | tf_op jit(solution)/shard_map/convert_element_type | solution.py:797
  503.1 5.2 fusion.405.dm_ref
  508.4 10.2 %reverse_recurrence.1 = (f32[1024,768]{1,0:T(8,128)}, f32[1024,768]{1,0:T(8,128)}, bf16[1024,768]{1,0:T(8,128)(2,1)}, f32[16,768]{1,0:T(8,128)}) custom-call(f32[1024,768]{1,0:T(8,128)} %fusion.405.dm_ref, f32[1024,1536]{1,0:T(8,128)} %copy-done.7, f32[1024,768]{1,0:T(8,128)} %get-tuple-element.208.r_ref, f32[1024,768]{1,0:T(8,128)} %copy-done.8, ...), custom_call_target="tpu_custom_call" | custom-call | flops 23592960 | bytes 20447232 | tf_op jit(solution)/shard_map/reverse_recurrence/pallas_call | solution.py:179
  519.8 9.8 %all_gather.27 = f32[8,2,8,768]{3,2,1,0:T(8,128)S(1)} all-gather(f32[1,2,8,768]{3,2,1,0:T(8,128)} %bitcast.1919), channel_id=1, replica_groups=mesh['seq'=8,'tp'=4] {'seq'}, dimensions={0}, use_global_device_ids=true | all-gather | bytes 442368 | tf_op jit(solution)/shard_map/all_gather | solution.py:803
  531.5 18.4 %gate_gradients.1 = (bf16[1024,1536]{1,0:T(8,128)(2,1)}, f32[32,768]{1,0:T(8,128)}, f32[24,768]{1,0:T(8,128)}, f32[64,768]{1,0:T(8,128)}, bf16[1024,1536]{1,0:T(8,128)(2,1)}) custom-call(f32[1024,768]{1,0:T(8,128)} %get-tuple-element.209.grad_ref, f32[1024,768]{1,0:T(8,128)} %get-tuple-element.210.reach_ref, f32[1024,768]{1,0:T(8,128)} %get-tuple-element.208.r_ref, ...), custom_call_target="tpu_custom_call" | custom-call | flops 2415919104 | bytes 29884416 | tf_op jit(solution)/shard_map/gate_gradients/pallas_call | solution.py:294
  556.0 11.1 %convolution_convert_fusion = bf16[1024,2048]{1,0:T(8,128)(2,1)} fusion(bf16[1024,1536]{1,0:T(8,128)(2,1)} %settle.1, bf16[1536,2048]{1,0:T(8,128)(2,1)} %fusion.7), kind=kOutput, calls=%fused_computation.25 | convolution fusion | flops 6444548096 | bytes 13631488 | tf_op jit(solution)/shard_map/dot_general | solution.py:22
  601.3 6.9 collective-permute-done.29
  608.6 4.3 convert_add_fusion.7
  619.0 12.5 %collective-permute-done.46 = bf16[704,512]{1,0:T(8,128)(2,1)S(1)} collective-permute-done((bf16[704,512]{1,0:T(8,128)(2,1)S(1)}, bf16[704,512]{1,0:T(8,128)(2,1)S(1)}, u32[]{:S(2)}, u32[]{:S(2)}) %collective-permute-start.46) | collective-permute-done | bytes 720928 | tf_op jit(solution)/shard_map/ppermute | solution.py:423
  649.1 4.1 collective-permute-done.51
  659.4 9.3 %collective-permute-done.37 = bf16[528,512]{1,0:T(8,128)(2,1)S(1)} collective-permute-done((bf16[528,512]{1,0:T(8,128)(2,1)S(1)}, bf16[528,512]{1,0:T(8,128)(2,1)S(1)}, u32[]{:S(2)}, u32[]{:S(2)}) %collective-permute-start.37) | collective-permute-done | bytes 540704 | tf_op jit(solution)/shard_map/ppermute | solution.py:423
  670.2 11.1 %collective-permute-done.52 = bf16[704,512]{1,0:T(8,128)(2,1)S(1)} collective-permute-done((bf16[704,512]{1,0:T(8,128)(2,1)S(1)}, bf16[704,512]{1,0:T(8,128)(2,1)S(1)}, u32[]{:S(2)}, u32[]{:S(2)}) %collective-permute-start.52) | collective-permute-done | bytes 720928 | tf_op jit(solution)/shard_map/ppermute | solution.py:423
  693.0 3.6 collective-permute-done.33
  699.0 5.2 collective-permute-done.34
  706.8 6.5 branch_gradients.1
  715.5 4.0 fusion.106
  727.2 6.7 other_gradients.1
  (551 shorter events, 245.8 us)
Async XLA Ops:
  7.2 86.6 %all-gather.6.cloned.1.call-start = ((), (), s32[]{:S(2)}) async-start(), calls=%async_computation.3 | async-start | bytes 5242880 | tf_op jit(solution)/shard_map/all_gather | solution.py:634
  10.2 120.4 %all-gather.8.cloned.1.call-start = ((), (), s32[]{:S(2)}) async-start(), calls=%async_computation.4 | async-start | bytes 1802240 | tf_op jit(solution)/shard_map/all_gather | solution.py:721
  10.7 29.1 %collective-permute-start.1 = (bf16[1,384,1536]{2,1,0:T(8,128)(2,1)S(1)}, bf16[1,384,1536]{2,1,0:T(8,128)(2,1)}, u32[]{:S(2)}, u32[]{:S(2)}) collective-permute-start(bf16[1,384,1536]{2,1,0:T(8,128)(2,1)S(1)} %maximum_bitcast_fusion.2), channel_id=1, source_target_pairs={{0,16},{4,20},{8,24},{12,28},{16,0},{20,4},{24,8},{28,12},{1,17},{... | collective-permute-start | bytes 3538952 | tf_op jit(solution)/shard_map/ppermute | solution.py:423
  14.9 27.8 %collective-permute-start = (bf16[1,384,1536]{2,1,0:T(8,128)(2,1)S(1)}, bf16[1,384,1536]{2,1,0:T(8,128)(2,1)}, u32[]{:S(2)}, u32[]{:S(2)}) collective-permute-start(bf16[1,384,1536]{2,1,0:T(8,128)(2,1)S(1)} %maximum_bitcast_fusion.1), channel_id=1, source_target_pairs={{0,8},{4,12},{8,0},{12,4},{16,24},{20,28},{24,16},{28,20},{1,9},{5... | collective-permute-start | bytes 3538952 | tf_op jit(solution)/shard_map/ppermute | solution.py:423
  45.0 29.6 %collective-permute-start.18 = (f32[1]{0:T(128)}, f32[1]{0:T(128)}, u32[]{:S(2)}, u32[]{:S(2)}) collective-permute-start(f32[1]{0:T(128)} %slice.1424), channel_id=1, source_target_pairs={{4,0},{8,4},{12,8},{16,12},{20,16},{24,20},{28,24},{5,1},{9,5},{13... | collective-permute-start | bytes 20 | tf_op jit(solution)/shard_map/ppermute | solution.py:412
  46.3 29.6 %collective-permute-start.2 = (f32[3]{0:T(128)S(1)}, f32[3]{0:T(128)S(1)}, u32[]{:S(2)}, u32[]{:S(2)}) collective-permute-start(f32[3]{0:T(128)S(1)} %slice.1279), channel_id=1, source_target_pairs={{0,4},{4,8},{8,12},{12,16},{16,20},{20,24},{24,28},{1,5},{5,9},{9,... | collective-permute-start | bytes 44 | tf_op jit(solution)/shard_map/ppermute | solution.py:412
  53.7 61.7 %collective-permute-start.3 = (bf16[2,384,1536]{2,1,0:T(8,128)(2,1)S(1)}, bf16[2,384,1536]{2,1,0:T(8,128)(2,1)}, u32[]{:S(2)}, u32[]{:S(2)}) collective-permute-start(bf16[2,384,1536]{2,1,0:T(8,128)(2,1)S(1)} %pad_maximum_fusion.26), channel_id=1, source_target_pairs={{0,16},{4,20},{8,24},{12,28},{16,0},{20,4},{24,8},{28,12},{1,17},{... | collective-permute-start | bytes 7077896 | tf_op jit(solution)/shard_map/ppermute | solution.py:423
  55.4 59.9 %collective-permute-start.4 = (bf16[2,384,1536]{2,1,0:T(8,128)(2,1)}, bf16[2,384,1536]{2,1,0:T(8,128)(2,1)}, u32[]{:S(2)}, u32[]{:S(2)}) collective-permute-start(bf16[2,384,1536]{2,1,0:T(8,128)(2,1)} %pad_maximum_fusion.27), channel_id=1, source_target_pairs={{0,8},{4,12},{8,0},{12,4},{16,24},{20,28},{24,16},{28,20},{1,9},{5... | collective-permute-start | bytes 7077896 | tf_op jit(solution)/shard_map/ppermute | solution.py:423
  96.9 161.3 %all-gather.10.cloned.1.call-start = ((), (), s32[]{:S(2)}) async-start(), calls=%async_computation.5 | async-start | bytes 7208960 | tf_op jit(solution)/shard_map/all_gather | solution.py:731
  153.8 251.4 %reduce-scatter.4.cloned.1.call-start = ((), (), s32[]{:S(2)}) async-start(), calls=%async_computation.6 | async-start | bytes 5242880 | tf_op jit(solution)/shard_map/reduce_scatter | solution.py:638
  157.6 56.2 %collective-permute-start.7 = (bf16[4,384,1536]{2,1,0:T(8,128)(2,1)S(1)}, bf16[4,384,1536]{2,1,0:T(8,128)(2,1)S(1)}, u32[]{:S(2)}, u32[]{:S(2)}) collective-permute-start(bf16[4,384,1536]{2,1,0:T(8,128)(2,1)S(1)} %constant_dynamic-update-slice_fusion.2.own_b_ref), channel_id=1, source_target_pairs={{0,4},{4,0},{8,12},{12,8},{16,20},{20,16},{24,28},{28,24},{1,5},{5... | collective-permute-start | bytes 14155784 | tf_op jit(solution)/shard_map/ppermute | solution.py:423
  160.5 53.4 %collective-permute-start.6 = (bf16[4,384,1536]{2,1,0:T(8,128)(2,1)S(1)}, bf16[4,384,1536]{2,1,0:T(8,128)(2,1)S(1)}, u32[]{:S(2)}, u32[]{:S(2)}) collective-permute-start(bf16[4,384,1536]{2,1,0:T(8,128)(2,1)S(1)} %constant_dynamic-update-slice_fusion.own_a_ref), channel_id=1, source_target_pairs={{0,4},{4,0},{8,12},{12,8},{16,20},{20,16},{24,28},{28,24},{1,5},{5... | collective-permute-start | bytes 14155784 | tf_op jit(solution)/shard_map/ppermute | solution.py:423
  161.1 18.3 %collective-permute-start.11 = (bf16[1,4,88,1024]{3,2,1,0:T(8,128)(2,1)S(1)}, bf16[1,4,88,1024]{3,2,1,0:T(8,128)(2,1)S(1)}, u32[]{:S(2)}, u32[]{:S(2)}) collective-permute-start(bf16[1,4,88,1024]{3,2,1,0:T(8,128)(2,1)S(1)} %get-tuple-element.418), channel_id=1, source_target_pairs={{0,16},{4,20},{8,24},{12,28},{16,0},{20,4},{24,8},{28,12},{1,17},{... | collective-permute-start | bytes 2162696 | tf_op jit(solution)/shard_map/ppermute | solution.py:423
  161.6 18.5 %collective-permute-start.8 = (bf16[1,4,88,1024]{3,2,1,0:T(8,128)(2,1)S(1)}, bf16[1,4,88,1024]{3,2,1,0:T(8,128)(2,1)S(1)}, u32[]{:S(2)}, u32[]{:S(2)}) collective-permute-start(bf16[1,4,88,1024]{3,2,1,0:T(8,128)(2,1)S(1)} %get-tuple-element.419), channel_id=1, source_target_pairs={{0,8},{4,12},{8,0},{12,4},{16,24},{20,28},{24,16},{28,20},{1,9},{5... | collective-permute-start | bytes 2162696 | tf_op jit(solution)/shard_map/ppermute | solution.py:423
  179.5 33.1 %collective-permute-start.12 = (bf16[2,4,88,1024]{3,2,1,0:T(8,128)(2,1)S(1)}, bf16[2,4,88,1024]{3,2,1,0:T(8,128)(2,1)S(1)}, u32[]{:S(2)}, u32[]{:S(2)}) collective-permute-start(bf16[2,4,88,1024]{3,2,1,0:T(8,128)(2,1)S(1)} %pad_maximum_fusion.53), channel_id=1, source_target_pairs={{0,8},{4,12},{8,0},{12,4},{16,24},{20,28},{24,16},{28,20},{1,9},{5... | collective-permute-start | bytes 4325384 | tf_op jit(solution)/shard_map/ppermute | solution.py:423
  180.2 32.8 %collective-permute-start.9 = (bf16[2,4,88,1024]{3,2,1,0:T(8,128)(2,1)S(1)}, bf16[2,4,88,1024]{3,2,1,0:T(8,128)(2,1)S(1)}, u32[]{:S(2)}, u32[]{:S(2)}) collective-permute-start(bf16[2,4,88,1024]{3,2,1,0:T(8,128)(2,1)S(1)} %pad_maximum_fusion.52), channel_id=1, source_target_pairs={{0,16},{4,20},{8,24},{12,28},{16,0},{20,4},{24,8},{28,12},{1,17},{... | collective-permute-start | bytes 4325384 | tf_op jit(solution)/shard_map/ppermute | solution.py:423
  212.9 26.7 %collective-permute-start.13 = (bf16[4,4,88,1024]{3,2,1,0:T(8,128)(2,1)S(1)}, bf16[4,4,88,1024]{3,2,1,0:T(8,128)(2,1)S(1)}, u32[]{:S(2)}, u32[]{:S(2)}) collective-permute-start(bf16[4,4,88,1024]{3,2,1,0:T(8,128)(2,1)S(1)} %pad_maximum_fusion.1.own_b_ref), channel_id=1, source_target_pairs={{0,4},{4,0},{8,12},{12,8},{16,20},{20,16},{24,28},{28,24},{1,5},{5... | collective-permute-start | bytes 8650760 | tf_op jit(solution)/shard_map/ppermute | solution.py:423
  213.3 26.3 %collective-permute-start.10 = (bf16[4,4,88,1024]{3,2,1,0:T(8,128)(2,1)S(1)}, bf16[4,4,88,1024]{3,2,1,0:T(8,128)(2,1)}, u32[]{:S(2)}, u32[]{:S(2)}) collective-permute-start(bf16[4,4,88,1024]{3,2,1,0:T(8,128)(2,1)S(1)} %pad_maximum_fusion.own_a_ref), channel_id=1, source_target_pairs={{0,4},{4,0},{8,12},{12,8},{16,20},{20,16},{24,28},{28,24},{1,5},{5... | collective-permute-start | bytes 8650760 | tf_op jit(solution)/shard_map/ppermute | solution.py:423
  329.7 161.0 %all-gather.12.cloned.1.call-start = ((), (), s32[]{:S(2)}) async-start(), calls=%async_computation.7 | async-start | bytes 5242880 | tf_op jit(solution)/shard_map/all_gather | solution.py:634
  336.6 27.0 %collective-permute-start.17 = (bf16[1024,768]{1,0:T(8,128)(2,1)}, bf16[1024,768]{1,0:T(8,128)(2,1)S(1)}, u32[]{:S(2)}, u32[]{:S(2)}) collective-permute-start(bf16[1024,768]{1,0:T(8,128)(2,1)} %fusion.78), channel_id=1, source_target_pairs={{0,4},{4,0},{8,12},{12,8},{16,20},{20,16},{24,28},{28,24},{1,5},{5... | collective-permute-start | bytes 4718600 | tf_op jit(solution)/shard_map/ppermute | solution.py:423
  344.7 31.5 %collective-permute-start.15 = (bf16[1024,1536]{1,0:T(8,128)(2,1)}, bf16[1024,1536]{1,0:T(8,128)(2,1)}, u32[]{:S(2)}, u32[]{:S(2)}) collective-permute-start(bf16[1024,1536]{1,0:T(8,128)(2,1)} %convolution_convert_fusion.2), channel_id=1, source_target_pairs={{0,4},{4,0},{8,12},{12,8},{16,20},{20,16},{24,28},{28,24},{1,5},{5... | collective-permute-start | bytes 9437192 | tf_op jit(solution)/shard_map/ppermute | solution.py:423
  349.8 33.7 %collective-permute-start.14 = (bf16[1024,1536]{1,0:T(8,128)(2,1)}, bf16[1024,1536]{1,0:T(8,128)(2,1)}, u32[]{:S(2)}, u32[]{:S(2)}) collective-permute-start(bf16[1024,1536]{1,0:T(8,128)(2,1)} %convolution_convert_fusion.3), channel_id=1, source_target_pairs={{0,4},{4,0},{8,12},{12,8},{16,20},{20,16},{24,28},{28,24},{1,5},{5... | collective-permute-start | bytes 9437192 | tf_op jit(solution)/shard_map/ppermute | solution.py:423
  353.4 17.6 %collective-permute-start.16 = (bf16[1024,768]{1,0:T(8,128)(2,1)}, bf16[1024,768]{1,0:T(8,128)(2,1)}, u32[]{:S(2)}, u32[]{:S(2)}) collective-permute-start(bf16[1024,768]{1,0:T(8,128)(2,1)} %fusion.79), channel_id=1, source_target_pairs={{0,4},{4,0},{8,12},{12,8},{16,20},{20,16},{24,28},{28,24},{1,5},{5... | collective-permute-start | bytes 4718600 | tf_op jit(solution)/shard_map/ppermute | solution.py:423
  409.3 159.6 %reduce-scatter.6.cloned.1.call-start = ((), (), s32[]{:S(2)}) async-start(), calls=%async_computation.8 | async-start | bytes 5242880 | tf_op jit(solution)/shard_map/reduce_scatter | solution.py:794
  412.1 40.3 %collective-permute-start.22 = (bf16[512,768]{1,0:T(8,128)(2,1)}, bf16[512,768]{1,0:T(8,128)(2,1)}, u32[]{:S(2)}, u32[]{:S(2)}) collective-permute-start(bf16[512,768]{1,0:T(8,128)(2,1)} %slice.3181), channel_id=1, source_target_pairs={{0,16},{4,20},{8,24},{12,28},{16,0},{20,4},{24,8},{28,12},{1,17},{... | collective-permute-start | bytes 2359304 | tf_op jit(solution)/shard_map/ppermute | solution.py:423
  416.0 38.6 %collective-permute-start.21 = (bf16[512,768]{1,0:T(8,128)(2,1)}, bf16[512,768]{1,0:T(8,128)(2,1)}, u32[]{:S(2)}, u32[]{:S(2)}) collective-permute-start(bf16[512,768]{1,0:T(8,128)(2,1)} %slice.3182), channel_id=1, source_target_pairs={{0,8},{4,12},{8,0},{12,4},{16,24},{20,28},{24,16},{28,20},{1,9},{5... | collective-permute-start | bytes 2359304 | tf_op jit(solution)/shard_map/ppermute | solution.py:423
  421.1 44.4 %collective-permute-start.20 = (bf16[512,1536]{1,0:T(8,128)(2,1)}, bf16[512,1536]{1,0:T(8,128)(2,1)}, u32[]{:S(2)}, u32[]{:S(2)}) collective-permute-start(bf16[512,1536]{1,0:T(8,128)(2,1)} %slice.3179), channel_id=1, source_target_pairs={{0,16},{4,20},{8,24},{12,28},{16,0},{20,4},{24,8},{28,12},{1,17},{... | collective-permute-start | bytes 4718600 | tf_op jit(solution)/shard_map/ppermute | solution.py:423
  424.8 44.3 %collective-permute-start.19 = (bf16[512,1536]{1,0:T(8,128)(2,1)}, bf16[512,1536]{1,0:T(8,128)(2,1)}, u32[]{:S(2)}, u32[]{:S(2)}) collective-permute-start(bf16[512,1536]{1,0:T(8,128)(2,1)} %slice.3180), channel_id=1, source_target_pairs={{0,8},{4,12},{8,0},{12,4},{16,24},{20,28},{24,16},{28,20},{1,9},{5... | collective-permute-start | bytes 4718600 | tf_op jit(solution)/shard_map/ppermute | solution.py:423
  490.7 222.7 %reduce-scatter.8.cloned.1.call-start = ((), (), s32[]{:S(2)}) async-start(), calls=%async_computation.9 | async-start | bytes 5242880 | tf_op jit(solution)/shard_map/reduce_scatter | solution.py:638
  490.8 29.0 %collective-permute-start.23 = (bf16[256,1536]{1,0:T(8,128)(2,1)S(1)}, bf16[256,1536]{1,0:T(8,128)(2,1)S(1)}, u32[]{:S(2)}, u32[]{:S(2)}) collective-permute-start(bf16[256,1536]{1,0:T(8,128)(2,1)S(1)} %slice.3184), channel_id=1, source_target_pairs={{0,16},{4,20},{8,24},{12,28},{16,0},{20,4},{24,8},{28,12},{1,17},{... | collective-permute-start | bytes 2359304 | tf_op jit(solution)/shard_map/ppermute | solution.py:423
  492.3 27.4 %collective-permute-start.24 = (bf16[256,1536]{1,0:T(8,128)(2,1)S(1)}, bf16[256,1536]{1,0:T(8,128)(2,1)S(1)}, u32[]{:S(2)}, u32[]{:S(2)}) collective-permute-start(bf16[256,1536]{1,0:T(8,128)(2,1)S(1)} %slice.3183), channel_id=1, source_target_pairs={{0,8},{4,12},{8,0},{12,4},{16,24},{20,28},{24,16},{28,20},{1,9},{5... | collective-permute-start | bytes 2359304 | tf_op jit(solution)/shard_map/ppermute | solution.py:423
  493.8 24.9 %collective-permute-start.25 = (bf16[256,768]{1,0:T(8,128)(2,1)S(1)}, bf16[256,768]{1,0:T(8,128)(2,1)S(1)}, u32[]{:S(2)}, u32[]{:S(2)}) collective-permute-start(bf16[256,768]{1,0:T(8,128)(2,1)S(1)} %slice.3188), channel_id=1, source_target_pairs={{0,16},{4,20},{8,24},{12,28},{16,0},{20,4},{24,8},{28,12},{1,17},{... | collective-permute-start | bytes 1179656 | tf_op jit(solution)/shard_map/ppermute | solution.py:423
  494.3 25.4 %collective-permute-start.26 = (bf16[256,768]{1,0:T(8,128)(2,1)S(1)}, bf16[256,768]{1,0:T(8,128)(2,1)S(1)}, u32[]{:S(2)}, u32[]{:S(2)}) collective-permute-start(bf16[256,768]{1,0:T(8,128)(2,1)S(1)} %slice.3187), channel_id=1, source_target_pairs={{0,8},{4,12},{8,0},{12,4},{16,24},{20,28},{24,16},{28,20},{1,9},{5... | collective-permute-start | bytes 1179656 | tf_op jit(solution)/shard_map/ppermute | solution.py:423
  578.1 30.5 %collective-permute-start.45 = (bf16[704,1024]{1,0:T(8,128)(2,1)}, bf16[704,1024]{1,0:T(8,128)(2,1)}, u32[]{:S(2)}, u32[]{:S(2)}) collective-permute-start(bf16[704,1024]{1,0:T(8,128)(2,1)} %fusion.87), channel_id=1, source_target_pairs={{0,4},{4,0},{8,12},{12,8},{16,20},{20,16},{24,28},{28,24},{1,5},{5... | collective-permute-start | bytes 4325384 | tf_op jit(solution)/shard_map/ppermute | solution.py:423
  580.7 33.7 %collective-permute-start.42 = (bf16[704,1024]{1,0:T(8,128)(2,1)}, bf16[704,1024]{1,0:T(8,128)(2,1)}, u32[]{:S(2)}, u32[]{:S(2)}) collective-permute-start(bf16[704,1024]{1,0:T(8,128)(2,1)} %fusion.84), channel_id=1, source_target_pairs={{0,4},{4,0},{8,12},{12,8},{16,20},{20,16},{24,28},{28,24},{1,5},{5... | collective-permute-start | bytes 4325384 | tf_op jit(solution)/shard_map/ppermute | solution.py:423
  583.3 16.0 %collective-permute-start.28 = (f32[5120]{0:T(1024)S(1)}, f32[5120]{0:T(1024)}, u32[]{:S(2)}, u32[]{:S(2)}) collective-permute-start(f32[5120]{0:T(1024)S(1)} %pad_maximum_fusion.74), channel_id=1, source_target_pairs={{0,1},{1,0},{2,3},{3,2},{4,5},{5,4},{6,7},{7,6},{8,9},{9,8},{10,11... | collective-permute-start | bytes 61448 | tf_op jit(solution)/shard_map/ppermute | solution.py:423
  596.7 41.0 %collective-permute-start.36 = (bf16[528,1024]{1,0:T(8,128)(2,1)}, bf16[528,1024]{1,0:T(8,128)(2,1)}, u32[]{:S(2)}, u32[]{:S(2)}) collective-permute-start(bf16[528,1024]{1,0:T(8,128)(2,1)} %maximum_maximum_fusion), channel_id=1, source_target_pairs={{0,4},{4,0},{8,12},{12,8},{16,20},{20,16},{24,28},{28,24},{1,5},{5... | collective-permute-start | bytes 3244040 | tf_op jit(solution)/shard_map/ppermute | solution.py:423
  613.0 18.5 %collective-permute-start.46 = (bf16[704,512]{1,0:T(8,128)(2,1)S(1)}, bf16[704,512]{1,0:T(8,128)(2,1)S(1)}, u32[]{:S(2)}, u32[]{:S(2)}) collective-permute-start(bf16[704,512]{1,0:T(8,128)(2,1)S(1)} %slice.3185), channel_id=1, source_target_pairs={{0,16},{4,20},{8,24},{12,28},{16,0},{20,4},{24,8},{28,12},{1,17},{... | collective-permute-start | bytes 2162696 | tf_op jit(solution)/shard_map/ppermute | solution.py:423
  617.5 19.1 %collective-permute-start.43 = (bf16[704,512]{1,0:T(8,128)(2,1)S(1)}, bf16[704,512]{1,0:T(8,128)(2,1)S(1)}, u32[]{:S(2)}, u32[]{:S(2)}) collective-permute-start(bf16[704,512]{1,0:T(8,128)(2,1)S(1)} %slice.3186), channel_id=1, source_target_pairs={{0,8},{4,12},{8,0},{12,4},{16,24},{20,28},{24,16},{28,20},{1,9},{5... | collective-permute-start | bytes 2162696 | tf_op jit(solution)/shard_map/ppermute | solution.py:423
  648.0 20.7 %collective-permute-start.37 = (bf16[528,512]{1,0:T(8,128)(2,1)S(1)}, bf16[528,512]{1,0:T(8,128)(2,1)S(1)}, u32[]{:S(2)}, u32[]{:S(2)}) collective-permute-start(bf16[528,512]{1,0:T(8,128)(2,1)S(1)} %fusion.104), channel_id=1, source_target_pairs={{0,16},{4,20},{8,24},{12,28},{16,0},{20,4},{24,8},{28,12},{1,17},{... | collective-permute-start | bytes 1622024 | tf_op jit(solution)/shard_map/ppermute | solution.py:423
  653.2 28.1 %collective-permute-start.52 = (bf16[704,512]{1,0:T(8,128)(2,1)S(1)}, bf16[704,512]{1,0:T(8,128)(2,1)S(1)}, u32[]{:S(2)}, u32[]{:S(2)}) collective-permute-start(bf16[704,512]{1,0:T(8,128)(2,1)S(1)} %pad_maximum_fusion.65), channel_id=1, source_target_pairs={{0,16},{4,20},{8,24},{12,28},{16,0},{20,4},{24,8},{28,12},{1,17},{... | collective-permute-start | bytes 2162696 | tf_op jit(solution)/shard_map/ppermute | solution.py:423
  657.2 24.4 %collective-permute-start.49 = (bf16[704,512]{1,0:T(8,128)(2,1)S(1)}, bf16[704,512]{1,0:T(8,128)(2,1)S(1)}, u32[]{:S(2)}, u32[]{:S(2)}) collective-permute-start(bf16[704,512]{1,0:T(8,128)(2,1)S(1)} %pad_maximum_fusion.64), channel_id=1, source_target_pairs={{0,8},{4,12},{8,0},{12,4},{16,24},{20,28},{24,16},{28,20},{1,9},{5... | collective-permute-start | bytes 2162696 | tf_op jit(solution)/shard_map/ppermute | solution.py:423
  658.5 23.8 %collective-permute-start.31 = (bf16[360,512]{1,0:T(8,128)(2,1)S(1)}, bf16[360,512]{1,0:T(8,128)(2,1)S(1)}, u32[]{:S(2)}, u32[]{:S(2)}) collective-permute-start(bf16[360,512]{1,0:T(8,128)(2,1)S(1)} %fusion.109), channel_id=1, source_target_pairs={{0,8},{4,12},{8,0},{12,4},{16,24},{20,28},{24,16},{28,20},{1,9},{5... | collective-permute-start | bytes 1105928 | tf_op jit(solution)/shard_map/ppermute | solution.py:423
  669.0 15.4 %collective-permute-start.38 = (bf16[528,256]{1,0:T(8,128)(2,1)S(1)}, bf16[528,256]{1,0:T(8,128)(2,1)S(1)}, u32[]{:S(2)}, u32[]{:S(2)}) collective-permute-start(bf16[528,256]{1,0:T(8,128)(2,1)S(1)} %slice.3191), channel_id=1, source_target_pairs={{0,8},{4,12},{8,0},{12,4},{16,24},{20,28},{24,16},{28,20},{1,9},{5... | collective-permute-start | bytes 811016 | tf_op jit(solution)/shard_map/ppermute | solution.py:423
  681.5 25.3 %collective-permute-start.53 = (bf16[704,1024]{1,0:T(8,128)(2,1)S(1)}, bf16[704,1024]{1,0:T(8,128)(2,1)S(1)}, u32[]{:S(2)}, u32[]{:S(2)}) collective-permute-start(bf16[704,1024]{1,0:T(8,128)(2,1)S(1)} %pad_maximum_fusion.55.own_b_ref), channel_id=1, source_target_pairs={{0,4},{4,0},{8,12},{12,8},{16,20},{20,16},{24,28},{28,24},{1,5},{5... | collective-permute-start | bytes 4325384 | tf_op jit(solution)/shard_map/ppermute | solution.py:423
  681.8 25.0 %collective-permute-start.50 = (bf16[704,1024]{1,0:T(8,128)(2,1)S(1)}, bf16[704,1024]{1,0:T(8,128)(2,1)S(1)}, u32[]{:S(2)}, u32[]{:S(2)}) collective-permute-start(bf16[704,1024]{1,0:T(8,128)(2,1)S(1)} %pad_maximum_fusion.54.own_a_ref), channel_id=1, source_target_pairs={{0,4},{4,0},{8,12},{12,8},{16,20},{20,16},{24,28},{28,24},{1,5},{5... | collective-permute-start | bytes 4325384 | tf_op jit(solution)/shard_map/ppermute | solution.py:423
  704.3 22.9 %collective-permute-start.35 = (bf16[360,1024]{1,0:T(8,128)(2,1)S(1)}, bf16[360,1024]{1,0:T(8,128)(2,1)}, u32[]{:S(2)}, u32[]{:S(2)}) collective-permute-start(bf16[360,1024]{1,0:T(8,128)(2,1)S(1)} %pad_maximum_fusion.63.own_a_ref), channel_id=1, source_target_pairs={{0,4},{4,0},{8,12},{12,8},{16,20},{20,16},{24,28},{28,24},{1,5},{5... | collective-permute-start | bytes 2211848 | tf_op jit(solution)/shard_map/ppermute | solution.py:423
  706.7 20.5 %collective-permute-start.41 = (bf16[528,1024]{1,0:T(8,128)(2,1)S(1)}, bf16[528,1024]{1,0:T(8,128)(2,1)S(1)}, u32[]{:S(2)}, u32[]{:S(2)}) collective-permute-start(bf16[528,1024]{1,0:T(8,128)(2,1)S(1)} %pad_maximum_fusion.61.own_b_ref), channel_id=1, source_target_pairs={{0,4},{4,0},{8,12},{12,8},{16,20},{20,16},{24,28},{28,24},{1,5},{5... | collective-permute-start | bytes 3244040 | tf_op jit(solution)/shard_map/ppermute | solution.py:423
  (140 other events, 1030.7 us)
Sparse Core Ops, SparseCore 0:
  10.3 83.4 all-gather.5
  97.0 33.4 all-gather.7
  153.9 104.2 all-gather.9
  329.8 75.3 reduce-scatter.3
  409.4 81.2 all-gather.11
  493.5 75.2 reduce-scatter.5
  571.1 78.1 reduce-scatter.7

commit v3 on v2

--- a/solution.py
+++ b/solution.py
@@ -143,20 +143,27 @@
 
 
 def reverse_kernel(
-    dm_ref, by_ref, r_ref, state_ref, mask_ref, par_ref,
-    grad_ref, reach_ref, dby_ref, head_ref,
-    slopes,
+    grad_in_ref, scaled_ref, n2_ref, factor_ref, gain_ref, weight_ref, by_ref, r_ref, state_ref,
+    mask_ref, par_ref,
+    resid_ref, grad_ref, reach_ref, dby_ref, head_ref,
+    dm, slopes,
 ):
-    width = dm_ref.shape[1]
+    width = by_ref.shape[1]
 
     @pl.when(pl.program_id(0) == 0)
     def _():
         head_ref[at(0), :] = jnp.zeros((8, width), F32)
         head_ref[at(1), :] = jnp.ones((8, width), F32)
 
+    centred = (n2_ref[...].astype(F32) * gain_ref[...]) * factor_ref[...]
+    d_resid = grad_in_ref[...].astype(F32) + scaled_ref[...].astype(F32) - centred
+    d_resid = d_resid.astype(BF16)
+    resid_ref[...] = d_resid
+    dm[...] = contract_last(d_resid, weight_ref[...])
+
     u, reach = head_ref[at(0), :], head_ref[at(1), :]
     for j in range(STEPS - 1, -1, -1):
-        d = dm_ref[at(j), :]
+        d = dm[at(j), :]
         act, slope = gelu_parts(by_ref[at(j), :])
         slopes[at(j), :] = slope * (state_ref[at(j), :] * d)
         live = jnp.broadcast_to(mask_ref[at(j), :][:, 1:2], u.shape) != 0.0
@@ -171,31 +178,38 @@
     dby_ref[...] = slopes[...].astype(BF16)
 
 
-def reverse_recurrence(dm, both, r, state, masks, params):
-    tokens, width = dm.shape
+def reverse_recurrence(grad_rows, scaled, n2, factor, gain, weight, both, r, state, masks, params):
+    tokens, full = grad_rows.shape
+    width = weight.shape[0]
     tiles = tokens // ROWS
     wide = wide_block(width, tiles)
-    shape = lambda d: jax.ShapeDtypeStruct(dm.shape, d)
+    whole_row = wide_block(full, tiles)
+    shape = lambda n, d: jax.ShapeDtypeStruct((tokens, n), d)
     return pl.pallas_call(
         reverse_kernel,
         name="reverse_recurrence",
         grid=(tiles,),
         in_specs=[
-            wide, wide_block(width, tiles, 1), wide, wide, wide_block(8, tiles), whole(params),
+            whole_row, whole_row, whole_row, wide_block(1, tiles), whole(gain), whole(weight),
+            wide_block(width, tiles, 1), wide, wide, wide_block(8, tiles), whole(params),
         ],
-        out_specs=[wide, wide, wide, fixed(16, width)],
-        out_shape=[shape(F32), shape(F32), shape(BF16), jax.ShapeDtypeStruct((16, width), F32)],
-        scratch_shapes=[pltpu.VMEM((ROWS, width), F32)],
+        out_specs=[whole_row, wide, wide, wide, fixed(16, width)],
+        out_shape=[
+            shape(full, BF16), shape(width, F32), shape(width, F32), shape(width, BF16),
+            jax.ShapeDtypeStruct((16, width), F32),
+        ],
+        scratch_shapes=[pltpu.VMEM((ROWS, width), F32), pltpu.VMEM((ROWS, width), F32)],
         compiler_params=tile_params(),
         cost_estimate=pl.CostEstimate(
-            flops=30 * dm.size, bytes_accessed=26 * dm.size, transcendentals=2 * dm.size
-        ),
-    )(dm, both, r, state, masks, params)
+            flops=2 * tokens * width * full, bytes_accessed=tokens * (8 * full + 24 * width),
+            transcendentals=2 * tokens * width,
+        ),
+    )(grad_rows, scaled, n2, factor, gain, weight, both, r, state, masks, params)
 
 
 def gate_grad_kernel(
     grad_ref, reach_ref, r_ref, i_ref, conv_ref, state_ref, before_ref, bx_ref, bx_before_ref,
-    mask_ref, dby_ref, prev_ref, ends_ref, par_ref, gates_ref,
+    mask_ref, prev_ref, ends_ref, par_ref, gates_ref,
     out_ref, tail_ref, edge_ref, sums_ref, both_ref,
     pair, direct, ahead,
 ):
@@ -276,15 +290,14 @@
         sums_ref[at(3 + n), :] += total
     for k, p in enumerate((p1, p2, p3)):
         edge_ref[at(k), :] = p
-    out_ref[:, pl.ds(0, width)] = direct[...].astype(BF16)
-    out_ref[:, pl.ds(width, width)] = dby_ref[...]
+    out_ref[...] = direct[...].astype(BF16)
 
     @pl.when(step_at == 0)
     def _():
         tail_ref[...] = direct[pl.ds(ROWS - 32, 32), :]
 
 
-def gate_gradients(grad, reach, r, i, conv, state, both, masks, dby, prev, ends, params, gates):
+def gate_gradients(grad, reach, r, i, conv, state, both, masks, prev, ends, params, gates):
     tokens, width = grad.shape
     tiles = tokens // ROWS
     wide = wide_block(width, tiles)
@@ -297,14 +310,13 @@
         grid=(tiles,),
         in_specs=[
             wide, wide, wide, wide, wide, wide, ahead(8), wide, ahead(32), wide_block(8, tiles),
-            wide, whole(prev), whole(ends), whole(params), whole(gates),
+            whole(prev), whole(ends), whole(params), whole(gates),
         ],
         out_specs=[
-            wide_block(2 * width, tiles), fixed(32, width), fixed(24, width), fixed(64, width),
-            wide_block(2 * width, tiles),
+            wide, fixed(32, width), fixed(24, width), fixed(64, width), wide_block(2 * width, tiles),
         ],
         out_shape=[
-            jax.ShapeDtypeStruct((tokens, 2 * width), BF16),
+            jax.ShapeDtypeStruct((tokens, width), BF16),
             jax.ShapeDtypeStruct((32, width), F32),
             jax.ShapeDtypeStruct((24, width), F32),
             jax.ShapeDtypeStruct((64, width), F32),
@@ -317,10 +329,10 @@
         ],
         compiler_params=tile_params(),
         cost_estimate=pl.CostEstimate(
-            flops=4 * grad.size * width, bytes_accessed=38 * grad.size,
+            flops=4 * grad.size * width, bytes_accessed=34 * grad.size,
             transcendentals=2 * grad.size,
         ),
-    )(grad, reach, r, i, conv, state, state, both, both, masks, dby, prev, ends, params, gates)
+    )(grad, reach, r, i, conv, state, state, both, both, masks, prev, ends, params, gates)
 
 
 def settle_kernel(main_ref, tail_ref, edge_ref, beyond_ref, out_ref):
@@ -406,6 +418,33 @@
     )(n2, gate_weight, up_weight, d_hid)
 
 
+def pair_kernel(left_ref, right_ref, over_ref, under_ref, out_ref):
+    out_ref[...] = (dot(left_ref[...], over_ref[...]) + dot(right_ref[...], under_ref[...])).astype(BF16)
+
+
+def pair_product(left, right, over, under):
+    tokens, depth = left.shape
+    width = over.shape[1]
+    rows = min(256, tokens)
+    tall = lambda n: pl.BlockSpec((rows, n), lambda t: (t, 0))
+    held = lambda a: pl.BlockSpec(a.shape, lambda t: (0, 0), pipeline_mode=pl.Buffered(1))
+    return pl.pallas_call(
+        pair_kernel,
+        name="pair_product",
+        grid=(tokens // rows,),
+        in_specs=[tall(depth), tall(depth), held(over), held(under)],
+        out_specs=tall(width),
+        out_shape=jax.ShapeDtypeStruct((tokens, width), BF16),
+        compiler_params=pltpu.CompilerParams(
+            dimension_semantics=("arbitrary",), vmem_limit_bytes=32 << 20
+        ),
+        cost_estimate=pl.CostEstimate(
+            flops=4 * tokens * depth * width, transcendentals=0,
+            bytes_accessed=2 * (tokens * (2 * depth + width) + 2 * depth * width),
+        ),
+    )(left, right, over, under)
+
+
 def shifted(x, axis, by):
     peers = lax.axis_size(axis)
     pairs = [(i, i + by) for i in range(peers) if 0 <= i + by < peers]
@@ -460,22 +499,24 @@
     return sum(((away >> bit) & 1) << (bits - 1 - k) for k, bit in enumerate(order))
 
 
-def picked(own_a, far_a, own_b, far_b, tables, fill, outs, name):
+def picked(routes, tables, fill, outs, name):
     n = lax.axis_size("seq")
     half = n // 2
-
-    def kernel(at_a, at_b, own_a_ref, far_a_ref, own_b_ref, far_b_ref, *refs):
+    count = len(routes)
+
+    def kernel(*refs):
         step_at = pl.program_id(0)
-        for at, side, own, far in ((at_a, 0, own_a_ref, far_a_ref), (at_b, 1, own_b_ref, far_b_ref)):
-            near = at[step_at] < half
+        sources, results = refs[count : 3 * count], refs[3 * count :]
+        for side in range(count):
+            near = refs[side][step_at] < half
 
             @pl.when(near)
             def _():
-                fill(side, own, refs)
+                fill(side, sources[2 * side], results)
 
             @pl.when(jnp.logical_not(near))
             def _():
-                fill(side, far, refs)
+                fill(side, sources[2 * side + 1], results)
 
     def pick(array, which, far):
         def block(s, *at):
@@ -484,16 +525,16 @@
 
         return pl.BlockSpec(array[1], block)
 
-    arrays = (own_a, far_a, own_b, far_b)
     return pl.pallas_call(
         kernel,
         name=name,
         grid_spec=pltpu.PrefetchScalarGridSpec(
-            num_scalar_prefetch=2,
+            num_scalar_prefetch=count,
             grid=(n,),
             in_specs=[
-                pick(own_a, 0, False), pick(far_a, 0, True), pick(own_b, 1, False),
-                pick(far_b, 1, True),
+                pick(array, side, far)
+                for side, route in enumerate(routes)
+                for far, array in enumerate(route)
             ],
             out_specs=[pl.BlockSpec(block, at) for _, block, at in outs],
         ),
@@ -503,14 +544,15 @@
         ),
         cost_estimate=pl.CostEstimate(
             flops=0, transcendentals=0,
-            bytes_accessed=sum(a[0].size * 2 for a in arrays) + sum(o[0].size * 4 for o in outs),
-        ),
-    )(*tables, *(a[0] for a in arrays))
-
-
-def ordered(own_a, far_a, own_b, far_b, tables, outputs, name):
+            bytes_accessed=sum(a[0].size * 2 for r in routes for a in r)
+            + sum(o[0].size * 4 for o in outs),
+        ),
+    )(*tables, *(a[0] for r in routes for a in r))
+
+
+def ordered(routes, tables, outputs, name):
     n = lax.axis_size("seq")
-    each = own_a.shape[1] // (n // 2)
+    each = routes[0][0].shape[1] // (n // 2)
     wrap = lambda a: (a, (a.shape[0], each), lambda place: (0, place))
 
     def fill(side, ref, refs):
@@ -521,12 +563,12 @@
                     out[pl.ds(row, rows), :] = ref[pl.ds(start, rows), :].astype(F32)
                 row += rows
 
-    heights = [sum(rows for _, _, rows in pieces) for pieces in outputs]
-    outs = [
-        (jax.ShapeDtypeStruct((h, n * each), F32), (h, each), lambda s, *at: (0, s))
-        for h in heights
-    ]
-    return picked(wrap(own_a), wrap(far_a), wrap(own_b), wrap(far_b), tables, fill, outs, name)
+    outs = []
+    for pieces in outputs:
+        rows = sum(piece[2] for piece in pieces)
+        shape = jax.ShapeDtypeStruct((rows, n * each), F32)
+        outs.append((shape, (rows, each), lambda s, *at: (0, s)))
+    return picked([[wrap(a) for a in route] for route in routes], tables, fill, outs, name)
 
 
 def joined(x, order):
@@ -551,9 +593,8 @@
         jax.ShapeDtypeStruct((n, 2, cut, units), BF16), (1, 2, cut, units),
         lambda s, *at: (s, 0, 0, 0),
     )
-    gate, up, down = picked(
-        wrap(own_a), wrap(far_a), wrap(own_b), wrap(far_b), tables, fill, [full, full, down], "mlp_weights"
-    )
+    routes = [[wrap(own_a), wrap(far_a)], [wrap(own_b), wrap(far_b)]]
+    gate, up, down = picked(routes, tables, fill, [full, full, down], "mlp_weights")
     return gate.reshape(-1, units), up.reshape(-1, units), down.reshape(-1, units)
 
 
@@ -569,9 +610,8 @@
         jax.ShapeDtypeStruct((groups, n, part, 2 * middle), BF16), (groups, 1, part, 2 * middle),
         lambda s, *at: (0, s, 0, 0),
     )
-    return picked(
-        wrap(own_a), wrap(far_a), wrap(own_b), wrap(far_b), tables, fill, [out], "output_rows"
-    )[0].reshape(-1, 2 * middle)
+    routes = [[wrap(own_a), wrap(far_a)], [wrap(own_b), wrap(far_b)]]
+    return picked(routes, tables, fill, [out], "output_rows")[0].reshape(-1, 2 * middle)
 
 
 def chained(decays, values, place, reverse):
@@ -702,12 +742,17 @@
         [block_diagonal(recur_gate, padded), block_diagonal(input_gate, padded)], axis=1
     )
     pad_rows = lambda a: jnp.pad(a, ((0, extra), (0, 0)))
-    branch_weight = jnp.concatenate([pad_rows(input_weight.T), pad_rows(gelu_weight.T)], axis=0)
+    input_padded, gelu_padded = pad_rows(input_weight.T), pad_rows(gelu_weight.T)
+    branch_weight = jnp.concatenate([input_padded, gelu_padded], axis=0)
     output_padded = pad_rows(output_weight)
     grad_rows = side_by_side(grad_out)
-    params, gates, branch_weight, output_padded, grad_rows, masks, own_rows, full = (
-        lax.optimization_barrier(
-            (params, gates, branch_weight, output_padded, grad_rows, masks, own_rows, full)
+    (
+        params, gates, branch_weight, output_padded, grad_rows, masks, own_rows, full,
+        input_padded, gelu_padded,
+    ) = lax.optimization_barrier(
+        (
+            params, gates, branch_weight, output_padded, grad_rows, masks, own_rows, full,
+            input_padded, gelu_padded,
         )
     )
 
@@ -751,11 +796,13 @@
 
     r2 = lax.rsqrt(jnp.mean(resid * resid, axis=1, keepdims=True) + EPSILON)
     n2 = (resid * r2 * second_gain).astype(BF16)
+    resid_share = lax.dynamic_slice_in_dim(resid, share_start, share, 1)
+    n2, resid_share = lax.optimization_barrier((n2, resid_share))
     hid, d_gate, d_up, pull2 = mlp_units(n2, gate_full, up_full, d_hid)
     d_n2_part = (contract_last(d_gate, gate_full) + contract_last(d_up, up_full)).astype(BF16)
     d_n2 = scatter_features(d_n2_part)
     n2_w, hid_w, pull2 = lax.optimization_barrier((n2, hid, pull2, d_n2_part))[:3]
-    pull2 = lax.psum(jnp.sum(pull2, axis=1), "tp")[:, None]
+    pull2 = lax.psum(jnp.sum(pull2, axis=1), "tp")
     grad_w = after(grad_rows, d_n2_part)
     grad_a, grad_b = relative(grad_w, route_a), relative(grad_w, route_b)
     half = units // 2
@@ -771,16 +818,16 @@
         for (l, r, _), give in zip(products, gives)
     ]
     d_n2, pull2, *sums2 = lax.optimization_barrier((d_n2, pull2, *sums2))
+    pull2 = pull2[:, None]
     gain_share = lax.dynamic_slice_in_dim(second_gain, share_start, share)
     scaled = d_n2 * gain_share * r2
     scaled_low = scaled.astype(BF16)
     scaled_full = gather_features(scaled_low)
-    hid_w, state_w, resid_w, d_n2_w, n1_w, _, *sums2 = lax.optimization_barrier(
-        (hid_w, state, resid, d_n2, n1, scaled_low, *sums2)
+    hid_w, state_w, d_n2_w, n1_w, _, *sums2 = lax.optimization_barrier(
+        (hid_w, state, d_n2, n1, scaled_low, *sums2)
     )
     n1_a, n1_b = relative(n1_w, route_a), relative(n1_w, route_b)
     finals = jnp.dot(picks, state_w, precision=lax.Precision.HIGHEST, preferred_element_type=F32)
-    resid_share = lax.dynamic_slice_in_dim(resid_w, share_start, share, 1)
     grad_second = jnp.sum(d_n2_w * resid_share * r2, axis=0)
     mlp = contract_last(hid_w, down_full).astype(BF16)
     for leg in range(len(order_a) - 1):
@@ -792,99 +839,116 @@
         (scaled_full, mlp, finals, grad_second, n1_a, n1_b, *last_gives)
     )
     mlp_sum = lax.psum_scatter(mlp, "tp", scatter_dimension=1, tiled=True)
-    d_resid_low = (
-        grad_rows.astype(F32) + scaled_full.astype(F32) - resid * centre
-    ).astype(BF16)
     last_gives = [across(v, order[-1]) for v, (_, _, order) in zip(last_gives, products)]
 
-    dm = row_major(contract_last(d_resid_low, output_padded))
-    grad_local, reach_back, dby, heads = reverse_recurrence(dm, both, r, state, masks, params)
-    heads, *last_gives = lax.optimization_barrier((heads, *last_gives))
+    d_resid_low, grad_local, reach_back, dby, heads = reverse_recurrence(
+        grad_rows, scaled_full, n2, r2 * pull2 * (1.0 / width), (1.0 / second_gain)[None],
+        output_padded, both, r, state, masks, params,
+    )
+    back = lambda l, r: contract_first(l, r[:, middle:]).astype(BF16)
+    front = lambda l, r: contract_first(l, r[:, :middle])
+
+    def split(totals):
+        half = totals[0].shape[1] // 2
+        return [t[:, :half] for t in totals], [t[:, half:].astype(BF16) for t in totals]
+
+    def sent(gives, orders, n):
+        return [across(give, order[n]) for give, order in zip(gives, orders)]
+
+    def met(keeps, fars):
+        return [keep + far.astype(F32) for keep, far in zip(keeps, fars)]
+
+    def returned(totals, orders, n):
+        return [
+            jnp.concatenate([t, across(t, order[n])], axis=1) for t, order in zip(totals, orders)
+        ]
+
+    orders = [order_a, order_b]
+    last = len(order_a) - 1
+    resid_a = relative(d_resid_low, route_a)
+    gives = [back(mixed, resid_a), back(dby, n1_b)]
+    heads, gives, last_gives = lax.optimization_barrier((heads, gives, last_gives))
+    fars = [across(give, 0) for give in gives]
     outgoing = lax.all_gather(heads.reshape(2, 8, padded), "seq", axis=0)
     message = chained(outgoing[:, 1], outgoing[:, 0], seq_place, True)
     border = jnp.concatenate([incoming, message])
+    keeps, gives = split(met([front(mixed, resid_a), front(dby, n1_b)], fars))
+    border, gives, keeps = lax.optimization_barrier((border, gives, keeps))
+    fars = sent(gives, orders, 0)
     d_main, tail, edge, sums, pair = gate_gradients(
-        grad_local, reach_back, r, i, conv, state, both, masks, dby, prev, border, params, gates
-    )
+        grad_local, reach_back, r, i, conv, state, both, masks, prev, border, params, gates
+    )
+    edge, fars, keeps = lax.optimization_barrier((edge, fars, keeps))
     beyond = shifted(edge.reshape(halo, 8, padded)[:, 0], "seq", -1)
-    d_branch = settled(d_main, tail, edge, beyond)
-    d_n1_part = dot(d_branch, branch_weight).astype(BF16)
+    early = met(keeps, fars)
+    for n in range(1, last):
+        keeps, gives = split(early)
+        early = met(keeps, sent(gives, orders, n))
+    keeps, gives = split(early)
+    fars = sent(gives, orders, last)
+    dbx = settled(d_main, tail, edge, beyond)
+    part_a = padded // 2
+    gives = [back(dbx[:, :part_a], n1_a), back(dbx[:, part_a:], n1_b)]
+    gives, dbx, fars = lax.optimization_barrier((gives, dbx, fars))
+    far_in = [across(give, 0) for give in gives]
+    early = [t.astype(BF16) for t in met(keeps, fars)]
+    dbx, early = lax.optimization_barrier((dbx, early))
+    early = returned(early, orders, last)
+    d_n1_part = pair_product(dbx, dby, input_padded, gelu_padded)
     d_n1_part, mlp_sum = lax.optimization_barrier((d_n1_part, mlp_sum))
     d_n1 = scatter_features(d_n1_part)
-    d_branch_w, pair, sums, d_n1_w = lax.optimization_barrier((d_branch, pair, sums, d_n1_part))
-    dbx_w, dby_w = d_branch_w[:, :channels], d_branch_w[:, padded : padded + channels]
-    back = lambda l, r: contract_first(l, r[:, middle:]).astype(BF16)
-    front = lambda l, r: contract_first(l, r[:, :middle])
-    give_a, give_b = back(dbx_w, n1_a), back(dby_w, n1_b)
-    give_a, give_b, pair, sums, d_resid_w, d_n1_w, dbx_w, dby_w = lax.optimization_barrier(
-        (give_a, give_b, pair, sums, d_resid_low, d_n1_w, dbx_w, dby_w)
-    )
-
-    def rest(total_a, total_b):
-        for bit_a, bit_b in zip(order_a, order_b):
-            total_a, total_b = crossed(total_a, bit_a, 1), crossed(total_b, bit_b, 1)
-        total_a, total_b = total_a.astype(BF16), total_b.astype(BF16)
-        alone = total_a, total_b
-        for bit_a, bit_b in zip(order_a[::-1], order_b[::-1]):
-            total_a = jnp.concatenate([total_a, across(total_a, bit_a)], axis=1)
-            total_b = jnp.concatenate([total_b, across(total_b, bit_b)], axis=1)
-        return alone, (total_a, across(total_a, 0), total_b, across(total_b, 0))
-
-    far_a, far_b = across(give_a, 0), across(give_b, 0)
-    ready, branch_parts = rest(
-        front(dbx_w, n1_a) + far_a.astype(F32), front(dby_w, n1_b) + far_b.astype(F32)
-    )
+    dbx, d_n1_w, early = lax.optimization_barrier((dbx, d_n1_part, early))
+    for n in range(last - 1, -1, -1):
+        early = returned(early, orders, n)
+    early_parts = [(t, across(t, 0)) for t in early]
+
+    totals = [front(dbx[:, :part_a], n1_a), front(dbx[:, part_a:], n1_b)]
+    keeps, gives = split(met(totals, far_in))
+    gives, pair, sums, d_n1_w = lax.optimization_barrier((gives, pair, sums, d_n1_w))
+    totals = met(keeps, sent(gives, orders, 0))
+    for n in range(1, last + 1):
+        keeps, gives = split(totals)
+        totals = met(keeps, sent(gives, orders, n))
+    ready = totals = [t.astype(BF16) for t in totals]
+    for n in range(last, 0, -1):
+        totals = returned(totals, orders, n)
+    far_in = sent(totals, orders, 0)
+    near_in = totals
+
     first_part = jnp.sum(d_n1_w.astype(F32) * n1.astype(F32), axis=0) / first_gain
     pull1 = jnp.sum(d_n1_w.astype(F32) * n1.astype(F32), axis=1)
     second_part = lax.dynamic_update_slice(jnp.zeros((width,), F32), grad_second, (share_start,))
     over_tp = exchanged(jnp.concatenate([pull1, first_part, second_part]), "tp")
     pull1, gains = over_tp[:tokens, None], over_tp[tokens:]
-    resid_a, resid_b = relative(d_resid_w, route_a), relative(d_resid_w, route_b)
-    cut = channels // 2
-    mixed_a, mixed_b = mixed[:, :cut], mixed[:, cut:]
     gate_grads = contract_first(low, pair)
     corner = lambda n, b: gate_grads[
         b * size : (b + 1) * size, n * padded + b * size : n * padded + (b + 1) * size
     ]
     corners = jnp.concatenate([corner(n, b) for b in range(blocks) for n in (0, 1)], axis=1)
     corners = jnp.pad(corners, ((0, 0), (0, width - corners.shape[1])))
-    corners = relative(corners, route_b)
     sums = jnp.sum(sums.reshape(8, 8, padded), axis=1)
     small = jnp.concatenate([sums, finals], axis=0)[:, :channels]
     packed = jnp.concatenate([gains, small.reshape(-1)])
     packed = jnp.pad(packed, (0, -packed.size % (8 * width))).reshape(-1, width)
     few = packed.shape[0]
-    packed = relative(packed, route_a)
-    far_a = across(
-        jnp.concatenate([back(mixed_a, resid_a), packed[:, middle:].astype(BF16)]), 0
-    )
-    far_b = across(
-        jnp.concatenate([back(mixed_b, resid_b), corners[:, middle:].astype(BF16)]), 0
-    )
-    _, other_parts = rest(
-        jnp.concatenate(
-            [
-                front(mixed_a, resid_a) + far_a[:cut].astype(F32),
-                packed[:, :middle] + far_a[cut:].astype(F32),
-            ]
-        ),
-        jnp.concatenate(
-            [
-                front(mixed_b, resid_b) + far_b[:cut].astype(F32),
-                corners[:, :middle] + far_b[cut:].astype(F32),
-            ]
-        ),
-    )
-
-    kept2, last_gives, mlp_sum, d_n1, resid_share = lax.optimization_barrier(
-        (kept2, last_gives, mlp_sum, d_n1, resid_share, ready)
-    )[:5]
+    extras = [relative(jnp.concatenate([corners, packed]), route_b)]
+    keeps, gives = split(extras)
+    extras = met(keeps, [across(gives[0], 0)])
+    for n in range(last + 1):
+        keeps, gives = split(extras)
+        extras = met(keeps, sent(gives, [order_b], n))
+    extras = [t.astype(BF16) for t in extras]
+
+    kept2, last_gives, mlp_sum, resid_out = lax.optimization_barrier(
+        (kept2, last_gives, mlp_sum, resid_share, gives)
+    )[:4]
+    d_n1, resid_share = lax.optimization_barrier((d_n1, resid_share, ready))[:2]
     done2 = [v + give.astype(F32) for v, give in zip(kept2, last_gives)]
     grad_gate_weight, grad_up_weight = done2[:2]
     grad_down_weight = jnp.concatenate(done2[2:], axis=1).T
     g_share = lax.dynamic_slice_in_dim(grad_rows, share_start, share, 1).astype(F32)
     d_resid_share = g_share + scaled - resid_share * centre
-    block_out = in_order((resid_share + mlp_sum.astype(F32)).astype(BF16))
+    block_out = in_order((resid_out + mlp_sum.astype(F32)).astype(BF16))
     gain1_share = lax.dynamic_slice_in_dim(first_gain, share_start, share)
     grad_in = (
         d_resid_share
@@ -892,23 +956,33 @@
         - x_low.astype(F32) * (r1 * r1 * pull1 * (1.0 / width))
     )
     grad_in = in_order(grad_in.astype(BF16))
+    outputs = (block_out, grad_gate_weight, grad_up_weight, grad_down_weight)
+    for n in range(last, -1, -1):
+        extras = returned(extras, [order_b], n)
+    extra_parts = [(t, across(t, 0)) for t in extras]
     tables = places(route_a), places(route_b)
-    grad_input, grad_gelu = ordered(
-        *branch_parts, tables, [[(0, 0, channels)], [(1, 0, channels)]], "branch_gradients"
-    )
-    done = (block_out, grad_in, grad_gate_weight, grad_up_weight, grad_down_weight, grad_input, grad_gelu)
-    other_parts, done = lax.optimization_barrier((other_parts, done))
-    block_out, grad_in, grad_gate_weight, grad_up_weight, grad_down_weight, grad_input, grad_gelu = done
-    grad_output_weight, packed, corners = ordered(
-        *other_parts,
-        tables,
-        [[(0, 0, cut), (1, 0, cut)], [(0, cut, few)], [(1, cut, size)]],
-        "other_gradients",
+    early_grads = ordered(
+        early_parts, tables, [[(0, 0, channels)], [(1, 0, channels)]], "early_gradients"
+    )
+    far_in, outputs, early_grads = lax.optimization_barrier((far_in, outputs, early_grads))
+    grad_output_weight, grad_gelu = early_grads
+    totals = [jnp.concatenate(both_ways, axis=1) for both_ways in zip(near_in, far_in)]
+    far_in = [across(t, 0) for t in totals]
+    far_in, extra_parts, grad_in = lax.optimization_barrier((far_in, extra_parts, grad_in))
+    in_parts = list(zip(totals, far_in))
+    block_out, grad_gate_weight, grad_up_weight, grad_down_weight = outputs
+    grad_input, corners, packed = ordered(
+        in_parts + extra_parts,
+        (*tables, tables[1]),
+        [[(0, 0, part_a), (1, 0, channels - part_a)], [(2, 0, size)], [(2, size, few)]],
+        "last_gradients",
     )
     packed = packed.reshape(-1)
     gains = packed[: 2 * width]
     small = packed[2 * width : 2 * width + small.size].reshape(small.shape)
-    corners = jnp.swapaxes(corners[:, : 2 * blocks * size].reshape(size, blocks, 2, size), 0, 1)
+    corner_of = lambda n: jnp.stack(
+        [corners[:, (2 * b + n) * size : (2 * b + n + 1) * size] for b in range(blocks)]
+    )
     grad_decay = small[2] * (DECAY_SCALE * jax.nn.sigmoid(-decay_param))
     return (
         block_out,
@@ -918,8 +992,8 @@
         grad_gelu.T,
         small[4:8],
         small[3],
-        corners[:, :, 0],
-        corners[:, :, 1],
+        corner_of(0),
+        corner_of(1),
         small[0],
         small[1],
         grad_decay,

time: 760 us -> 739 us (0.972)
  waiting for transfers between devices: 212 us -> 145 us
  local copies, waits for them, and re-layouts: 96.8 us -> 123 us
  Pallas kernels: 99.4 us -> 125 us
  matrix products: 157 us -> 148 us
    ppermute x50 -> x56, waiting for transfers between devices: 149 us -> 98.6 us  [across(): return lax.ppermute(x, axis, [(i, i ^ 1 << bit) for i in range(n)])]
    dot_general x3 -> x2, matrix products: 41.5 us -> 29.1 us  [dot(): return jnp.dot(left, right, preferred_element_type=F32)]
    unnamed x262 -> x292, local copies, waits for them, and re-layouts: 35.4 us -> 47.8 us
    pallas_call x4, Pallas kernels: 33.8 us -> 45 us  [picked(): pl.pallas_call(kernel, name=name, grid_spec=pltpu.PrefetchScalarGridSpec(...]
    all_gather x1, waiting for transfers between devices: 9.82 us -> 0.01 us  [on_device(): mixed_full = lax.all_gather(mixed, 'tp', axis=1, tiled=True)]
    pallas_call x1, Pallas kernels: 10.2 us -> 18.1 us  [reverse_recurrence(): pl.pallas_call(reverse_kernel, name='reverse_recurrence', grid=(tiles,),...]
    dot_general x5 -> x4, matrix products: 47.4 us -> 42.6 us  [contract_last(): lax.dot_general(left, right, (((1,), (1,)), ((), ())), preferred_element_...]
    ppermute x50 -> x56, starting transfers between devices: 48 us -> 48.7 us  [across(): return lax.ppermute(x, axis, [(i, i ^ 1 << bit) for i in range(n)])]
  transfers between devices with their start and end apart: 61 -> 67, of which waited for: 29 -> 16; matrix products, arithmetic and copies ran while one was open for 32% -> 35% of each run, Pallas kernels for 9% -> 13%
where the time goes in v3:
time: 739 us; the launch traced here: 730 us
  matrix products  148 us (20%)
  waiting for transfers between devices  145 us (20%)
  Pallas kernels  125 us (17%)
  local copies, waits for them, and re-layouts  123 us (17%)
  other arithmetic  82.4 us (11%)
  starting transfers between devices  56.8 us (8%)
  blocking collectives  32.4 us (4%)
  between operations  17.4 us (2%)
    ppermute x56, waiting for transfers between devices, across(): return lax.ppermute(x, axis, [(i, i ^ 1 << bit) for i in range(n)])  98.6 us
    dot_general x17, matrix products, contract_first(): lax.dot_general(left, right, (((0,), (0,)), ((), ())), preferred_element_...  71.5 us
    ppermute x56, starting transfers between devices, across(): return lax.ppermute(x, axis, [(i, i ^ 1 << bit) for i in range(n)])  48.7 us
    unnamed x292, local copies, waits for them, and re-layouts  47.8 us
    pallas_call x4, Pallas kernels, picked(): pl.pallas_call(kernel, name=name, grid_spec=pltpu.PrefetchScalarGridSpec(...  45 us
    dot_general x4, matrix products, contract_last(): lax.dot_general(left, right, (((1,), (1,)), ((), ())), preferred_element_...  42.6 us
    all_gather x2, waiting for transfers between devices, gather_features(): return lax.all_gather(x, 'tp', axis=1, tiled=True)  33.2 us
    dot_general x2, matrix products, dot(): return jnp.dot(left, right, preferred_element_type=F32)  29.1 us
  transfers between devices with their start and end apart: 67, of which 16 were waited for; matrix products, arithmetic and copies ran while one was open for 35% of the time, Pallas kernels for 13%

profile of v3, /device:TPU:0, one launch (start us, length us, event | category | flops | bytes accessed | tf_op | source)
XLA Modules:
  0.0 729.7 jit_solution(17617869732091843321)
XLA Ops:
  17.3 22.5 %collective-permute-done.1 = bf16[1,384,1536]{2,1,0:T(8,128)(2,1)} collective-permute-done((bf16[1,384,1536]{2,1,0:T(8,128)(2,1)S(1)}, bf16[1,384,1536]{2,1,0:T(8,128)(2,1)}, u32[]{:S(2)}, u32[]{:S(2)}) %collective-permute-start.1) | collective-permute-done | bytes 1179680 | tf_op jit(solution)/shard_map/ppermute | solution.py:462
  58.8 4.3 copy.98
  71.5 3.8 pad_maximum_fusion
  77.7 16.1 %all-gather.6.cloned.1.call-done = bf16[1024,2048]{1,0:T(8,128)(2,1)} async-done(((bf16[1024,512]{1,0:T(8,128)(2,1)}), bf16[1024,2048]{1,0:T(8,128)(2,1)}) %all-gather.6.cloned.1.call-update) | async-done | bytes 4194320 | tf_op jit(solution)/shard_map/all_gather | solution.py:674
  100.4 10.4 %fusion.390.bx_ref.by_ref.bx_before_ref = f32[1024,1536]{1,0:T(8,128)S(1)} fusion(bf16[1024,2048]{1,0:T(8,128)(2,1)S(1)} %fusion.2, bf16[1536,2048]{1,0:T(8,128)(2,1)} %pad_maximum_fusion), kind=kOutput, calls=%fused_computation.852 | convolution fusion | flops 6442450944 | bytes 16777216 | tf_op jit(solution)/shard_map/dot_general | solution.py:30
  119.8 12.0 %forward_recurrence.1 = (f32[1024,768]{1,0:T(8,128)}, bf16[1024,768]{1,0:T(8,128)(2,1)}, f32[1024,768]{1,0:T(8,128)}, f32[1024,768]{1,0:T(8,128)}, f32[1024,768]{1,0:T(8,128)}, /*index=5*/f32[1024,768]{1,0:T(8,128)}) custom-call(f32[1024,1536]{1,0:T(8,128)} %copy-done.21, f32[24,768]{1,0:T(8,128)} %maximum_bitcast_fusion.3.prev_ref, f32[1024,8]{1,0:T(8,128)} %bitcast.1898, ...), custom_call_target="tpu_custom_call" | custom-call | flops 2415919104 | bytes 23592960 | tf_op jit(solution)/shard_map/forward_recurrence/pallas_call | solution.py:123
  133.3 9.8 %all-gather = f32[16,8,768]{2,1,0:T(8,128)S(1)} all-gather(f32[2,8,768]{2,1,0:T(8,128)S(1)} %pad_maximum_fusion.55), channel_id=2, replica_groups=mesh['seq'=8,'tp'=4] {'seq'}, dimensions={0}, use_global_device_ids=true | all-gather | bytes 442368 | tf_op jit(solution)/shard_map/all_gather | solution.py:771
  143.8 3.2 fusion.8.state_ref.before_ref
  148.8 4.0 fusion.7
  155.4 3.2 constant_dynamic-update-slice_fusion.3
  162.2 3.5 constant_dynamic-update-slice_fusion.1
  165.7 3.5 constant_dynamic-update-slice_fusion.refs_2_
  171.5 16.5 %collective-permute-done.11 = bf16[1,4,88,1024]{3,2,1,0:T(8,128)(2,1)S(1)} collective-permute-done((bf16[1,4,88,1024]{3,2,1,0:T(8,128)(2,1)S(1)}, bf16[1,4,88,1024]{3,2,1,0:T(8,128)(2,1)S(1)}, u32[]{:S(2)}, u32[]{:S(2)}) %collective-permute-start.11) | collective-permute-done | bytes 720928 | tf_op jit(solution)/shard_map/ppermute | solution.py:462
  190.3 31.0 %collective-permute-done.12 = bf16[2,4,88,1024]{3,2,1,0:T(8,128)(2,1)S(1)} collective-permute-done((bf16[2,4,88,1024]{3,2,1,0:T(8,128)(2,1)S(1)}, bf16[2,4,88,1024]{3,2,1,0:T(8,128)(2,1)S(1)}, u32[]{:S(2)}, u32[]{:S(2)}) %collective-permute-start.12) | collective-permute-done | bytes 1441824 | tf_op jit(solution)/shard_map/ppermute | solution.py:462
  225.7 18.7 %mlp_weights.1 = (bf16[8,256,1536]{2,1,0:T(8,128)(2,1)}, bf16[8,256,1536]{2,1,0:T(8,128)(2,1)}, bf16[8,2,128,1536]{3,2,1,0:T(8,128)(2,1)}) custom-call(s32[8]{0:T(128)S(1)} %get-tuple-element.510.refs_0_.refs_1_.refs_2_, s32[8]{0:T(128)S(1)} %get-tuple-element.509.refs_1_.refs_0_, bf16[4,384,1536]{2,1,0:T(8,128)(2,1)} %constant_dynamic-update-slice_fusion.refs_2_, ...), custom_call_target="tpu_custom_call" | custom-call | bytes 56623104 | tf_op jit(solution)/shard_map/mlp_weights/pallas_call | solution.py:528
  244.4 10.4 %fusion.391.d_hid_ref = f32[1024,1536]{1,0:T(8,128)} fusion(bf16[1024,2048]{1,0:T(8,128)(2,1)S(1)} %bitcast.1896, bf16[2048,1536]{1,0:T(8,128)(2,1)} %bitcast.1935), kind=kOutput, calls=%fused_computation.853 | convolution fusion | flops 6442450944 | bytes 16777216 | tf_op jit(solution)/shard_map/dot_general | solution.py:22
  254.8 12.8 %output_rows.1 = bf16[4,8,88,2048]{3,2,1,0:T(8,128)(2,1)} custom-call(s32[8]{0:T(128)S(1)} %get-tuple-element.510.refs_0_.refs_1_.refs_2_, s32[8]{0:T(128)S(1)} %get-tuple-element.509.refs_1_.refs_0_, bf16[4,4,88,1024]{3,2,1,0:T(8,128)(2,1)} %pad_maximum_fusion.1.refs_2_, bf16[4,4,88,1024]{3,2,1,0:T(8,128)(2,1)} %collective-permute-done.10.refs_3_, ...), custom_call_target="tpu_custom_call" | custom-call | bytes 34603008 | tf_op jit(solution)/shard_map/output_rows/pallas_call | solution.py:528
  267.6 18.7 %multiply_reduce_fusion = (f32[1024]{0:T(1024)S(1)}, f32[1024,2048]{1,0:T(8,128)S(1)}) fusion(bf16[1024,2816]{0,1:T(8,128)(2,1)} %all-gather.10.cloned.1.call-done, bf16[2816,2048]{1,0:T(8,128)(2,1)} %bitcast.1897, bf16[1024,2048]{1,0:T(8,128)(2,1)} %all-gather.6.cloned.1.call-done), kind=kOutput, calls=%fused_computation.9 | convolution fusion | flops 11819547648 | bytes 29888512 | tf_op jit(solution)/shard_map/dot_general | solution.py:22
  290.7 23.4 %mlp_units.1 = (bf16[1024,1536]{1,0:T(8,128)(2,1)S(1)}, bf16[1024,1536]{1,0:T(8,128)(2,1)}, bf16[1024,1536]{1,0:T(8,128)(2,1)}, f32[1024,128]{1,0:T(8,128)S(1)}) custom-call(bf16[1024,2048]{1,0:T(8,128)(2,1)} %multiply_convert_fusion.n2_ref, bf16[2048,1536]{1,0:T(8,128)(2,1)} %bitcast.1943, bf16[2048,1536]{1,0:T(8,128)(2,1)} %bitcast.1939, ...), custom_call_target="tpu_custom_call" | custom-call | flops 12884901888 | bytes 32505856 | tf_op jit(solution)/shard_map/mlp_units/pallas_call | solution.py:401
  314.1 13.2 %fusion.392 = f32[1024,2048]{1,0:T(8,128)} fusion(bf16[1024,1536]{1,0:T(8,128)(2,1)} %get-tuple-element.208, bf16[2048,1536]{1,0:T(8,128)(2,1)} %bitcast.1944), kind=kOutput, calls=%fused_computation.854 | convolution fusion | flops 6442450944 | bytes 17825792 | tf_op jit(solution)/shard_map/dot_general | solution.py:30
  327.3 10.4 %add_convert_fusion = bf16[1024,2048]{1,0:T(8,128)(2,1)} fusion(f32[1024,2048]{1,0:T(8,128)} %fusion.392, bf16[1024,1536]{1,0:T(8,128)(2,1)S(1)} %copy-done.126, bf16[2048,1536]{1,0:T(8,128)(2,1)S(1)} %bitcast.1942), kind=kOutput, calls=%fused_computation.7 | convolution fusion | flops 6446645248 | bytes 22020096 | tf_op jit(solution)/shard_map/dot_general | solution.py:30
  337.9 3.8 constant_dynamic-slice_fusion.44
  347.3 5.4 convolution_convert_fusion.1
  352.7 5.1 convolution_convert_fusion.2
  362.7 12.9 %psum.7 = f32[1024]{0:T(1024)} all-reduce(f32[1024]{0:T(1024)S(1)} %reduce_sum.65), channel_id=1, replica_groups=mesh['seq'=8,'tp'=4] {'tp'}, use_global_device_ids=true, to_apply=%region_4.5 | all-reduce | flops 1024 | bytes 8192 | tf_op jit(solution)/shard_map/psum | solution.py:805
  375.7 6.2 convert_add_fusion.6
  382.0 5.1 convert_add_fusion.7
  387.1 7.2 convert_add_fusion.1
  394.3 7.1 convert_add_fusion.2
  401.4 13.5 %reduce-scatter.4.cloned.1.call-done = bf16[1024,512]{1,0:T(8,128)(2,1)} async-done(((bf16[1024,2048]{1,0:T(8,128)(2,1)}), bf16[1024,512]{1,0:T(8,128)(2,1)}) %reduce-scatter.4.cloned.1.call-update) | async-done | bytes 1048592 | tf_op jit(solution)/shard_map/reduce_scatter | solution.py:678
  427.2 3.7 slice.3189
  440.8 8.6 %convolution_convert_fusion = bf16[1024,2048]{1,0:T(8,128)(2,1)} fusion(bf16[1024,1536]{1,0:T(8,128)(2,1)S(1)} %copy-done.20, bf16[2048,1536]{1,0:T(8,128)(2,1)S(1)} %bitcast.1938), kind=kOutput, calls=%fused_computation.20 | convolution fusion | flops 6444548096 | bytes 13631488 | tf_op jit(solution)/shard_map/dot_general | solution.py:30
  451.8 4.6 fusion.121
  467.3 7.9 %collective-permute-done.20 = bf16[512,1536]{1,0:T(8,128)(2,1)} collective-permute-done((bf16[512,1536]{1,0:T(8,128)(2,1)}, bf16[512,1536]{1,0:T(8,128)(2,1)}, u32[]{:S(2)}, u32[]{:S(2)}) %collective-permute-start.20) | collective-permute-done | bytes 1572896 | tf_op jit(solution)/shard_map/ppermute | solution.py:462
  483.3 17.1 %all-gather.12.cloned.1.call-done.scaled_ref = bf16[1024,2048]{1,0:T(8,128)(2,1)} async-done(((bf16[1024,512]{1,0:T(8,128)(2,1)}), bf16[1024,2048]{1,0:T(8,128)(2,1)}) %all-gather.12.cloned.1.call-update) | async-done | bytes 4194320 | tf_op jit(solution)/shard_map/all_gather | solution.py:674
  507.5 18.1 %reverse_recurrence.1 = (bf16[1024,2048]{1,0:T(8,128)(2,1)}, f32[1024,768]{1,0:T(8,128)}, f32[1024,768]{1,0:T(8,128)}, bf16[1024,768]{1,0:T(8,128)(2,1)}, f32[16,768]{1,0:T(8,128)}) custom-call(bf16[1024,2048]{1,0:T(8,128)(2,1)} %bitcast.1894, bf16[1024,2048]{1,0:T(8,128)(2,1)} %all-gather.12.cloned.1.call-done.scaled_ref, ...), custom_call_target="tpu_custom_call" | custom-call | flops 3221225472 | bytes 35651584 | tf_op jit(solution)/shard_map/reverse_recurrence/pallas_call | solution.py:188
  525.6 3.8 constant_dynamic-slice_fusion.31
  537.3 5.6 fusion.69
  542.9 9.7 %all_gather.27 = f32[8,2,8,768]{3,2,1,0:T(8,128)S(1)} all-gather(f32[1,2,8,768]{3,2,1,0:T(8,128)S(1)} %bitcast.1922), channel_id=1, replica_groups=mesh['seq'=8,'tp'=4] {'seq'}, dimensions={0}, use_global_device_ids=true | all-gather | bytes 442368 | tf_op jit(solution)/shard_map/all_gather | solution.py:872
  554.5 4.2 convert_add_fusion.8
  568.8 17.7 %gate_gradients.1 = (bf16[1024,768]{1,0:T(8,128)(2,1)}, f32[32,768]{1,0:T(8,128)}, f32[24,768]{1,0:T(8,128)}, f32[64,768]{1,0:T(8,128)}, bf16[1024,1536]{1,0:T(8,128)(2,1)}) custom-call(f32[1024,768]{1,0:T(8,128)} %get-tuple-element.234.grad_ref, f32[1024,768]{1,0:T(8,128)} %get-tuple-element.235.reach_ref, f32[1024,768]{1,0:T(8,128)} %get-tuple-element.233.r_ref, ...), custom_call_target="tpu_custom_call" | custom-call | flops 2415919104 | bytes 26738688 | tf_op jit(solution)/shard_map/gate_gradients/pallas_call | solution.py:307
  597.5 3.9 fusion.89
  609.6 7.2 pair_product.1
  647.5 4.7 collective-permute-done.47
  666.0 3.9 collective-permute-done.49
  687.0 6.8 early_gradients.1
  702.0 3.5 fusion.106
  710.9 6.6 last_gradients.1
  (602 shorter events, 257.1 us)
Async XLA Ops:
  7.2 86.6 %all-gather.6.cloned.1.call-start = ((), (), s32[]{:S(2)}) async-start(), calls=%async_computation.3 | async-start | bytes 5242880 | tf_op jit(solution)/shard_map/all_gather | solution.py:674
  10.2 123.2 %all-gather.8.cloned.1.call-start = ((), (), s32[]{:S(2)}) async-start(), calls=%async_computation.4 | async-start | bytes 1802240 | tf_op jit(solution)/shard_map/all_gather | solution.py:766
  10.7 29.1 %collective-permute-start.1 = (bf16[1,384,1536]{2,1,0:T(8,128)(2,1)S(1)}, bf16[1,384,1536]{2,1,0:T(8,128)(2,1)}, u32[]{:S(2)}, u32[]{:S(2)}) collective-permute-start(bf16[1,384,1536]{2,1,0:T(8,128)(2,1)S(1)} %maximum_bitcast_fusion.2), channel_id=1, source_target_pairs={{0,16},{4,20},{8,24},{12,28},{16,0},{20,4},{24,8},{28,12},{1,17},{... | collective-permute-start | bytes 3538952 | tf_op jit(solution)/shard_map/ppermute | solution.py:462
  15.0 27.8 %collective-permute-start = (bf16[1,384,1536]{2,1,0:T(8,128)(2,1)S(1)}, bf16[1,384,1536]{2,1,0:T(8,128)(2,1)}, u32[]{:S(2)}, u32[]{:S(2)}) collective-permute-start(bf16[1,384,1536]{2,1,0:T(8,128)(2,1)S(1)} %maximum_bitcast_fusion.1), channel_id=1, source_target_pairs={{0,8},{4,12},{8,0},{12,4},{16,24},{20,28},{24,16},{28,20},{1,9},{5... | collective-permute-start | bytes 3538952 | tf_op jit(solution)/shard_map/ppermute | solution.py:462
  46.5 28.9 %collective-permute-start.18 = (f32[1]{0:T(128)}, f32[1]{0:T(128)}, u32[]{:S(2)}, u32[]{:S(2)}) collective-permute-start(f32[1]{0:T(128)} %slice.1434), channel_id=1, source_target_pairs={{4,0},{8,4},{12,8},{16,12},{20,16},{24,20},{28,24},{5,1},{9,5},{13... | collective-permute-start | bytes 20 | tf_op jit(solution)/shard_map/ppermute | solution.py:451
  47.7 28.8 %collective-permute-start.2 = (f32[3]{0:T(128)S(1)}, f32[3]{0:T(128)S(1)}, u32[]{:S(2)}, u32[]{:S(2)}) collective-permute-start(f32[3]{0:T(128)S(1)} %slice.1290), channel_id=1, source_target_pairs={{0,4},{4,8},{8,12},{12,16},{16,20},{20,24},{24,28},{1,5},{5,9},{9,... | collective-permute-start | bytes 44 | tf_op jit(solution)/shard_map/ppermute | solution.py:451
  63.1 54.1 %collective-permute-start.3 = (bf16[2,384,1536]{2,1,0:T(8,128)(2,1)}, bf16[2,384,1536]{2,1,0:T(8,128)(2,1)}, u32[]{:S(2)}, u32[]{:S(2)}) collective-permute-start(bf16[2,384,1536]{2,1,0:T(8,128)(2,1)} %pad_maximum_fusion.19), channel_id=1, source_target_pairs={{0,16},{4,20},{8,24},{12,28},{16,0},{20,4},{24,8},{28,12},{1,17},{... | collective-permute-start | bytes 7077896 | tf_op jit(solution)/shard_map/ppermute | solution.py:462
  64.8 54.3 %collective-permute-start.4 = (bf16[2,384,1536]{2,1,0:T(8,128)(2,1)}, bf16[2,384,1536]{2,1,0:T(8,128)(2,1)}, u32[]{:S(2)}, u32[]{:S(2)}) collective-permute-start(bf16[2,384,1536]{2,1,0:T(8,128)(2,1)} %pad_maximum_fusion.20), channel_id=1, source_target_pairs={{0,8},{4,12},{8,0},{12,4},{16,24},{20,28},{24,16},{28,20},{1,9},{5... | collective-permute-start | bytes 7077896 | tf_op jit(solution)/shard_map/ppermute | solution.py:462
  96.9 170.7 %all-gather.10.cloned.1.call-start = ((), (), s32[]{:S(2)}) async-start(), calls=%async_computation.5 | async-start | bytes 7208960 | tf_op jit(solution)/shard_map/all_gather | solution.py:776
  155.4 259.5 %reduce-scatter.4.cloned.1.call-start = ((), (), s32[]{:S(2)}) async-start(), calls=%async_computation.6 | async-start | bytes 5242880 | tf_op jit(solution)/shard_map/reduce_scatter | solution.py:678
  161.8 63.8 %collective-permute-start.7 = (bf16[4,384,1536]{2,1,0:T(8,128)(2,1)}, bf16[4,384,1536]{2,1,0:T(8,128)(2,1)}, u32[]{:S(2)}, u32[]{:S(2)}) collective-permute-start(bf16[4,384,1536]{2,1,0:T(8,128)(2,1)} %constant_dynamic-update-slice_fusion.2.refs_4_), channel_id=1, source_target_pairs={{0,4},{4,0},{8,12},{12,8},{16,20},{20,16},{24,28},{28,24},{1,5},{5... | collective-permute-start | bytes 14155784 | tf_op jit(solution)/shard_map/ppermute | solution.py:462
  169.2 56.4 %collective-permute-start.6 = (bf16[4,384,1536]{2,1,0:T(8,128)(2,1)}, bf16[4,384,1536]{2,1,0:T(8,128)(2,1)}, u32[]{:S(2)}, u32[]{:S(2)}) collective-permute-start(bf16[4,384,1536]{2,1,0:T(8,128)(2,1)} %constant_dynamic-update-slice_fusion.refs_2_), channel_id=1, source_target_pairs={{0,4},{4,0},{8,12},{12,8},{16,20},{20,16},{24,28},{28,24},{1,5},{5... | collective-permute-start | bytes 14155784 | tf_op jit(solution)/shard_map/ppermute | solution.py:462
  169.5 18.5 %collective-permute-start.11 = (bf16[1,4,88,1024]{3,2,1,0:T(8,128)(2,1)S(1)}, bf16[1,4,88,1024]{3,2,1,0:T(8,128)(2,1)S(1)}, u32[]{:S(2)}, u32[]{:S(2)}) collective-permute-start(bf16[1,4,88,1024]{3,2,1,0:T(8,128)(2,1)S(1)} %get-tuple-element.474), channel_id=1, source_target_pairs={{0,16},{4,20},{8,24},{12,28},{16,0},{20,4},{24,8},{28,12},{1,17},{... | collective-permute-start | bytes 2162696 | tf_op jit(solution)/shard_map/ppermute | solution.py:462
  170.1 18.6 %collective-permute-start.8 = (bf16[1,4,88,1024]{3,2,1,0:T(8,128)(2,1)S(1)}, bf16[1,4,88,1024]{3,2,1,0:T(8,128)(2,1)S(1)}, u32[]{:S(2)}, u32[]{:S(2)}) collective-permute-start(bf16[1,4,88,1024]{3,2,1,0:T(8,128)(2,1)S(1)} %get-tuple-element.475), channel_id=1, source_target_pairs={{0,8},{4,12},{8,0},{12,4},{16,24},{20,28},{24,16},{28,20},{1,9},{5... | collective-permute-start | bytes 2162696 | tf_op jit(solution)/shard_map/ppermute | solution.py:462
  188.1 33.2 %collective-permute-start.12 = (bf16[2,4,88,1024]{3,2,1,0:T(8,128)(2,1)S(1)}, bf16[2,4,88,1024]{3,2,1,0:T(8,128)(2,1)S(1)}, u32[]{:S(2)}, u32[]{:S(2)}) collective-permute-start(bf16[2,4,88,1024]{3,2,1,0:T(8,128)(2,1)S(1)} %pad_maximum_fusion.42), channel_id=1, source_target_pairs={{0,8},{4,12},{8,0},{12,4},{16,24},{20,28},{24,16},{28,20},{1,9},{5... | collective-permute-start | bytes 4325384 | tf_op jit(solution)/shard_map/ppermute | solution.py:462
  188.8 34.3 %collective-permute-start.9 = (bf16[2,4,88,1024]{3,2,1,0:T(8,128)(2,1)S(1)}, bf16[2,4,88,1024]{3,2,1,0:T(8,128)(2,1)S(1)}, u32[]{:S(2)}, u32[]{:S(2)}) collective-permute-start(bf16[2,4,88,1024]{3,2,1,0:T(8,128)(2,1)S(1)} %pad_maximum_fusion.41), channel_id=1, source_target_pairs={{0,16},{4,20},{8,24},{12,28},{16,0},{20,4},{24,8},{28,12},{1,17},{... | collective-permute-start | bytes 4325384 | tf_op jit(solution)/shard_map/ppermute | solution.py:462
  223.2 31.6 %collective-permute-start.13 = (bf16[4,4,88,1024]{3,2,1,0:T(8,128)(2,1)}, bf16[4,4,88,1024]{3,2,1,0:T(8,128)(2,1)}, u32[]{:S(2)}, u32[]{:S(2)}) collective-permute-start(bf16[4,4,88,1024]{3,2,1,0:T(8,128)(2,1)} %pad_maximum_fusion.2.refs_4_), channel_id=1, source_target_pairs={{0,4},{4,0},{8,12},{12,8},{16,20},{20,16},{24,28},{28,24},{1,5},{5... | collective-permute-start | bytes 8650760 | tf_op jit(solution)/shard_map/ppermute | solution.py:462
  225.1 29.6 %collective-permute-start.10 = (bf16[4,4,88,1024]{3,2,1,0:T(8,128)(2,1)}, bf16[4,4,88,1024]{3,2,1,0:T(8,128)(2,1)}, u32[]{:S(2)}, u32[]{:S(2)}) collective-permute-start(bf16[4,4,88,1024]{3,2,1,0:T(8,128)(2,1)} %pad_maximum_fusion.1.refs_2_), channel_id=1, source_target_pairs={{0,4},{4,0},{8,12},{12,8},{16,20},{20,16},{24,28},{28,24},{1,5},{5... | collective-permute-start | bytes 8650760 | tf_op jit(solution)/shard_map/ppermute | solution.py:462
  337.7 162.7 %all-gather.12.cloned.1.call-start = ((), (), s32[]{:S(2)}) async-start(), calls=%async_computation.7 | async-start | bytes 5242880 | tf_op jit(solution)/shard_map/all_gather | solution.py:674
  344.7 31.0 %collective-permute-start.17 = (bf16[1024,768]{1,0:T(8,128)(2,1)}, bf16[1024,768]{1,0:T(8,128)(2,1)}, u32[]{:S(2)}, u32[]{:S(2)}) collective-permute-start(bf16[1024,768]{1,0:T(8,128)(2,1)} %fusion.82), channel_id=1, source_target_pairs={{0,4},{4,0},{8,12},{12,8},{16,20},{20,16},{24,28},{28,24},{1,5},{5... | collective-permute-start | bytes 4718600 | tf_op jit(solution)/shard_map/ppermute | solution.py:462
  352.7 34.4 %collective-permute-start.15 = (bf16[1024,1536]{1,0:T(8,128)(2,1)}, bf16[1024,1536]{1,0:T(8,128)(2,1)}, u32[]{:S(2)}, u32[]{:S(2)}) collective-permute-start(bf16[1024,1536]{1,0:T(8,128)(2,1)} %convolution_convert_fusion.1), channel_id=1, source_target_pairs={{0,4},{4,0},{8,12},{12,8},{16,20},{20,16},{24,28},{28,24},{1,5},{5... | collective-permute-start | bytes 9437192 | tf_op jit(solution)/shard_map/ppermute | solution.py:462
  357.8 36.5 %collective-permute-start.14 = (bf16[1024,1536]{1,0:T(8,128)(2,1)}, bf16[1024,1536]{1,0:T(8,128)(2,1)}, u32[]{:S(2)}, u32[]{:S(2)}) collective-permute-start(bf16[1024,1536]{1,0:T(8,128)(2,1)} %convolution_convert_fusion.2), channel_id=1, source_target_pairs={{0,4},{4,0},{8,12},{12,8},{16,20},{20,16},{24,28},{28,24},{1,5},{5... | collective-permute-start | bytes 9437192 | tf_op jit(solution)/shard_map/ppermute | solution.py:462
  361.4 20.5 %collective-permute-start.16 = (bf16[1024,768]{1,0:T(8,128)(2,1)}, bf16[1024,768]{1,0:T(8,128)(2,1)}, u32[]{:S(2)}, u32[]{:S(2)}) collective-permute-start(bf16[1024,768]{1,0:T(8,128)(2,1)} %fusion.83), channel_id=1, source_target_pairs={{0,4},{4,0},{8,12},{12,8},{16,20},{20,16},{24,28},{28,24},{1,5},{5... | collective-permute-start | bytes 4718600 | tf_op jit(solution)/shard_map/ppermute | solution.py:462
  419.0 203.8 %reduce-scatter.6.cloned.1.call-start = ((), (), s32[]{:S(2)}) async-start(), calls=%async_computation.8 | async-start | bytes 5242880 | tf_op jit(solution)/shard_map/reduce_scatter | solution.py:841
  421.8 40.1 %collective-permute-start.22 = (bf16[512,768]{1,0:T(8,128)(2,1)}, bf16[512,768]{1,0:T(8,128)(2,1)}, u32[]{:S(2)}, u32[]{:S(2)}) collective-permute-start(bf16[512,768]{1,0:T(8,128)(2,1)} %slice.3192), channel_id=1, source_target_pairs={{0,16},{4,20},{8,24},{12,28},{16,0},{20,4},{24,8},{28,12},{1,17},{... | collective-permute-start | bytes 2359304 | tf_op jit(solution)/shard_map/ppermute | solution.py:462
  425.7 38.2 %collective-permute-start.21 = (bf16[512,768]{1,0:T(8,128)(2,1)}, bf16[512,768]{1,0:T(8,128)(2,1)}, u32[]{:S(2)}, u32[]{:S(2)}) collective-permute-start(bf16[512,768]{1,0:T(8,128)(2,1)} %slice.3193), channel_id=1, source_target_pairs={{0,8},{4,12},{8,0},{12,4},{16,24},{20,28},{24,16},{28,20},{1,9},{5... | collective-permute-start | bytes 2359304 | tf_op jit(solution)/shard_map/ppermute | solution.py:462
  430.8 44.4 %collective-permute-start.20 = (bf16[512,1536]{1,0:T(8,128)(2,1)}, bf16[512,1536]{1,0:T(8,128)(2,1)}, u32[]{:S(2)}, u32[]{:S(2)}) collective-permute-start(bf16[512,1536]{1,0:T(8,128)(2,1)} %slice.3189), channel_id=1, source_target_pairs={{0,16},{4,20},{8,24},{12,28},{16,0},{20,4},{24,8},{28,12},{1,17},{... | collective-permute-start | bytes 4718600 | tf_op jit(solution)/shard_map/ppermute | solution.py:462
  434.6 44.1 %collective-permute-start.19 = (bf16[512,1536]{1,0:T(8,128)(2,1)}, bf16[512,1536]{1,0:T(8,128)(2,1)}, u32[]{:S(2)}, u32[]{:S(2)}) collective-permute-start(bf16[512,1536]{1,0:T(8,128)(2,1)} %slice.3190), channel_id=1, source_target_pairs={{0,8},{4,12},{8,0},{12,4},{16,24},{20,28},{24,16},{28,20},{1,9},{5... | collective-permute-start | bytes 4718600 | tf_op jit(solution)/shard_map/ppermute | solution.py:462
  500.5 199.3 %reduce-scatter.8.cloned.1.call-start = ((), (), s32[]{:S(2)}) async-start(), calls=%async_computation.9 | async-start | bytes 5242880 | tf_op jit(solution)/shard_map/reduce_scatter | solution.py:678
  503.4 32.5 %collective-permute-start.23 = (bf16[256,1536]{1,0:T(8,128)(2,1)}, bf16[256,1536]{1,0:T(8,128)(2,1)}, u32[]{:S(2)}, u32[]{:S(2)}) collective-permute-start(bf16[256,1536]{1,0:T(8,128)(2,1)} %slice.3195), channel_id=1, source_target_pairs={{0,16},{4,20},{8,24},{12,28},{16,0},{20,4},{24,8},{28,12},{1,17},{... | collective-permute-start | bytes 2359304 | tf_op jit(solution)/shard_map/ppermute | solution.py:462
  504.9 31.8 %collective-permute-start.24 = (bf16[256,1536]{1,0:T(8,128)(2,1)}, bf16[256,1536]{1,0:T(8,128)(2,1)}, u32[]{:S(2)}, u32[]{:S(2)}) collective-permute-start(bf16[256,1536]{1,0:T(8,128)(2,1)} %slice.3194), channel_id=1, source_target_pairs={{0,8},{4,12},{8,0},{12,4},{16,24},{20,28},{24,16},{28,20},{1,9},{5... | collective-permute-start | bytes 2359304 | tf_op jit(solution)/shard_map/ppermute | solution.py:462
  506.4 28.8 %collective-permute-start.25 = (bf16[256,768]{1,0:T(8,128)(2,1)}, bf16[256,768]{1,0:T(8,128)(2,1)S(1)}, u32[]{:S(2)}, u32[]{:S(2)}) collective-permute-start(bf16[256,768]{1,0:T(8,128)(2,1)} %slice.3201), channel_id=1, source_target_pairs={{0,16},{4,20},{8,24},{12,28},{16,0},{20,4},{24,8},{28,12},{1,17},{... | collective-permute-start | bytes 1179656 | tf_op jit(solution)/shard_map/ppermute | solution.py:462
  506.9 28.2 %collective-permute-start.26 = (bf16[256,768]{1,0:T(8,128)(2,1)S(1)}, bf16[256,768]{1,0:T(8,128)(2,1)S(1)}, u32[]{:S(2)}, u32[]{:S(2)}) collective-permute-start(bf16[256,768]{1,0:T(8,128)(2,1)S(1)} %slice.3200), channel_id=1, source_target_pairs={{0,8},{4,12},{8,0},{12,4},{16,24},{20,28},{24,16},{28,20},{1,9},{5... | collective-permute-start | bytes 1179656 | tf_op jit(solution)/shard_map/ppermute | solution.py:462
  536.7 17.8 %collective-permute-start.27 = (bf16[704,1024]{1,0:T(8,128)(2,1)}, bf16[704,1024]{1,0:T(8,128)(2,1)}, u32[]{:S(2)}, u32[]{:S(2)}) collective-permute-start(bf16[704,1024]{1,0:T(8,128)(2,1)} %fusion.86), channel_id=1, source_target_pairs={{0,4},{4,0},{8,12},{12,8},{16,20},{20,16},{24,28},{28,24},{1,5},{5... | collective-permute-start | bytes 4325384 | tf_op jit(solution)/shard_map/ppermute | solution.py:462
  536.8 23.7 %collective-permute-start.28 = (bf16[768,1024]{1,0:T(8,128)(2,1)}, bf16[768,1024]{1,0:T(8,128)(2,1)}, u32[]{:S(2)}, u32[]{:S(2)}) collective-permute-start(bf16[768,1024]{1,0:T(8,128)(2,1)} %fusion.79), channel_id=1, source_target_pairs={{0,4},{4,0},{8,12},{12,8},{16,20},{20,16},{24,28},{28,24},{1,5},{5... | collective-permute-start | bytes 4718600 | tf_op jit(solution)/shard_map/ppermute | solution.py:462
  565.1 21.4 %collective-permute-start.30 = (bf16[768,512]{1,0:T(8,128)(2,1)}, bf16[768,512]{1,0:T(8,128)(2,1)}, u32[]{:S(2)}, u32[]{:S(2)}) collective-permute-start(bf16[768,512]{1,0:T(8,128)(2,1)} %slice.3191), channel_id=1, source_target_pairs={{0,16},{4,20},{8,24},{12,28},{16,0},{20,4},{24,8},{28,12},{1,17},{... | collective-permute-start | bytes 2359304 | tf_op jit(solution)/shard_map/ppermute | solution.py:462
  566.6 19.9 %collective-permute-start.29 = (bf16[704,512]{1,0:T(8,128)(2,1)}, bf16[704,512]{1,0:T(8,128)(2,1)}, u32[]{:S(2)}, u32[]{:S(2)}) collective-permute-start(bf16[704,512]{1,0:T(8,128)(2,1)} %slice.3196), channel_id=1, source_target_pairs={{0,8},{4,12},{8,0},{12,4},{16,24},{20,28},{24,16},{28,20},{1,9},{5... | collective-permute-start | bytes 2162696 | tf_op jit(solution)/shard_map/ppermute | solution.py:462
  588.1 16.4 %collective-permute-start.33 = (bf16[768,256]{1,0:T(8,128)(2,1)S(1)}, bf16[768,256]{1,0:T(8,128)(2,1)S(1)}, u32[]{:S(2)}, u32[]{:S(2)}) collective-permute-start(bf16[768,256]{1,0:T(8,128)(2,1)S(1)} %slice.3199), channel_id=1, source_target_pairs={{0,8},{4,12},{8,0},{12,4},{16,24},{20,28},{24,16},{28,20},{1,9},{5... | collective-permute-start | bytes 1179656 | tf_op jit(solution)/shard_map/ppermute | solution.py:462
  605.5 15.2 %collective-permute-start.35 = (bf16[768,256]{1,0:T(8,128)(2,1)S(1)}, bf16[768,256]{1,0:T(8,128)(2,1)}, u32[]{:S(2)}, u32[]{:S(2)}) collective-permute-start(bf16[768,256]{1,0:T(8,128)(2,1)S(1)} %fusion.107), channel_id=1, source_target_pairs={{0,8},{4,12},{8,0},{12,4},{16,24},{20,28},{24,16},{28,20},{1,9},{5... | collective-permute-start | bytes 1179656 | tf_op jit(solution)/shard_map/ppermute | solution.py:462
  609.1 13.8 %collective-permute-start.37 = (bf16[384,1024]{1,0:T(8,128)(2,1)}, bf16[384,1024]{1,0:T(8,128)(2,1)}, u32[]{:S(2)}, u32[]{:S(2)}) collective-permute-start(bf16[384,1024]{1,0:T(8,128)(2,1)} %fusion.89), channel_id=1, source_target_pairs={{0,4},{4,0},{8,12},{12,8},{16,20},{20,16},{24,28},{28,24},{1,5},{5... | collective-permute-start | bytes 2359304 | tf_op jit(solution)/shard_map/ppermute | solution.py:462
  609.4 17.7 %collective-permute-start.36 = (bf16[384,1024]{1,0:T(8,128)(2,1)}, bf16[384,1024]{1,0:T(8,128)(2,1)}, u32[]{:S(2)}, u32[]{:S(2)}) collective-permute-start(bf16[384,1024]{1,0:T(8,128)(2,1)} %fusion.92), channel_id=1, source_target_pairs={{0,4},{4,0},{8,12},{12,8},{16,20},{20,16},{24,28},{28,24},{1,5},{5... | collective-permute-start | bytes 2359304 | tf_op jit(solution)/shard_map/ppermute | solution.py:462
  630.4 23.6 %collective-permute-start.42 = (bf16[384,512]{1,0:T(8,128)(2,1)}, bf16[384,512]{1,0:T(8,128)(2,1)}, u32[]{:S(2)}, u32[]{:S(2)}) collective-permute-start(bf16[384,512]{1,0:T(8,128)(2,1)} %slice.3197), channel_id=1, source_target_pairs={{0,16},{4,20},{8,24},{12,28},{16,0},{20,4},{24,8},{28,12},{1,17},{... | collective-permute-start | bytes 1179656 | tf_op jit(solution)/shard_map/ppermute | solution.py:462
  632.1 24.8 %collective-permute-start.38 = (bf16[384,512]{1,0:T(8,128)(2,1)}, bf16[384,512]{1,0:T(8,128)(2,1)}, u32[]{:S(2)}, u32[]{:S(2)}) collective-permute-start(bf16[384,512]{1,0:T(8,128)(2,1)} %slice.3198), channel_id=1, source_target_pairs={{0,8},{4,12},{8,0},{12,4},{16,24},{20,28},{24,16},{28,20},{1,9},{5... | collective-permute-start | bytes 1179656 | tf_op jit(solution)/shard_map/ppermute | solution.py:462
  635.1 42.0 %collective-permute-start.52 = (bf16[768,512]{1,0:T(8,128)(2,1)}, bf16[768,512]{1,0:T(8,128)(2,1)}, u32[]{:S(2)}, u32[]{:S(2)}) collective-permute-start(bf16[768,512]{1,0:T(8,128)(2,1)} %pad_maximum_fusion.43), channel_id=1, source_target_pairs={{0,16},{4,20},{8,24},{12,28},{16,0},{20,4},{24,8},{28,12},{1,17},{... | collective-permute-start | bytes 2359304 | tf_op jit(solution)/shard_map/ppermute | solution.py:462
  636.8 39.0 %collective-permute-start.50 = (bf16[704,512]{1,0:T(8,128)(2,1)}, bf16[704,512]{1,0:T(8,128)(2,1)}, u32[]{:S(2)}, u32[]{:S(2)}) collective-permute-start(bf16[704,512]{1,0:T(8,128)(2,1)} %pad_maximum_fusion.46), channel_id=1, source_target_pairs={{0,8},{4,12},{8,0},{12,4},{16,24},{20,28},{24,16},{28,20},{1,9},{5... | collective-permute-start | bytes 2162696 | tf_op jit(solution)/shard_map/ppermute | solution.py:462
  663.0 18.3 %collective-permute-start.44 = (bf16[384,256]{1,0:T(8,128)(2,1)S(1)}, bf16[384,256]{1,0:T(8,128)(2,1)S(1)}, u32[]{:S(2)}, u32[]{:S(2)}) collective-permute-start(bf16[384,256]{1,0:T(8,128)(2,1)S(1)} %fusion.123), channel_id=1, source_target_pairs={{0,8},{4,12},{8,0},{12,4},{16,24},{20,28},{24,16},{28,20},{1,9},{5... | collective-permute-start | bytes 589832 | tf_op jit(solution)/shard_map/ppermute | solution.py:462
  665.9 15.5 %collective-permute-start.40 = (bf16[384,256]{1,0:T(8,128)(2,1)S(1)}, bf16[384,256]{1,0:T(8,128)(2,1)S(1)}, u32[]{:S(2)}, u32[]{:S(2)}) collective-permute-start(bf16[384,256]{1,0:T(8,128)(2,1)S(1)} %fusion.124), channel_id=1, source_target_pairs={{0,16},{4,20},{8,24},{12,28},{16,0},{20,4},{24,8},{28,12},{1,17},{... | collective-permute-start | bytes 589832 | tf_op jit(solution)/shard_map/ppermute | solution.py:462
  694.1 13.6 %collective-permute-start.54 = (bf16[384,1024]{1,0:T(8,128)(2,1)S(1)}, bf16[384,1024]{1,0:T(8,128)(2,1)S(1)}, u32[]{:S(2)}, u32[]{:S(2)}) collective-permute-start(bf16[384,1024]{1,0:T(8,128)(2,1)S(1)} %pad_maximum_fusion.44.refs_3_), channel_id=1, source_target_pairs={{0,4},{4,0},{8,12},{12,8},{16,20},{20,16},{24,28},{28,24},{1,5},{5... | collective-permute-start | bytes 2359304 | tf_op jit(solution)/shard_map/ppermute | solution.py:462
  (162 other events, 1179.8 us)
Sparse Core Ops, SparseCore 0:
  10.3 83.4 all-gather.5
  97.0 33.4 all-gather.7
  155.5 106.7 all-gather.9
  337.9 76.9 reduce-scatter.3
  419.1 81.2 all-gather.11
  503.3 75.2 reduce-scatter.5
  623.0 75.7 reduce-scatter.7

commit v4 on v3

--- a/solution.py
+++ b/solution.py
@@ -764,10 +764,9 @@
     before = shifted(last[:, 7], "seq", 1)
     prev = jnp.concatenate([before[:, None], last[:, :7]], axis=1).reshape(8 * halo, padded)
     over_tp = lax.all_gather(own_rows, "tp", axis=0, tiled=True)
-    both, *second = lax.optimization_barrier((both, *second))
     conv, low, r, i, local, reach = forward_recurrence(both, prev, masks, params, gates)
     ends = jnp.stack([reach[tokens - 8 :], local[tokens - 8 :]])
-    ends, over_tp = lax.optimization_barrier((ends, over_tp))
+    ends, over_tp, *second = lax.optimization_barrier((ends, over_tp, *second))
     ends = lax.all_gather(ends, "seq", axis=0)
     incoming = chained(ends[:, 0], ends[:, 1], seq_place, False)
     steps = lambda a: a.reshape(tokens // 8, 8, padded)

time: 739 us -> 735 us (level)
    unnamed x292 -> x300, local copies, waits for them, and re-layouts: 47.8 us -> 46.4 us
  transfers between devices with their start and end apart: 67 -> 67, of which waited for: 16 -> 17; matrix products, arithmetic and copies ran while one was open for 35% -> 35% of each run, Pallas kernels for 13% -> 13%
where the time goes in v4:
time: 735 us; the launch traced here: 726 us
  matrix products  145 us (20%)
  waiting for transfers between devices  144 us (20%)
  Pallas kernels  125 us (17%)
  local copies, waits for them, and re-layouts  120 us (16%)
  other arithmetic  82.7 us (11%)
  starting transfers between devices  56.8 us (8%)
  blocking collectives  35.2 us (5%)
  between operations  17.6 us (2%)
    ppermute x56, waiting for transfers between devices, across(): return lax.ppermute(x, axis, [(i, i ^ 1 << bit) for i in range(n)])  94.6 us
    dot_general x17, matrix products, contract_first(): lax.dot_general(left, right, (((0,), (0,)), ((), ())), preferred_element_...  68.6 us
    ppermute x56, starting transfers between devices, across(): return lax.ppermute(x, axis, [(i, i ^ 1 << bit) for i in range(n)])  48.9 us
    unnamed x300, local copies, waits for them, and re-layouts  46.4 us
    pallas_call x4, Pallas kernels, picked(): pl.pallas_call(kernel, name=name, grid_spec=pltpu.PrefetchScalarGridSpec(...  44.9 us
    dot_general x4, matrix products, contract_last(): lax.dot_general(left, right, (((1,), (1,)), ((), ())), preferred_element_...  42.7 us
    all_gather x2, waiting for transfers between devices, gather_features(): return lax.all_gather(x, 'tp', axis=1, tiled=True)  33.1 us
    dot_general x2, matrix products, dot(): return jnp.dot(left, right, preferred_element_type=F32)  29.1 us
  transfers between devices with their start and end apart: 67, of which 17 were waited for; matrix products, arithmetic and copies ran while one was open for 35% of the time, Pallas kernels for 13%

profile of v4, /device:TPU:0, one launch (start us, length us, event | category | flops | bytes accessed | tf_op | source)
XLA Modules:
  0.0 726.4 jit_solution(13039535807018877339)
XLA Ops:
  17.3 22.5 %collective-permute-done.1 = bf16[1,384,1536]{2,1,0:T(8,128)(2,1)} collective-permute-done((bf16[1,384,1536]{2,1,0:T(8,128)(2,1)S(1)}, bf16[1,384,1536]{2,1,0:T(8,128)(2,1)}, u32[]{:S(2)}, u32[]{:S(2)}) %collective-permute-start.1) | collective-permute-done | bytes 1179680 | tf_op jit(solution)/shard_map/ppermute | solution.py:462
  58.7 4.3 copy.98
  71.6 3.8 pad_maximum_fusion
  77.8 15.9 %all-gather.6.cloned.1.call-done = bf16[1024,2048]{1,0:T(8,128)(2,1)} async-done(((bf16[1024,512]{1,0:T(8,128)(2,1)}), bf16[1024,2048]{1,0:T(8,128)(2,1)}) %all-gather.6.cloned.1.call-update) | async-done | bytes 4194320 | tf_op jit(solution)/shard_map/all_gather | solution.py:674
  100.4 10.4 %fusion.388.bx_ref.by_ref.bx_before_ref = f32[1024,1536]{1,0:T(8,128)S(1)} fusion(bf16[1024,2048]{1,0:T(8,128)(2,1)S(1)} %fusion.2, bf16[1536,2048]{1,0:T(8,128)(2,1)} %pad_maximum_fusion), kind=kOutput, calls=%fused_computation.852 | convolution fusion | flops 6442450944 | bytes 16777216 | tf_op jit(solution)/shard_map/dot_general | solution.py:30
  116.7 12.0 %forward_recurrence.1 = (f32[1024,768]{1,0:T(8,128)}, bf16[1024,768]{1,0:T(8,128)(2,1)}, f32[1024,768]{1,0:T(8,128)}, f32[1024,768]{1,0:T(8,128)}, f32[1024,768]{1,0:T(8,128)}, /*index=5*/f32[1024,768]{1,0:T(8,128)}) custom-call(f32[1024,1536]{1,0:T(8,128)} %copy-done.21, f32[24,768]{1,0:T(8,128)} %maximum_bitcast_fusion.3.prev_ref, f32[1024,8]{1,0:T(8,128)} %bitcast.1898, ...), custom_call_target="tpu_custom_call" | custom-call | flops 2415919104 | bytes 23592960 | tf_op jit(solution)/shard_map/forward_recurrence/pallas_call | solution.py:123
  130.5 12.6 %all-gather = f32[16,8,768]{2,1,0:T(8,128)S(1)} all-gather(f32[2,8,768]{2,1,0:T(8,128)S(1)} %pad_maximum_fusion.55), channel_id=2, replica_groups=mesh['seq'=8,'tp'=4] {'seq'}, dimensions={0}, use_global_device_ids=true | all-gather | bytes 442368 | tf_op jit(solution)/shard_map/all_gather | solution.py:770
  143.8 3.2 fusion.8.state_ref.before_ref
  148.8 4.0 fusion.7
  155.4 3.2 constant_dynamic-update-slice_fusion.3
  158.6 3.2 constant_dynamic-update-slice_fusion.2.refs_4_
  162.2 3.5 constant_dynamic-update-slice_fusion.1
  165.7 3.5 constant_dynamic-update-slice_fusion.refs_2_
  171.5 16.5 %collective-permute-done.11 = bf16[1,4,88,1024]{3,2,1,0:T(8,128)(2,1)S(1)} collective-permute-done((bf16[1,4,88,1024]{3,2,1,0:T(8,128)(2,1)S(1)}, bf16[1,4,88,1024]{3,2,1,0:T(8,128)(2,1)S(1)}, u32[]{:S(2)}, u32[]{:S(2)}) %collective-permute-start.11) | collective-permute-done | bytes 720928 | tf_op jit(solution)/shard_map/ppermute | solution.py:462
  190.3 31.0 %collective-permute-done.12 = bf16[2,4,88,1024]{3,2,1,0:T(8,128)(2,1)S(1)} collective-permute-done((bf16[2,4,88,1024]{3,2,1,0:T(8,128)(2,1)S(1)}, bf16[2,4,88,1024]{3,2,1,0:T(8,128)(2,1)S(1)}, u32[]{:S(2)}, u32[]{:S(2)}) %collective-permute-start.12) | collective-permute-done | bytes 1441824 | tf_op jit(solution)/shard_map/ppermute | solution.py:462
  225.7 18.6 %mlp_weights.1 = (bf16[8,256,1536]{2,1,0:T(8,128)(2,1)}, bf16[8,256,1536]{2,1,0:T(8,128)(2,1)}, bf16[8,2,128,1536]{3,2,1,0:T(8,128)(2,1)}) custom-call(s32[8]{0:T(128)S(1)} %get-tuple-element.508.refs_0_.refs_1_.refs_2_, s32[8]{0:T(128)S(1)} %get-tuple-element.507.refs_1_.refs_0_, bf16[4,384,1536]{2,1,0:T(8,128)(2,1)} %constant_dynamic-update-slice_fusion.refs_2_, ...), custom_call_target="tpu_custom_call" | custom-call | bytes 56623104 | tf_op jit(solution)/shard_map/mlp_weights/pallas_call | solution.py:528
  244.3 10.4 %fusion.389.d_hid_ref = f32[1024,1536]{1,0:T(8,128)} fusion(bf16[1024,2048]{1,0:T(8,128)(2,1)S(1)} %bitcast.1896, bf16[2048,1536]{1,0:T(8,128)(2,1)} %bitcast.1935), kind=kOutput, calls=%fused_computation.853 | convolution fusion | flops 6442450944 | bytes 16777216 | tf_op jit(solution)/shard_map/dot_general | solution.py:22
  254.8 12.8 %output_rows.1 = bf16[4,8,88,2048]{3,2,1,0:T(8,128)(2,1)} custom-call(s32[8]{0:T(128)S(1)} %get-tuple-element.508.refs_0_.refs_1_.refs_2_, s32[8]{0:T(128)S(1)} %get-tuple-element.507.refs_1_.refs_0_, bf16[4,4,88,1024]{3,2,1,0:T(8,128)(2,1)} %pad_maximum_fusion.1.refs_2_, bf16[4,4,88,1024]{3,2,1,0:T(8,128)(2,1)} %collective-permute-done.10.refs_3_, ...), custom_call_target="tpu_custom_call" | custom-call | bytes 34603008 | tf_op jit(solution)/shard_map/output_rows/pallas_call | solution.py:528
  267.6 18.7 %multiply_reduce_fusion = (f32[1024]{0:T(1024)S(1)}, f32[1024,2048]{1,0:T(8,128)S(1)}) fusion(bf16[1024,2816]{0,1:T(8,128)(2,1)} %all-gather.10.cloned.1.call-done, bf16[2816,2048]{1,0:T(8,128)(2,1)} %bitcast.1897, bf16[1024,2048]{1,0:T(8,128)(2,1)} %all-gather.6.cloned.1.call-done), kind=kOutput, calls=%fused_computation.9 | convolution fusion | flops 11819547648 | bytes 29888512 | tf_op jit(solution)/shard_map/dot_general | solution.py:22
  290.7 23.4 %mlp_units.1 = (bf16[1024,1536]{1,0:T(8,128)(2,1)S(1)}, bf16[1024,1536]{1,0:T(8,128)(2,1)}, bf16[1024,1536]{1,0:T(8,128)(2,1)}, f32[1024,128]{1,0:T(8,128)S(1)}) custom-call(bf16[1024,2048]{1,0:T(8,128)(2,1)} %multiply_convert_fusion.n2_ref, bf16[2048,1536]{1,0:T(8,128)(2,1)} %bitcast.1943, bf16[2048,1536]{1,0:T(8,128)(2,1)} %bitcast.1939, ...), custom_call_target="tpu_custom_call" | custom-call | flops 12884901888 | bytes 32505856 | tf_op jit(solution)/shard_map/mlp_units/pallas_call | solution.py:401
  314.1 13.1 %fusion.390 = f32[1024,2048]{1,0:T(8,128)} fusion(bf16[1024,1536]{1,0:T(8,128)(2,1)} %get-tuple-element.206, bf16[2048,1536]{1,0:T(8,128)(2,1)} %bitcast.1944), kind=kOutput, calls=%fused_computation.854 | convolution fusion | flops 6442450944 | bytes 17825792 | tf_op jit(solution)/shard_map/dot_general | solution.py:30
  327.3 10.4 %add_convert_fusion = bf16[1024,2048]{1,0:T(8,128)(2,1)} fusion(f32[1024,2048]{1,0:T(8,128)} %fusion.390, bf16[1024,1536]{1,0:T(8,128)(2,1)S(1)} %copy-done.130, bf16[2048,1536]{1,0:T(8,128)(2,1)S(1)} %bitcast.1942), kind=kOutput, calls=%fused_computation.7 | convolution fusion | flops 6446645248 | bytes 22020096 | tf_op jit(solution)/shard_map/dot_general | solution.py:30
  337.8 3.8 constant_dynamic-slice_fusion.44
  347.3 5.4 convolution_convert_fusion.1
  352.7 5.1 convolution_convert_fusion.2
  362.7 12.9 %psum.7 = f32[1024]{0:T(1024)} all-reduce(f32[1024]{0:T(1024)S(1)} %reduce_sum.65), channel_id=1, replica_groups=mesh['seq'=8,'tp'=4] {'tp'}, use_global_device_ids=true, to_apply=%region_4.5 | all-reduce | flops 1024 | bytes 8192 | tf_op jit(solution)/shard_map/psum | solution.py:804
  375.7 6.2 convert_add_fusion.6
  382.0 5.1 convert_add_fusion.7
  387.1 7.2 convert_add_fusion.1
  394.3 7.1 convert_add_fusion.2
  401.4 13.5 %reduce-scatter.4.cloned.1.call-done = bf16[1024,512]{1,0:T(8,128)(2,1)} async-done(((bf16[1024,2048]{1,0:T(8,128)(2,1)}), bf16[1024,512]{1,0:T(8,128)(2,1)}) %reduce-scatter.4.cloned.1.call-update) | async-done | bytes 1048592 | tf_op jit(solution)/shard_map/reduce_scatter | solution.py:678
  427.2 3.7 slice.3190
  440.8 8.7 %convolution_convert_fusion = bf16[1024,2048]{1,0:T(8,128)(2,1)} fusion(bf16[1024,1536]{1,0:T(8,128)(2,1)S(1)} %copy-done.20, bf16[2048,1536]{1,0:T(8,128)(2,1)S(1)} %bitcast.1938), kind=kOutput, calls=%fused_computation.20 | convolution fusion | flops 6444548096 | bytes 13631488 | tf_op jit(solution)/shard_map/dot_general | solution.py:30
  451.8 4.6 fusion.119
  467.4 7.8 %collective-permute-done.20 = bf16[512,1536]{1,0:T(8,128)(2,1)} collective-permute-done((bf16[512,1536]{1,0:T(8,128)(2,1)}, bf16[512,1536]{1,0:T(8,128)(2,1)}, u32[]{:S(2)}, u32[]{:S(2)}) %collective-permute-start.20) | collective-permute-done | bytes 1572896 | tf_op jit(solution)/shard_map/ppermute | solution.py:462
  483.3 17.1 %all-gather.12.cloned.1.call-done.scaled_ref = bf16[1024,2048]{1,0:T(8,128)(2,1)} async-done(((bf16[1024,512]{1,0:T(8,128)(2,1)}), bf16[1024,2048]{1,0:T(8,128)(2,1)}) %all-gather.12.cloned.1.call-update) | async-done | bytes 4194320 | tf_op jit(solution)/shard_map/all_gather | solution.py:674
  507.5 18.1 %reverse_recurrence.1 = (bf16[1024,2048]{1,0:T(8,128)(2,1)}, f32[1024,768]{1,0:T(8,128)}, f32[1024,768]{1,0:T(8,128)}, bf16[1024,768]{1,0:T(8,128)(2,1)}, f32[16,768]{1,0:T(8,128)}) custom-call(bf16[1024,2048]{1,0:T(8,128)(2,1)} %bitcast.1894, bf16[1024,2048]{1,0:T(8,128)(2,1)} %all-gather.12.cloned.1.call-done.scaled_ref, ...), custom_call_target="tpu_custom_call" | custom-call | flops 3221225472 | bytes 35651584 | tf_op jit(solution)/shard_map/reverse_recurrence/pallas_call | solution.py:188
  534.8 3.5 fusion.69
  538.4 3.3 fusion.54
  541.8 9.7 %all_gather.27 = f32[8,2,8,768]{3,2,1,0:T(8,128)S(1)} all-gather(f32[1,2,8,768]{3,2,1,0:T(8,128)S(1)} %bitcast.1922), channel_id=1, replica_groups=mesh['seq'=8,'tp'=4] {'seq'}, dimensions={0}, use_global_device_ids=true | all-gather | bytes 442368 | tf_op jit(solution)/shard_map/all_gather | solution.py:871
  566.1 17.8 %gate_gradients.1 = (bf16[1024,768]{1,0:T(8,128)(2,1)}, f32[32,768]{1,0:T(8,128)}, f32[24,768]{1,0:T(8,128)}, f32[64,768]{1,0:T(8,128)}, bf16[1024,1536]{1,0:T(8,128)(2,1)}) custom-call(f32[1024,768]{1,0:T(8,128)} %get-tuple-element.232.grad_ref, f32[1024,768]{1,0:T(8,128)} %get-tuple-element.233.reach_ref, f32[1024,768]{1,0:T(8,128)} %get-tuple-element.231.r_ref, ...), custom_call_target="tpu_custom_call" | custom-call | flops 2415919104 | bytes 26738688 | tf_op jit(solution)/shard_map/gate_gradients/pallas_call | solution.py:307
  594.8 3.9 fusion.87
  607.1 7.4 %pair_product.1 = bf16[1024,2048]{1,0:T(8,128)(2,1)S(1)} custom-call(bf16[1024,768]{1,0:T(8,128)(2,1)S(1)} %copy-done.4, bf16[1024,768]{1,0:T(8,128)(2,1)S(1)} %copy-done.16, bf16[768,2048]{1,0:T(8,128)(2,1)S(1)} %pad.68.over_ref, bf16[768,2048]{1,0:T(8,128)(2,1)S(1)} %copy-done.3), custom_call_target="tpu_custom_call" | custom-call | flops 6442450944 | bytes 13631488 | tf_op jit(solution)/shard_map/pair_product/pallas_call | solution.py:431
  645.2 4.7 collective-permute-done.47
  663.7 3.9 collective-permute-done.49
  682.5 6.8 early_gradients.1
  698.7 3.5 fusion.104
  707.6 6.6 last_gradients.1
  (611 shorter events, 254.2 us)
Async XLA Ops:
  7.2 86.6 %all-gather.6.cloned.1.call-start = ((), (), s32[]{:S(2)}) async-start(), calls=%async_computation.3 | async-start | bytes 5242880 | tf_op jit(solution)/shard_map/all_gather | solution.py:674
  10.2 120.4 %all-gather.8.cloned.1.call-start = ((), (), s32[]{:S(2)}) async-start(), calls=%async_computation.4 | async-start | bytes 1802240 | tf_op jit(solution)/shard_map/all_gather | solution.py:766
  10.7 29.1 %collective-permute-start.1 = (bf16[1,384,1536]{2,1,0:T(8,128)(2,1)S(1)}, bf16[1,384,1536]{2,1,0:T(8,128)(2,1)}, u32[]{:S(2)}, u32[]{:S(2)}) collective-permute-start(bf16[1,384,1536]{2,1,0:T(8,128)(2,1)S(1)} %maximum_bitcast_fusion.2), channel_id=1, source_target_pairs={{0,16},{4,20},{8,24},{12,28},{16,0},{20,4},{24,8},{28,12},{1,17},{... | collective-permute-start | bytes 3538952 | tf_op jit(solution)/shard_map/ppermute | solution.py:462
  15.0 27.8 %collective-permute-start = (bf16[1,384,1536]{2,1,0:T(8,128)(2,1)S(1)}, bf16[1,384,1536]{2,1,0:T(8,128)(2,1)}, u32[]{:S(2)}, u32[]{:S(2)}) collective-permute-start(bf16[1,384,1536]{2,1,0:T(8,128)(2,1)S(1)} %maximum_bitcast_fusion.1), channel_id=1, source_target_pairs={{0,8},{4,12},{8,0},{12,4},{16,24},{20,28},{24,16},{28,20},{1,9},{5... | collective-permute-start | bytes 3538952 | tf_op jit(solution)/shard_map/ppermute | solution.py:462
  46.5 28.9 %collective-permute-start.18 = (f32[1]{0:T(128)}, f32[1]{0:T(128)}, u32[]{:S(2)}, u32[]{:S(2)}) collective-permute-start(f32[1]{0:T(128)} %slice.1434), channel_id=1, source_target_pairs={{4,0},{8,4},{12,8},{16,12},{20,16},{24,20},{28,24},{5,1},{9,5},{13... | collective-permute-start | bytes 20 | tf_op jit(solution)/shard_map/ppermute | solution.py:451
  47.7 29.0 %collective-permute-start.2 = (f32[3]{0:T(128)S(1)}, f32[3]{0:T(128)S(1)}, u32[]{:S(2)}, u32[]{:S(2)}) collective-permute-start(f32[3]{0:T(128)S(1)} %slice.1290), channel_id=1, source_target_pairs={{0,4},{4,8},{8,12},{12,16},{16,20},{20,24},{24,28},{1,5},{5,9},{9,... | collective-permute-start | bytes 44 | tf_op jit(solution)/shard_map/ppermute | solution.py:451
  63.1 67.2 %collective-permute-start.4 = (bf16[2,384,1536]{2,1,0:T(8,128)(2,1)}, bf16[2,384,1536]{2,1,0:T(8,128)(2,1)}, u32[]{:S(2)}, u32[]{:S(2)}) collective-permute-start(bf16[2,384,1536]{2,1,0:T(8,128)(2,1)} %pad_maximum_fusion.19), channel_id=1, source_target_pairs={{0,16},{4,20},{8,24},{12,28},{16,0},{20,4},{24,8},{28,12},{1,17},{... | collective-permute-start | bytes 7077896 | tf_op jit(solution)/shard_map/ppermute | solution.py:462
  64.8 65.4 %collective-permute-start.5 = (bf16[2,384,1536]{2,1,0:T(8,128)(2,1)}, bf16[2,384,1536]{2,1,0:T(8,128)(2,1)}, u32[]{:S(2)}, u32[]{:S(2)}) collective-permute-start(bf16[2,384,1536]{2,1,0:T(8,128)(2,1)} %pad_maximum_fusion.20), channel_id=1, source_target_pairs={{0,8},{4,12},{8,0},{12,4},{16,24},{20,28},{24,16},{28,20},{1,9},{5... | collective-permute-start | bytes 7077896 | tf_op jit(solution)/shard_map/ppermute | solution.py:462
  96.9 170.7 %all-gather.10.cloned.1.call-start = ((), (), s32[]{:S(2)}) async-start(), calls=%async_computation.5 | async-start | bytes 7208960 | tf_op jit(solution)/shard_map/all_gather | solution.py:775
  155.4 259.5 %reduce-scatter.4.cloned.1.call-start = ((), (), s32[]{:S(2)}) async-start(), calls=%async_computation.6 | async-start | bytes 5242880 | tf_op jit(solution)/shard_map/reduce_scatter | solution.py:678
  161.9 63.8 %collective-permute-start.7 = (bf16[4,384,1536]{2,1,0:T(8,128)(2,1)}, bf16[4,384,1536]{2,1,0:T(8,128)(2,1)}, u32[]{:S(2)}, u32[]{:S(2)}) collective-permute-start(bf16[4,384,1536]{2,1,0:T(8,128)(2,1)} %constant_dynamic-update-slice_fusion.2.refs_4_), channel_id=1, source_target_pairs={{0,4},{4,0},{8,12},{12,8},{16,20},{20,16},{24,28},{28,24},{1,5},{5... | collective-permute-start | bytes 14155784 | tf_op jit(solution)/shard_map/ppermute | solution.py:462
  169.3 56.4 %collective-permute-start.6 = (bf16[4,384,1536]{2,1,0:T(8,128)(2,1)}, bf16[4,384,1536]{2,1,0:T(8,128)(2,1)}, u32[]{:S(2)}, u32[]{:S(2)}) collective-permute-start(bf16[4,384,1536]{2,1,0:T(8,128)(2,1)} %constant_dynamic-update-slice_fusion.refs_2_), channel_id=1, source_target_pairs={{0,4},{4,0},{8,12},{12,8},{16,20},{20,16},{24,28},{28,24},{1,5},{5... | collective-permute-start | bytes 14155784 | tf_op jit(solution)/shard_map/ppermute | solution.py:462
  169.5 18.5 %collective-permute-start.11 = (bf16[1,4,88,1024]{3,2,1,0:T(8,128)(2,1)S(1)}, bf16[1,4,88,1024]{3,2,1,0:T(8,128)(2,1)S(1)}, u32[]{:S(2)}, u32[]{:S(2)}) collective-permute-start(bf16[1,4,88,1024]{3,2,1,0:T(8,128)(2,1)S(1)} %get-tuple-element.472), channel_id=1, source_target_pairs={{0,16},{4,20},{8,24},{12,28},{16,0},{20,4},{24,8},{28,12},{1,17},{... | collective-permute-start | bytes 2162696 | tf_op jit(solution)/shard_map/ppermute | solution.py:462
  170.1 18.6 %collective-permute-start.8 = (bf16[1,4,88,1024]{3,2,1,0:T(8,128)(2,1)S(1)}, bf16[1,4,88,1024]{3,2,1,0:T(8,128)(2,1)S(1)}, u32[]{:S(2)}, u32[]{:S(2)}) collective-permute-start(bf16[1,4,88,1024]{3,2,1,0:T(8,128)(2,1)S(1)} %get-tuple-element.473), channel_id=1, source_target_pairs={{0,8},{4,12},{8,0},{12,4},{16,24},{20,28},{24,16},{28,20},{1,9},{5... | collective-permute-start | bytes 2162696 | tf_op jit(solution)/shard_map/ppermute | solution.py:462
  188.1 33.2 %collective-permute-start.12 = (bf16[2,4,88,1024]{3,2,1,0:T(8,128)(2,1)S(1)}, bf16[2,4,88,1024]{3,2,1,0:T(8,128)(2,1)S(1)}, u32[]{:S(2)}, u32[]{:S(2)}) collective-permute-start(bf16[2,4,88,1024]{3,2,1,0:T(8,128)(2,1)S(1)} %pad_maximum_fusion.42), channel_id=1, source_target_pairs={{0,8},{4,12},{8,0},{12,4},{16,24},{20,28},{24,16},{28,20},{1,9},{5... | collective-permute-start | bytes 4325384 | tf_op jit(solution)/shard_map/ppermute | solution.py:462
  188.9 34.4 %collective-permute-start.9 = (bf16[2,4,88,1024]{3,2,1,0:T(8,128)(2,1)S(1)}, bf16[2,4,88,1024]{3,2,1,0:T(8,128)(2,1)S(1)}, u32[]{:S(2)}, u32[]{:S(2)}) collective-permute-start(bf16[2,4,88,1024]{3,2,1,0:T(8,128)(2,1)S(1)} %pad_maximum_fusion.41), channel_id=1, source_target_pairs={{0,16},{4,20},{8,24},{12,28},{16,0},{20,4},{24,8},{28,12},{1,17},{... | collective-permute-start | bytes 4325384 | tf_op jit(solution)/shard_map/ppermute | solution.py:462
  223.2 31.6 %collective-permute-start.13 = (bf16[4,4,88,1024]{3,2,1,0:T(8,128)(2,1)}, bf16[4,4,88,1024]{3,2,1,0:T(8,128)(2,1)}, u32[]{:S(2)}, u32[]{:S(2)}) collective-permute-start(bf16[4,4,88,1024]{3,2,1,0:T(8,128)(2,1)} %pad_maximum_fusion.2.refs_4_), channel_id=1, source_target_pairs={{0,4},{4,0},{8,12},{12,8},{16,20},{20,16},{24,28},{28,24},{1,5},{5... | collective-permute-start | bytes 8650760 | tf_op jit(solution)/shard_map/ppermute | solution.py:462
  225.2 29.6 %collective-permute-start.10 = (bf16[4,4,88,1024]{3,2,1,0:T(8,128)(2,1)}, bf16[4,4,88,1024]{3,2,1,0:T(8,128)(2,1)}, u32[]{:S(2)}, u32[]{:S(2)}) collective-permute-start(bf16[4,4,88,1024]{3,2,1,0:T(8,128)(2,1)} %pad_maximum_fusion.1.refs_2_), channel_id=1, source_target_pairs={{0,4},{4,0},{8,12},{12,8},{16,20},{20,16},{24,28},{28,24},{1,5},{5... | collective-permute-start | bytes 8650760 | tf_op jit(solution)/shard_map/ppermute | solution.py:462
  337.7 162.7 %all-gather.12.cloned.1.call-start = ((), (), s32[]{:S(2)}) async-start(), calls=%async_computation.7 | async-start | bytes 5242880 | tf_op jit(solution)/shard_map/all_gather | solution.py:674
  344.7 31.0 %collective-permute-start.17 = (bf16[1024,768]{1,0:T(8,128)(2,1)}, bf16[1024,768]{1,0:T(8,128)(2,1)}, u32[]{:S(2)}, u32[]{:S(2)}) collective-permute-start(bf16[1024,768]{1,0:T(8,128)(2,1)} %fusion.82), channel_id=1, source_target_pairs={{0,4},{4,0},{8,12},{12,8},{16,20},{20,16},{24,28},{28,24},{1,5},{5... | collective-permute-start | bytes 4718600 | tf_op jit(solution)/shard_map/ppermute | solution.py:462
  352.7 34.3 %collective-permute-start.15 = (bf16[1024,1536]{1,0:T(8,128)(2,1)}, bf16[1024,1536]{1,0:T(8,128)(2,1)}, u32[]{:S(2)}, u32[]{:S(2)}) collective-permute-start(bf16[1024,1536]{1,0:T(8,128)(2,1)} %convolution_convert_fusion.1), channel_id=1, source_target_pairs={{0,4},{4,0},{8,12},{12,8},{16,20},{20,16},{24,28},{28,24},{1,5},{5... | collective-permute-start | bytes 9437192 | tf_op jit(solution)/shard_map/ppermute | solution.py:462
  357.8 36.4 %collective-permute-start.14 = (bf16[1024,1536]{1,0:T(8,128)(2,1)}, bf16[1024,1536]{1,0:T(8,128)(2,1)}, u32[]{:S(2)}, u32[]{:S(2)}) collective-permute-start(bf16[1024,1536]{1,0:T(8,128)(2,1)} %convolution_convert_fusion.2), channel_id=1, source_target_pairs={{0,4},{4,0},{8,12},{12,8},{16,20},{20,16},{24,28},{28,24},{1,5},{5... | collective-permute-start | bytes 9437192 | tf_op jit(solution)/shard_map/ppermute | solution.py:462
  361.4 20.5 %collective-permute-start.16 = (bf16[1024,768]{1,0:T(8,128)(2,1)}, bf16[1024,768]{1,0:T(8,128)(2,1)}, u32[]{:S(2)}, u32[]{:S(2)}) collective-permute-start(bf16[1024,768]{1,0:T(8,128)(2,1)} %fusion.83), channel_id=1, source_target_pairs={{0,4},{4,0},{8,12},{12,8},{16,20},{20,16},{24,28},{28,24},{1,5},{5... | collective-permute-start | bytes 4718600 | tf_op jit(solution)/shard_map/ppermute | solution.py:462
  419.0 201.5 %reduce-scatter.6.cloned.1.call-start = ((), (), s32[]{:S(2)}) async-start(), calls=%async_computation.8 | async-start | bytes 5242880 | tf_op jit(solution)/shard_map/reduce_scatter | solution.py:840
  421.8 40.2 %collective-permute-start.22 = (bf16[512,768]{1,0:T(8,128)(2,1)}, bf16[512,768]{1,0:T(8,128)(2,1)}, u32[]{:S(2)}, u32[]{:S(2)}) collective-permute-start(bf16[512,768]{1,0:T(8,128)(2,1)} %slice.3193), channel_id=1, source_target_pairs={{0,16},{4,20},{8,24},{12,28},{16,0},{20,4},{24,8},{28,12},{1,17},{... | collective-permute-start | bytes 2359304 | tf_op jit(solution)/shard_map/ppermute | solution.py:462
  425.7 38.2 %collective-permute-start.21 = (bf16[512,768]{1,0:T(8,128)(2,1)}, bf16[512,768]{1,0:T(8,128)(2,1)}, u32[]{:S(2)}, u32[]{:S(2)}) collective-permute-start(bf16[512,768]{1,0:T(8,128)(2,1)} %slice.3194), channel_id=1, source_target_pairs={{0,8},{4,12},{8,0},{12,4},{16,24},{20,28},{24,16},{28,20},{1,9},{5... | collective-permute-start | bytes 2359304 | tf_op jit(solution)/shard_map/ppermute | solution.py:462
  430.8 44.4 %collective-permute-start.20 = (bf16[512,1536]{1,0:T(8,128)(2,1)}, bf16[512,1536]{1,0:T(8,128)(2,1)}, u32[]{:S(2)}, u32[]{:S(2)}) collective-permute-start(bf16[512,1536]{1,0:T(8,128)(2,1)} %slice.3190), channel_id=1, source_target_pairs={{0,16},{4,20},{8,24},{12,28},{16,0},{20,4},{24,8},{28,12},{1,17},{... | collective-permute-start | bytes 4718600 | tf_op jit(solution)/shard_map/ppermute | solution.py:462
  434.7 44.1 %collective-permute-start.19 = (bf16[512,1536]{1,0:T(8,128)(2,1)}, bf16[512,1536]{1,0:T(8,128)(2,1)}, u32[]{:S(2)}, u32[]{:S(2)}) collective-permute-start(bf16[512,1536]{1,0:T(8,128)(2,1)} %slice.3191), channel_id=1, source_target_pairs={{0,8},{4,12},{8,0},{12,4},{16,24},{20,28},{24,16},{28,20},{1,9},{5... | collective-permute-start | bytes 4718600 | tf_op jit(solution)/shard_map/ppermute | solution.py:462
  500.5 196.1 %reduce-scatter.8.cloned.1.call-start = ((), (), s32[]{:S(2)}) async-start(), calls=%async_computation.9 | async-start | bytes 5242880 | tf_op jit(solution)/shard_map/reduce_scatter | solution.py:678
  503.5 30.7 %collective-permute-start.23 = (bf16[256,1536]{1,0:T(8,128)(2,1)}, bf16[256,1536]{1,0:T(8,128)(2,1)S(1)}, u32[]{:S(2)}, u32[]{:S(2)}) collective-permute-start(bf16[256,1536]{1,0:T(8,128)(2,1)} %slice.3196), channel_id=1, source_target_pairs={{0,16},{4,20},{8,24},{12,28},{16,0},{20,4},{24,8},{28,12},{1,17},{... | collective-permute-start | bytes 2359304 | tf_op jit(solution)/shard_map/ppermute | solution.py:462
  504.9 29.3 %collective-permute-start.24 = (bf16[256,1536]{1,0:T(8,128)(2,1)}, bf16[256,1536]{1,0:T(8,128)(2,1)S(1)}, u32[]{:S(2)}, u32[]{:S(2)}) collective-permute-start(bf16[256,1536]{1,0:T(8,128)(2,1)} %slice.3195), channel_id=1, source_target_pairs={{0,8},{4,12},{8,0},{12,4},{16,24},{20,28},{24,16},{28,20},{1,9},{5... | collective-permute-start | bytes 2359304 | tf_op jit(solution)/shard_map/ppermute | solution.py:462
  506.4 27.8 %collective-permute-start.25 = (bf16[256,768]{1,0:T(8,128)(2,1)}, bf16[256,768]{1,0:T(8,128)(2,1)S(1)}, u32[]{:S(2)}, u32[]{:S(2)}) collective-permute-start(bf16[256,768]{1,0:T(8,128)(2,1)} %slice.3202), channel_id=1, source_target_pairs={{0,16},{4,20},{8,24},{12,28},{16,0},{20,4},{24,8},{28,12},{1,17},{... | collective-permute-start | bytes 1179656 | tf_op jit(solution)/shard_map/ppermute | solution.py:462
  507.0 27.2 %collective-permute-start.26 = (bf16[256,768]{1,0:T(8,128)(2,1)S(1)}, bf16[256,768]{1,0:T(8,128)(2,1)S(1)}, u32[]{:S(2)}, u32[]{:S(2)}) collective-permute-start(bf16[256,768]{1,0:T(8,128)(2,1)S(1)} %slice.3201), channel_id=1, source_target_pairs={{0,8},{4,12},{8,0},{12,4},{16,24},{20,28},{24,16},{28,20},{1,9},{5... | collective-permute-start | bytes 1179656 | tf_op jit(solution)/shard_map/ppermute | solution.py:462
  534.2 23.7 %collective-permute-start.28 = (bf16[768,1024]{1,0:T(8,128)(2,1)}, bf16[768,1024]{1,0:T(8,128)(2,1)}, u32[]{:S(2)}, u32[]{:S(2)}) collective-permute-start(bf16[768,1024]{1,0:T(8,128)(2,1)} %fusion.79), channel_id=1, source_target_pairs={{0,4},{4,0},{8,12},{12,8},{16,20},{20,16},{24,28},{28,24},{1,5},{5... | collective-permute-start | bytes 4718600 | tf_op jit(solution)/shard_map/ppermute | solution.py:462
  534.3 19.0 %collective-permute-start.27 = (bf16[704,1024]{1,0:T(8,128)(2,1)}, bf16[704,1024]{1,0:T(8,128)(2,1)}, u32[]{:S(2)}, u32[]{:S(2)}) collective-permute-start(bf16[704,1024]{1,0:T(8,128)(2,1)} %fusion.84), channel_id=1, source_target_pairs={{0,4},{4,0},{8,12},{12,8},{16,20},{20,16},{24,28},{28,24},{1,5},{5... | collective-permute-start | bytes 4325384 | tf_op jit(solution)/shard_map/ppermute | solution.py:462
  562.6 21.3 %collective-permute-start.30 = (bf16[768,512]{1,0:T(8,128)(2,1)}, bf16[768,512]{1,0:T(8,128)(2,1)}, u32[]{:S(2)}, u32[]{:S(2)}) collective-permute-start(bf16[768,512]{1,0:T(8,128)(2,1)} %slice.3192), channel_id=1, source_target_pairs={{0,16},{4,20},{8,24},{12,28},{16,0},{20,4},{24,8},{28,12},{1,17},{... | collective-permute-start | bytes 2359304 | tf_op jit(solution)/shard_map/ppermute | solution.py:462
  564.1 19.8 %collective-permute-start.29 = (bf16[704,512]{1,0:T(8,128)(2,1)}, bf16[704,512]{1,0:T(8,128)(2,1)}, u32[]{:S(2)}, u32[]{:S(2)}) collective-permute-start(bf16[704,512]{1,0:T(8,128)(2,1)} %slice.3197), channel_id=1, source_target_pairs={{0,8},{4,12},{8,0},{12,4},{16,24},{20,28},{24,16},{28,20},{1,9},{5... | collective-permute-start | bytes 2162696 | tf_op jit(solution)/shard_map/ppermute | solution.py:462
  585.5 16.4 %collective-permute-start.33 = (bf16[768,256]{1,0:T(8,128)(2,1)S(1)}, bf16[768,256]{1,0:T(8,128)(2,1)S(1)}, u32[]{:S(2)}, u32[]{:S(2)}) collective-permute-start(bf16[768,256]{1,0:T(8,128)(2,1)S(1)} %slice.3200), channel_id=1, source_target_pairs={{0,8},{4,12},{8,0},{12,4},{16,24},{20,28},{24,16},{28,20},{1,9},{5... | collective-permute-start | bytes 1179656 | tf_op jit(solution)/shard_map/ppermute | solution.py:462
  602.9 15.5 %collective-permute-start.35 = (bf16[768,256]{1,0:T(8,128)(2,1)S(1)}, bf16[768,256]{1,0:T(8,128)(2,1)}, u32[]{:S(2)}, u32[]{:S(2)}) collective-permute-start(bf16[768,256]{1,0:T(8,128)(2,1)S(1)} %fusion.105), channel_id=1, source_target_pairs={{0,8},{4,12},{8,0},{12,4},{16,24},{20,28},{24,16},{28,20},{1,9},{5... | collective-permute-start | bytes 1179656 | tf_op jit(solution)/shard_map/ppermute | solution.py:462
  606.5 14.0 %collective-permute-start.37 = (bf16[384,1024]{1,0:T(8,128)(2,1)}, bf16[384,1024]{1,0:T(8,128)(2,1)}, u32[]{:S(2)}, u32[]{:S(2)}) collective-permute-start(bf16[384,1024]{1,0:T(8,128)(2,1)} %fusion.87), channel_id=1, source_target_pairs={{0,4},{4,0},{8,12},{12,8},{16,20},{20,16},{24,28},{28,24},{1,5},{5... | collective-permute-start | bytes 2359304 | tf_op jit(solution)/shard_map/ppermute | solution.py:462
  606.9 17.9 %collective-permute-start.36 = (bf16[384,1024]{1,0:T(8,128)(2,1)}, bf16[384,1024]{1,0:T(8,128)(2,1)}, u32[]{:S(2)}, u32[]{:S(2)}) collective-permute-start(bf16[384,1024]{1,0:T(8,128)(2,1)} %fusion.90), channel_id=1, source_target_pairs={{0,4},{4,0},{8,12},{12,8},{16,20},{20,16},{24,28},{28,24},{1,5},{5... | collective-permute-start | bytes 2359304 | tf_op jit(solution)/shard_map/ppermute | solution.py:462
  628.1 23.7 %collective-permute-start.42 = (bf16[384,512]{1,0:T(8,128)(2,1)}, bf16[384,512]{1,0:T(8,128)(2,1)}, u32[]{:S(2)}, u32[]{:S(2)}) collective-permute-start(bf16[384,512]{1,0:T(8,128)(2,1)} %slice.3198), channel_id=1, source_target_pairs={{0,16},{4,20},{8,24},{12,28},{16,0},{20,4},{24,8},{28,12},{1,17},{... | collective-permute-start | bytes 1179656 | tf_op jit(solution)/shard_map/ppermute | solution.py:462
  629.6 24.9 %collective-permute-start.38 = (bf16[384,512]{1,0:T(8,128)(2,1)}, bf16[384,512]{1,0:T(8,128)(2,1)}, u32[]{:S(2)}, u32[]{:S(2)}) collective-permute-start(bf16[384,512]{1,0:T(8,128)(2,1)} %slice.3199), channel_id=1, source_target_pairs={{0,8},{4,12},{8,0},{12,4},{16,24},{20,28},{24,16},{28,20},{1,9},{5... | collective-permute-start | bytes 1179656 | tf_op jit(solution)/shard_map/ppermute | solution.py:462
  632.9 39.7 %collective-permute-start.52 = (bf16[768,512]{1,0:T(8,128)(2,1)}, bf16[768,512]{1,0:T(8,128)(2,1)}, u32[]{:S(2)}, u32[]{:S(2)}) collective-permute-start(bf16[768,512]{1,0:T(8,128)(2,1)} %pad_maximum_fusion.43), channel_id=1, source_target_pairs={{0,16},{4,20},{8,24},{12,28},{16,0},{20,4},{24,8},{28,12},{1,17},{... | collective-permute-start | bytes 2359304 | tf_op jit(solution)/shard_map/ppermute | solution.py:462
  634.5 36.6 %collective-permute-start.50 = (bf16[704,512]{1,0:T(8,128)(2,1)}, bf16[704,512]{1,0:T(8,128)(2,1)}, u32[]{:S(2)}, u32[]{:S(2)}) collective-permute-start(bf16[704,512]{1,0:T(8,128)(2,1)} %pad_maximum_fusion.46), channel_id=1, source_target_pairs={{0,8},{4,12},{8,0},{12,4},{16,24},{20,28},{24,16},{28,20},{1,9},{5... | collective-permute-start | bytes 2162696 | tf_op jit(solution)/shard_map/ppermute | solution.py:462
  660.7 16.1 %collective-permute-start.44 = (bf16[384,256]{1,0:T(8,128)(2,1)S(1)}, bf16[384,256]{1,0:T(8,128)(2,1)S(1)}, u32[]{:S(2)}, u32[]{:S(2)}) collective-permute-start(bf16[384,256]{1,0:T(8,128)(2,1)S(1)} %fusion.121), channel_id=1, source_target_pairs={{0,8},{4,12},{8,0},{12,4},{16,24},{20,28},{24,16},{28,20},{1,9},{5... | collective-permute-start | bytes 589832 | tf_op jit(solution)/shard_map/ppermute | solution.py:462
  689.4 14.1 %collective-permute-start.55 = (bf16[384,1024]{1,0:T(8,128)(2,1)S(1)}, bf16[384,1024]{1,0:T(8,128)(2,1)S(1)}, u32[]{:S(2)}, u32[]{:S(2)}) collective-permute-start(bf16[384,1024]{1,0:T(8,128)(2,1)S(1)} %pad_maximum_fusion.45.refs_5_), channel_id=1, source_target_pairs={{0,4},{4,0},{8,12},{12,8},{16,20},{20,16},{24,28},{28,24},{1,5},{5... | collective-permute-start | bytes 2359304 | tf_op jit(solution)/shard_map/ppermute | solution.py:462
  689.6 14.9 %collective-permute-start.54 = (bf16[384,1024]{1,0:T(8,128)(2,1)S(1)}, bf16[384,1024]{1,0:T(8,128)(2,1)S(1)}, u32[]{:S(2)}, u32[]{:S(2)}) collective-permute-start(bf16[384,1024]{1,0:T(8,128)(2,1)S(1)} %pad_maximum_fusion.44.refs_3_), channel_id=1, source_target_pairs={{0,4},{4,0},{8,12},{12,8},{16,20},{20,16},{24,28},{28,24},{1,5},{5... | collective-permute-start | bytes 2359304 | tf_op jit(solution)/shard_map/ppermute | solution.py:462
  (166 other events, 1188.9 us)
Sparse Core Ops, SparseCore 0:
  10.3 83.4 all-gather.5
  97.0 33.4 all-gather.7
  155.5 106.7 all-gather.9
  337.8 76.9 reduce-scatter.3
  419.1 81.2 all-gather.11
  503.3 75.2 reduce-scatter.5
  620.7 75.8 reduce-scatter.7
